TPU v7x, 256 devices: a whole 4x4x8 slice. The times are simulated.
256 devices in a mesh: gx: 8 (over x, core), gy: 32 (over y, z).
Axes of the slice: x: 4, y: 4, z: 8, core: 2. Of those that a mesh axis runs over, the one named last changes fastest.
Arguments:
- forcing: float32 [8, 8, 8, 8, 32, 128], P(None, None, None, 'gx', 'gy'), may hold values from -6 to 6
- coefficient: float32 [8, 8, 8, 8, 32, 128], P(None, None, None, 'gx', 'gy'), may hold values from 0.3 to 3
Outputs:
- pressure: float32 [8, 8, 8, 8, 32, 128], P(None, None, None, 'gx', 'gy')
- residual: float32 [8, 8, 8, 8, 32, 128], P(None, None, None, 'gx', 'gy')
All inputs are finite; a program needn't handle non-finite values.
Results may differ from a plain program's by a relative error of at most 0.0003.
Values sent between devices are 32-bit elements; how exact they have to be, the bound alone decides.
No kernel may reach another device: no remote copies, remote signals or barrier semaphores. Data moves between devices by JAX's collectives and lax.ppermute only.
A program may use at most 64 MiB of HBM per device.

v0:
```python
import math

import jax
import jax.numpy as jnp
from jax import lax
from jax.sharding import PartitionSpec as P

ITERS = 2


stretch = (1.0, 64.0, 1.0)


def with_halo(cells, sides, width):
    for axis, dim in sides:
        count = lax.axis_size(axis)
        ends = count - 1
        head = lax.slice_in_dim(cells, 0, width, axis=dim)
        tail = lax.slice_in_dim(cells, cells.shape[dim] - width, cells.shape[dim], axis=dim)
        cells = jnp.concatenate(
            [
                lax.ppermute(tail, axis, [(i, (i + 1) % count) for i in range(ends)]),
                cells,
                lax.ppermute(head, axis, [((i + 1) % count, i) for i in range(ends)]),
            ],
            axis=dim,
        )
    return cells


def legendre_value(order, position):
    prev_value = 1.0
    this_value = position
    for degree_now in range(2, order + 1):
        next_value = (
            (2 * degree_now - 1) * position * this_value - (degree_now - 1) * prev_value
        ) / degree_now
        prev_value = this_value
        this_value = next_value
    return this_value


def gll_points():
    points = [-1.0]
    for node_index in range(1, 7):
        position = -math.cos(math.pi * node_index / 7.0)
        for newton_step in range(60):
            target = legendre_value(8, position) - legendre_value(6, position)
            slope = 15.0 * legendre_value(7, position)
            position = position - target / slope
        points.append(position)
    points.append(1.0)
    return points


def jacobi_eigen(matrix_in):
    order_n = len(matrix_in)
    work_mat = [list(one_row) for one_row in matrix_in]
    vectors = [
        [1.0 if row_index == col_index else 0.0 for col_index in range(order_n)]
        for row_index in range(order_n)
    ]
    for sweep_index in range(40):
        for first_idx in range(order_n):
            for second_idx in range(first_idx + 1, order_n):
                rotation = 0.5 * math.atan2(
                    2.0 * work_mat[first_idx][second_idx],
                    work_mat[second_idx][second_idx] - work_mat[first_idx][first_idx],
                )
                cosine = math.cos(rotation)
                sine_part = math.sin(rotation)
                for other in range(order_n):
                    left_val = work_mat[other][first_idx]
                    right_val = work_mat[other][second_idx]
                    work_mat[other][first_idx] = cosine * left_val - sine_part * right_val
                    work_mat[other][second_idx] = sine_part * left_val + cosine * right_val
                for other in range(order_n):
                    left_val = work_mat[first_idx][other]
                    right_val = work_mat[second_idx][other]
                    work_mat[first_idx][other] = cosine * left_val - sine_part * right_val
                    work_mat[second_idx][other] = sine_part * left_val + cosine * right_val
                for other in range(order_n):
                    left_val = vectors[other][first_idx]
                    right_val = vectors[other][second_idx]
                    vectors[other][first_idx] = cosine * left_val - sine_part * right_val
                    vectors[other][second_idx] = sine_part * left_val + cosine * right_val
    return ([work_mat[diag_index][diag_index] for diag_index in range(order_n)], vectors)


def spectral_tables():
    nodes = gll_points()
    values_at = [legendre_value(7, position) for position in nodes]
    weights = [2.0 / (56.0 * value_now * value_now) for value_now in values_at]
    derivative = [[0.0] * 8 for row_index in range(8)]
    for row_index in range(8):
        for col_index in range(8):
            if row_index != col_index:
                derivative[row_index][col_index] = values_at[row_index] / (
                    values_at[col_index] * (nodes[row_index] - nodes[col_index])
                )
    derivative[0][0] = -14.0
    derivative[7][7] = 14.0
    stiffness = [
        [
            sum(
                (
                    derivative[mid][row_index] * weights[mid] * derivative[mid][col_index]
                    for mid in range(8)
                )
            )
            for col_index in range(8)
        ]
        for row_index in range(8)
    ]
    stiffness[0][0] = 2.0 * stiffness[0][0]
    stiffness[7][7] = 2.0 * stiffness[7][7]
    inv_root = [1.0 / math.sqrt(weight_now) for weight_now in weights]
    symmetric = [
        [
            inv_root[row_index] * stiffness[row_index][col_index] * inv_root[col_index]
            for col_index in range(8)
        ]
        for row_index in range(8)
    ]
    eigen_values, eigen_vectors = jacobi_eigen(symmetric)
    fdm_basis = [
        [inv_root[row_index] * eigen_vectors[row_index][col_index] for col_index in range(8)]
        for row_index in range(8)
    ]
    linear_hat = [
        [(1.0 - position) / 2.0 for position in nodes],
        [(1.0 + position) / 2.0 for position in nodes],
    ]
    return tuple(
        (
            jnp.asarray(one_table, dtype=jnp.float32)
            for one_table in (weights, derivative, fdm_basis, eigen_values, linear_hat)
        )
    )


def contract(form, table, field):
    return jnp.einsum(form, table, field, precision=lax.Precision.HIGHEST)


def edge_factors(local_count, offset, total_count):
    node_ids = jnp.arange(8, dtype=jnp.int32)[:, None]
    element_ids = offset + jnp.arange(local_count, dtype=jnp.int32)[None, :]
    at_first = node_ids == 0
    at_last = node_ids == 7
    outside = at_first & (element_ids == 0) | at_last & (element_ids == total_count - 1)
    shared = at_first & (element_ids > 0) | at_last & (element_ids < total_count - 1)
    keep_factor = jnp.where(outside, 0.0, 1.0).astype(jnp.float32)
    share_factor = jnp.where(shared, 0.5, 1.0).astype(jnp.float32)
    return (keep_factor, share_factor)


def node_masks(counts, offsets, totals):
    keep_x, share_x = edge_factors(counts[0], offsets[0], totals[0])
    keep_y, share_y = edge_factors(counts[1], offsets[1], totals[1])
    keep_z, share_z = edge_factors(counts[2], offsets[2], totals[2])
    keep_mask = (
        keep_x[:, None, None, :, None, None],
        keep_y[None, :, None, None, :, None],
        keep_z[None, None, :, None, None, :],
    )
    inv_mult = (
        share_x[:, None, None, :, None, None],
        share_y[None, :, None, None, :, None],
        share_z[None, None, :, None, None, :],
    )
    return (keep_mask, inv_mult)


def apply_factors(field, factors):
    return field * factors[0] * factors[1] * factors[2]


def no_neighbours(first_rim, last_rim, elem_dim):
    return (jnp.zeros_like(last_rim), jnp.zeros_like(first_rim))


def x_neighbours(first_rim, last_rim, elem_dim):
    stacked = jnp.stack([first_rim, last_rim], axis=2)
    extended = with_halo(stacked, (("gx", 2),), 1)
    return (extended[:, :, 0], extended[:, :, 3])


def y_neighbours(first_rim, last_rim, elem_dim):
    stacked = jnp.stack([first_rim, last_rim], axis=3)
    extended = with_halo(stacked, (("gy", 3),), 1)
    return (extended[:, :, :, 0], extended[:, :, :, 3])


def pair_sum(field, node_dim, remote):
    elem_dim = node_dim + 2
    first = jnp.take(field, 0, axis=node_dim)
    last_face = jnp.take(field, 7, axis=node_dim)
    count = first.shape[elem_dim]
    first_rim = lax.index_in_dim(first, 0, elem_dim, keepdims=False)
    last_rim = lax.index_in_dim(last_face, count - 1, elem_dim, keepdims=False)
    prev_last, next_first = remote(first_rim, last_rim, elem_dim)
    next_all = jnp.concatenate(
        [lax.slice_in_dim(first, 1, count, axis=elem_dim), jnp.expand_dims(next_first, elem_dim)],
        axis=elem_dim,
    )
    prev_all = jnp.concatenate(
        [
            jnp.expand_dims(prev_last, elem_dim),
            lax.slice_in_dim(last_face, 0, count - 1, axis=elem_dim),
        ],
        axis=elem_dim,
    )
    new_first = first + prev_all
    new_last = last_face + next_all
    middle = lax.slice_in_dim(field, 1, 7, axis=node_dim)
    return jnp.concatenate(
        [jnp.expand_dims(new_first, node_dim), middle, jnp.expand_dims(new_last, node_dim)],
        axis=node_dim,
    )


def direct_sum(field):
    field = pair_sum(field, 0, x_neighbours)
    field = pair_sum(field, 1, y_neighbours)
    return pair_sum(field, 2, no_neighbours)


def stiffness_apply(field, coefficient, derivative, weight_cube):
    scaled = coefficient * weight_cube
    grad_i = contract("pi,ijkxyz->pjkxyz", derivative, field)
    grad_j = contract("qj,ijkxyz->iqkxyz", derivative, field)
    grad_k = contract("rk,ijkxyz->ijrxyz", derivative, field)
    result = contract("pi,pjkxyz->ijkxyz", derivative, stretch[0] * scaled * grad_i)
    result = result + contract("qj,iqkxyz->ijkxyz", derivative, stretch[1] * scaled * grad_j)
    return result + contract("rk,ijrxyz->ijkxyz", derivative, stretch[2] * scaled * grad_k)


def fdm_apply(field, fdm_basis, denominator):
    moved = contract("ip,ijkxyz->pjkxyz", fdm_basis, field)
    moved = contract("jq,pjkxyz->pqkxyz", fdm_basis, moved)
    moved = contract("kr,pqkxyz->pqrxyz", fdm_basis, moved)
    moved = moved * denominator
    moved = contract("ip,pqrxyz->iqrxyz", fdm_basis, moved)
    moved = contract("jq,iqrxyz->ijrxyz", fdm_basis, moved)
    return contract("kr,ijrxyz->ijkxyz", fdm_basis, moved)


def restrict_corners(weighted, linear_hat):
    corners = contract("ai,ijkxyz->ajkxyz", linear_hat, weighted)
    corners = contract("bj,ajkxyz->abkxyz", linear_hat, corners)
    return contract("ck,abkxyz->abcxyz", linear_hat, corners)


def vertex_sum(corners):
    total_grid = jnp.zeros(
        (corners.shape[3] + 1, corners.shape[4] + 1, corners.shape[5] + 1), jnp.float32
    )
    for side_x in range(2):
        for side_y in range(2):
            for side_z in range(2):
                total_grid = total_grid + jnp.pad(
                    corners[side_x, side_y, side_z],
                    ((side_x, 1 - side_x), (side_y, 1 - side_y), (side_z, 1 - side_z)),
                )
    return total_grid


def prolong(vertices, linear_hat):
    count_x = vertices.shape[0] - 1
    count_y = vertices.shape[1] - 1
    count_z = vertices.shape[2] - 1
    corner_vals = jnp.stack(
        [
            jnp.stack(
                [
                    jnp.stack(
                        [
                            vertices[
                                side_x : side_x + count_x,
                                side_y : side_y + count_y,
                                side_z : side_z + count_z,
                            ]
                            for side_z in range(2)
                        ]
                    )
                    for side_y in range(2)
                ]
            )
            for side_x in range(2)
        ]
    )
    nodal = contract("ck,abcxyz->abkxyz", linear_hat, corner_vals)
    nodal = contract("bj,abkxyz->ajkxyz", linear_hat, nodal)
    return contract("ai,ajkxyz->ijkxyz", linear_hat, nodal)


def sine_system(cells):
    wave_ints = jnp.arange(1, cells, dtype=jnp.int32)
    product_ids = wave_ints[:, None] * wave_ints[None, :] % (2 * cells)
    sine_table = math.sqrt(2.0 / cells) * jnp.sin(math.pi * product_ids.astype(jnp.float32) / cells)
    cosines = jnp.cos(math.pi * wave_ints.astype(jnp.float32) / cells)
    stiff_eig = (2.0 - 2.0 * cosines) / 2.0
    mass_eig = 2.0 * (4.0 + 2.0 * cosines) / 6.0
    return (sine_table, stiff_eig, mass_eig)


def coarse_solve(vertices):
    interior = vertices[1:-1, 1:-1, 1:-1]
    table_x, stiff_x, mass_x = sine_system(vertices.shape[0] - 1)
    table_y, stiff_y, mass_y = sine_system(vertices.shape[1] - 1)
    table_z, stiff_z, mass_z = sine_system(vertices.shape[2] - 1)
    moved = contract("mi,ijk->mjk", table_x, interior)
    moved = contract("nj,mjk->mnk", table_y, moved)
    moved = contract("ok,mnk->mno", table_z, moved)
    denominator = (
        stretch[0] * stiff_x[:, None, None] * mass_y[None, :, None] * mass_z[None, None, :]
    )
    denominator = (
        denominator
        + stretch[1] * mass_x[:, None, None] * stiff_y[None, :, None] * mass_z[None, None, :]
    )
    denominator = (
        denominator
        + stretch[2] * mass_x[:, None, None] * mass_y[None, :, None] * stiff_z[None, None, :]
    )
    moved = moved / denominator
    moved = contract("mi,mno->ino", table_x, moved)
    moved = contract("nj,ino->ijo", table_y, moved)
    moved = contract("ok,ijo->ijk", table_z, moved)
    return jnp.pad(moved, 1)


def on_device(forcing, coefficient):
    weights, derivative, fdm_basis, eigen_values, linear_hat = spectral_tables()
    local_x = forcing.shape[3]
    local_y = forcing.shape[4]
    depth_count = forcing.shape[5]
    size_x = lax.axis_size("gx")
    size_y = lax.axis_size("gy")
    start_x = lax.axis_index("gx") * local_x
    start_y = lax.axis_index("gy") * local_y
    total_x = local_x * size_x
    total_y = local_y * size_y
    keep_mask, inv_mult = node_masks(
        (local_x, local_y, depth_count), (start_x, start_y, 0), (total_x, total_y, depth_count)
    )
    weight_cube = (weights[:, None, None] * weights[None, :, None] * weights[None, None, :])[
        :, :, :, None, None, None
    ]
    eigen_sum = (
        stretch[0] * eigen_values[:, None, None]
        + stretch[1] * eigen_values[None, :, None]
        + stretch[2] * eigen_values[None, None, :]
    )
    denominator = (1.0 / eigen_sum)[:, :, :, None, None, None]

    def coarse_part(field):
        vertices = vertex_sum(restrict_corners(apply_factors(field, inv_mult), linear_hat))
        whole_grid = jnp.zeros((total_x + 1, total_y + 1, depth_count + 1), jnp.float32)
        whole_grid = lax.dynamic_update_slice(
            whole_grid, vertices, (start_x, start_y, jnp.int32(0))
        )
        whole_grid = lax.psum(whole_grid, ("gx", "gy"))
        solved = coarse_solve(whole_grid)
        own_block = lax.dynamic_slice(solved, (start_x, start_y, jnp.int32(0)), vertices.shape)
        return prolong(own_block, linear_hat)

    def precondition(field):
        local_part = apply_factors(direct_sum(fdm_apply(field, fdm_basis, denominator)), keep_mask)
        return local_part + coarse_part(field)

    def inner_sum(left, right):
        return jnp.sum(apply_factors(left * right, inv_mult))

    def energy_sum(left, right):
        return lax.psum(inner_sum(left, right), ("gx", "gy"))

    load_vec = apply_factors(direct_sum(forcing), keep_mask)
    pressure = jnp.zeros_like(load_vec)
    residual = load_vec
    smoothed = precondition(residual)
    direction = smoothed
    energy_now = energy_sum(residual, smoothed)
    for step_index in range(ITERS):
        image_dir = apply_factors(
            direct_sum(stiffness_apply(direction, coefficient, derivative, weight_cube)), keep_mask
        )
        step_size = energy_now / lax.psum(inner_sum(direction, image_dir), ("gx", "gy"))
        pressure = pressure + step_size * direction
        residual = residual - step_size * image_dir
        if step_index + 1 < ITERS:
            smoothed = precondition(residual)
            energy_next = energy_sum(residual, smoothed)
            direction = smoothed + energy_next / energy_now * direction
            energy_now = energy_next
    return (pressure, residual)


def solution(mesh):
    in_specs = (P(None, None, None, "gx", "gy", None), P(None, None, None, "gx", "gy", None))
    out_specs = (P(None, None, None, "gx", "gy", None), P(None, None, None, "gx", "gy", None))
    return jax.shard_map(
        on_device, mesh=mesh, in_specs=in_specs, out_specs=out_specs, check_vma=False
    )
```

profile of v0, /device:TPU:10, one launch (start us, length us, event | category | flops | bytes accessed | tf_op | source)
XLA Modules:
  0.0 853.5 jit_solution(11557859143102917298)
XLA Ops:
  7.3 0.8 slice_bitcast_fusion.9
  8.1 1.9 collective-permute-start
  10.0 3.6 collective-permute-start.1
  14.6 0.6 collective-permute-done.1
  15.3 3.8 collective-permute-start.2
  19.1 5.7 collective-permute-done.2
  24.8 3.9 collective-permute-start.3
  28.9 1.8 collective-permute-done.3
  31.3 0.7 copy-done.6
  34.7 0.5 convolution_bitcast_fusion.10
  35.7 1.9 collective-permute-start.4
  37.6 3.6 collective-permute-start.5
  41.3 1.5 collective-permute-done.5
  42.8 1.9 collective-permute-start.6
  45.1 0.8 copy-done.2
  45.9 4.9 collective-permute-done.6
  50.8 3.8 collective-permute-start.7
  54.6 243.7 %all-reduce.32.cloned.1.call-done = f32[9,33,129]{2,1,0:T(8,128)} async-done(((f32[9,33,129]{2,1,0:T(8,128)}), f32[9,33,129]{2,1,0:T(8,128)}) %all-reduce.32.cloned.1.call-update) | async-done | bytes 153268 | tf_op jit(solution)/shard_map/psum | solution.py:364
  298.3 1.0 slice.406
  299.7 0.9 convolution_bitcast_fusion.1
  300.6 1.0 convolution_divide_fusion.1
  302.5 0.6 fusion.109
  304.7 0.5 copy-done.3
  306.0 0.6 copy-done
  306.5 0.6 fusion.3
  307.1 0.5 fusion.35
  307.7 0.5 fusion.68
  309.1 2.0 collective-permute-start.8
  311.1 3.7 collective-permute-start.9
  315.0 1.2 collective-permute-done.9
  316.3 2.0 collective-permute-start.10
  318.3 0.7 fusion.76
  319.1 5.1 collective-permute-done.10
  324.2 1.9 collective-permute-start.11
  326.3 3.7 collective-permute-done.11
  330.4 0.8 multiply_reduce_fusion.1
  331.2 72.3 %all-reduce.28 = (f32[]{:T(128)}, f32[]{:T(128)}) all-reduce(f32[]{:T(128)} %fusion.76, f32[]{:T(128)} %multiply_reduce_fusion.1), channel_id=1, replica_groups=mesh['gx'=8,'gy'=32] {'gx','gy'}, use_global_device_ids=true, to_apply=%region_2.9 | all-reduce | flops 2 | bytes 16 | tf_op jit(solution)/shard_map/psum | solution.py:377
  407.8 0.5 convolution_bitcast_fusion.5
  408.8 1.9 collective-permute-start.12
  410.7 3.6 collective-permute-start.13
  414.8 0.8 copy-done.1
  416.0 2.7 collective-permute-start.14
  418.9 5.0 collective-permute-done.14
  423.9 2.6 collective-permute-start.15
  426.5 236.6 %all-reduce.34.cloned.1.call-done = f32[9,33,129]{2,1,0:T(8,128)} async-done(((f32[9,33,129]{2,1,0:T(8,128)}), f32[9,33,129]{2,1,0:T(8,128)}) %all-reduce.34.cloned.1.call-update) | async-done | bytes 153268 | tf_op jit(solution)/shard_map/psum | solution.py:364
  663.0 1.0 slice.425
  664.4 0.9 convolution_bitcast_fusion
  665.4 1.0 convolution_divide_fusion
  667.3 0.6 fusion.106
  669.4 0.8 multiply_reduce_fusion
  670.2 73.8 %psum.46 = f32[]{:T(128)} all-reduce(f32[]{:T(128)} %multiply_reduce_fusion), channel_id=1, replica_groups=mesh['gx'=8,'gy'=32] {'gx','gy'}, use_global_device_ids=true, to_apply=%region_7.14 | all-reduce | flops 1 | bytes 8 | tf_op jit(solution)/shard_map/psum | solution.py:377
  746.3 0.6 fusion.8
  746.9 0.5 fusion.33
  748.8 1.9 collective-permute-start.16
  750.7 3.6 collective-permute-start.17
  754.6 1.3 collective-permute-done.17
  756.0 2.7 collective-permute-start.18
  758.8 5.4 collective-permute-done.18
  764.2 1.9 collective-permute-start.19
  766.3 3.7 collective-permute-done.19
  770.4 0.8 fusion.58
  771.3 72.1 %psum.47 = f32[]{:T(128)} all-reduce(f32[]{:T(128)} %fusion.58), channel_id=1, replica_groups=mesh['gx'=8,'gy'=32] {'gx','gy'}, use_global_device_ids=true, to_apply=%region_9.16 | all-reduce | flops 1 | bytes 8 | tf_op jit(solution)/shard_map/psum | solution.py:389
  844.8 0.7 multiply_add_fusion
  845.7 1.0 copy.108
  (184 shorter events, 20.7 us)
Async XLA Ops:
  7.2 6.7 copy-start.7
  7.2 6.9 copy-start.8
  7.2 6.9 copy-start.9
  7.2 7.2 copy-start.5
  7.2 291.1 %all-reduce.32.cloned.1.call-start = ((), (), s32[]{:S(2)}) async-start(), calls=%async_computation | async-start | bytes 737280 | tf_op jit(solution)/shard_map/psum | solution.py:364
  8.1 6.5 collective-permute-start
  10.0 5.2 collective-permute-start.1
  15.3 9.5 %collective-permute-start.2 = (f32[8,8,1,1,128]{4,0,1,3,2:T(8,128)S(1)}, f32[8,8,1,1,128]{4,0,1,3,2:T(8,128)S(1)}, u32[]{:S(2)}, u32[]{:S(2)}) collective-permute-start(f32[8,8,1,1,128]{4,0,1,3,2:T(8,128)S(1)} %maximum_bitcast_fusion.16), channel_id=1, source_target_pairs={{0,1},{1,2},{2,3},{3,4},{4,5},{5,6},{6,7},{7,8},{8,9},{9,10},{10,1... | collective-permute-start | bytes 98312 | tf_op jit(solution)/shard_map/ppermute | solution.py:22
  24.8 5.9 collective-permute-start.3
  31.2 0.7 copy-start.6
  32.3 0.7 copy-start.4
  35.7 5.6 collective-permute-start.4
  37.6 5.2 collective-permute-start.5
  42.8 7.9 collective-permute-start.6
  45.0 0.8 copy-start.2
  45.8 617.2 %all-reduce.34.cloned.1.call-start = ((), (), s32[]{:S(2)}) async-start(), calls=%async_computation.1 | async-start | bytes 737280 | tf_op jit(solution)/shard_map/psum | solution.py:364
  50.8 253.5 %collective-permute-start.7 = (f32[8,8,1,1,128]{4,1,0,3,2:T(8,128)S(1)}, f32[8,8,1,1,128]{4,1,0,3,2:T(8,128)S(1)}, u32[]{:S(2)}, u32[]{:S(2)}) collective-permute-start(f32[8,8,1,1,128]{4,1,0,3,2:T(8,128)S(1)} %get-tuple-element.97), channel_id=1, source_target_pairs={{1,0},{2,1},{3,2},{4,3},{5,4},{6,5},{7,6},{8,7},{9,8},{10,9},{11,1... | collective-permute-start | bytes 98312 | tf_op jit(solution)/shard_map/ppermute | solution.py:24
  304.5 0.7 copy-start.3
  305.6 1.0 copy-start
  309.1 5.9 collective-permute-start.8
  311.1 5.1 collective-permute-start.9
  316.3 7.9 collective-permute-start.10
  324.2 5.8 collective-permute-start.11
  408.8 6.8 collective-permute-start.12
  410.7 5.2 collective-permute-start.13
  414.8 0.8 copy-start.1
  416.0 7.9 collective-permute-start.14
  423.9 245.1 %collective-permute-start.15 = (f32[8,8,1,1,128]{4,0,1,3,2:T(8,128)S(1)}, f32[8,8,1,1,128]{4,0,1,3,2:T(8,128)S(1)}, u32[]{:S(2)}, u32[]{:S(2)}) collective-permute-start(f32[8,8,1,1,128]{4,0,1,3,2:T(8,128)S(1)} %get-tuple-element.87), channel_id=1, source_target_pairs={{1,0},{2,1},{3,2},{4,3},{5,4},{6,5},{7,6},{8,7},{9,8},{10,9},{11,1... | collective-permute-start | bytes 98312 | tf_op jit(solution)/shard_map/ppermute | solution.py:24
  748.8 5.8 collective-permute-start.16
  750.7 5.2 collective-permute-start.17
  756.0 8.2 collective-permute-start.18
  764.2 5.8 collective-permute-start.19
Sparse Core Ops, SparseCore 0:
  46.0 252.2 all-reduce.31
  415.7 247.2 all-reduce.33
where the time goes:
time: 858 us; the launch traced here: 854 us
  waiting for transfers between devices  521 us (61%)
  blocking collectives  218 us (25%)
  starting transfers between devices  55.4 us (6%)
  matrix products  21.5 us (3%)
  between operations  19.3 us (2%)
  local copies, waits for them, and re-layouts  9.86 us (1%)
  other arithmetic  8.64 us (1%)
    psum x2, waiting for transfers between devices, coarse_part(): whole_grid = lax.psum(whole_grid, ('gx', 'gy'))  480 us
    psum x2, blocking collectives, energy_sum(): return lax.psum(inner_sum(left, right), ('gx', 'gy'))  146 us
    psum x1, blocking collectives, on_device(): lax.psum(inner_sum(direction, image_dir), ('gx', 'gy'))  72.1 us
    ppermute x10, starting transfers between devices, with_halo(): lax.ppermute(head, axis, [((i + 1) % count, i) for i in range(ends)])  32.4 us
    ppermute x10, waiting for transfers between devices, with_halo(): lax.ppermute(tail, axis, [(i, (i + 1) % count) for i in range(ends)])  26.1 us
    ppermute x10, starting transfers between devices, with_halo(): lax.ppermute(tail, axis, [(i, (i + 1) % count) for i in range(ends)])  22.9 us
    dot_general x48, matrix products, contract(): return jnp.einsum(form, table, field, precision=lax.Precision.HIGHEST)  21.5 us
  transfers between devices with their start and end apart: 22, of which 15 were waited for; matrix products, arithmetic and copies ran while one was open for 2% of the time, Pallas kernels for 0%

commit v1 on v0

v1 whole, which is shorter than its diff:
```python
import functools
import math

import jax
import jax.numpy as jnp
import numpy as np
from jax import lax
from jax.experimental import pallas as pl
from jax.experimental.pallas import tpu as pltpu
from jax.sharding import Mesh
from jax.sharding import PartitionSpec as P

NP = 8
EX = 8
EY = 32
EZ = 128
STRETCH = (1.0, 64.0, 1.0)
CHIPS = 128
MODES = (EX - 1) * (EY - 1)
MODES_PAD = 224
F32 = jnp.float32
HIGHEST = lax.Precision.HIGHEST


def legendre(order, x):
    before, now = 1.0, x
    for n in range(2, order + 1):
        before, now = now, ((2 * n - 1) * x * now - (n - 1) * before) / n
    return now


def gll_points():
    points = [-1.0]
    for n in range(1, 7):
        x = -math.cos(math.pi * n / 7.0)
        for _ in range(60):
            x = x - (legendre(8, x) - legendre(6, x)) / (15.0 * legendre(7, x))
        points.append(x)
    points.append(1.0)
    return points


@functools.lru_cache(maxsize=None)
def spectral_tables():
    nodes = gll_points()
    values = [legendre(7, x) for x in nodes]
    w = np.array([2.0 / (56.0 * v * v) for v in values])
    deriv = np.zeros((8, 8))
    for i in range(8):
        for j in range(8):
            if i != j:
                deriv[i, j] = values[i] / (values[j] * (nodes[i] - nodes[j]))
    deriv[0, 0] = -14.0
    deriv[7, 7] = 14.0
    stiff = deriv.T @ np.diag(w) @ deriv
    stiff[0, 0] *= 2.0
    stiff[7, 7] *= 2.0
    root = 1.0 / np.sqrt(w)
    lam, vec = np.linalg.eigh(root[:, None] * stiff * root[None, :])
    basis = root[:, None] * vec
    x = np.array(nodes)
    hat = np.stack([(1.0 - x) / 2.0, (1.0 + x) / 2.0])
    hat[0, 7] = 0.0
    hat[1, 0] = 0.0
    return w, deriv, basis, lam, hat


def sine_system(cells):
    n = np.arange(1, cells)
    table = math.sqrt(2.0 / cells) * np.sin(math.pi * ((n[:, None] * n[None, :]) % (2 * cells)) / cells)
    cosines = np.cos(math.pi * n / cells)
    return table, (2.0 - 2.0 * cosines) / 2.0, 2.0 * (4.0 + 2.0 * cosines) / 6.0


@functools.lru_cache(maxsize=None)
def all_tables():
    w, deriv, basis, lam, hat = spectral_tables()
    denom = (
        STRETCH[0] * lam[:, None, None] + STRETCH[1] * lam[None, :, None] + STRETCH[2] * lam[None, None, :]
    )
    big = np.kron(np.kron(basis, basis), basis)
    local_solve = (big / denom.reshape(1, 512)) @ big.T
    corner = np.stack(
        [
            np.einsum("i,j,k->ijk", hat[a], hat[b], hat[c]).reshape(512)
            for c in range(2)
            for a in range(2)
            for b in range(2)
        ]
    )
    tx, sx, mx = sine_system(EX)
    ty, sy, my = sine_system(EY)
    tz, sz, mz = sine_system(EZ)
    vx = np.zeros((EX + 1, EX - 1))
    vx[1:-1] = tx
    vy = np.zeros((EY + 1, EY - 1))
    vy[1:-1] = ty
    vz = np.zeros((EZ + 1, EZ))
    vz[1:-1, : EZ - 1] = tz
    z_low, z_high = vz[:-1], vz[1:]
    eig = (
        STRETCH[0] * sx[:, None, None] * my[None, :, None] * mz[None, None, :]
        + STRETCH[1] * mx[:, None, None] * sy[None, :, None] * mz[None, None, :]
        + STRETCH[2] * mx[:, None, None] * my[None, :, None] * sz[None, None, :]
    )
    inv_eig = np.zeros((MODES_PAD, EZ))
    inv_eig[:MODES, : EZ - 1] = (1.0 / eig).reshape(MODES, EZ - 1)
    gather = np.zeros((2, MODES_PAD, 4 * CHIPS))
    for core in range(2):
        part = np.zeros((MODES, EX // 2, EY, 2, 2))
        for a in range(2):
            for b in range(2):
                rows_x = vx[core + a : core + a + EX - 1 : 2]
                rows_y = vy[b : b + EY]
                part[:, :, :, a, b] = np.einsum("xm,yn->mnxy", rows_x, rows_y).reshape(MODES, EX // 2, EY)
        gather[core, :MODES] = part.reshape(MODES, 4 * CHIPS)
    own_x = np.zeros((EX, 8, MODES_PAD))
    own_y = np.zeros((EY, 8, MODES_PAD))
    for side in range(2):
        for a in range(2):
            for b in range(2):
                row = side * 4 + a * 2 + b
                for x in range(EX):
                    own_x[x, row, :MODES] = np.repeat(vx[(x ^ side) + a], EY - 1)
                for y in range(EY):
                    own_y[y, row, :MODES] = np.tile(vy[y + b], EX - 1)
    lanes = np.ones((1, 128))
    roll_tables = np.zeros((18, 8, 128))
    for s in range(8):
        for r in range(8):
            roll_tables[s, r] = deriv[r, (r - s) % 8]
            roll_tables[8 + s, r] = deriv[(r - s) % 8, r]
    roll_tables[16] = hat[0][:, None] * lanes
    roll_tables[17] = hat[1][:, None] * lanes
    weight = np.einsum("i,j,k->ijk", w, w, w)[..., None] * lanes
    f = lambda t: np.asarray(t, np.float32)
    return dict(
        deriv=f(deriv),
        hat=f(hat),
        local_solve=f(local_solve),
        corner=f(corner),
        z_low=f(z_low),
        z_high=f(z_high),
        z_low_t=f(z_low.T),
        z_high_t=f(z_high.T),
        inv_eig=f(inv_eig),
        gather=f(gather),
        own_x=f(own_x),
        own_y=f(own_y),
        rolls=f(roll_tables),
        weight=f(weight),
    )


FACE = jax.ShapeDtypeStruct((8, 8, 128), F32)
NODES = jax.ShapeDtypeStruct((8, 8, 8, 128), F32)
ROWS = jax.ShapeDtypeStruct((4 * CHIPS, 128), F32)
SMALL = jax.ShapeDtypeStruct((8, 128), F32)
VMEM = pl.BlockSpec(memory_space=pltpu.VMEM)
SMEM = pl.BlockSpec(memory_space=pltpu.SMEM)


def call(body, outs, place, *args, scratch=(), name=None):
    return pl.pallas_call(
        body,
        out_shape=outs,
        in_specs=[SMEM] + [VMEM] * len(args),
        out_specs=[VMEM] * len(outs),
        scratch_shapes=list(scratch),
        name=name,
    )(place, *args)


def dot(a, b):
    return jnp.dot(a, b, precision=HIGHEST, preferred_element_type=F32)


def inner_x(place):
    return 7 * (1 - (place[0] & 1))


def inner_y(place):
    return 7 * (1 - (place[1] & 1))


def put_x_faces(place, u, inner, outer):
    at = inner_x(place)
    inner[...] = u[at]
    outer[...] = u[7 - at]


def lane_iota():
    return lax.broadcasted_iota(jnp.int32, (8, 128), 1)


def row_iota():
    return lax.broadcasted_iota(jnp.int32, (8, 128), 0)


def restrict_rows(u, corner, z_low, z_high):
    c = dot(corner[...], u[...].reshape(512, 128))
    return dot(c[0:4], z_low[...]) + dot(c[4:8], z_high[...])


def send_rows(rows, out):
    pair = jnp.concatenate([rows, rows], axis=0)
    for t in range(4 * CHIPS // 8):
        out[8 * t : 8 * t + 8] = pair


def assemble(place, u, xin, xout, yin, yout, v):
    ax, ay = inner_x(place), inner_y(place)
    keep_x = jnp.where((place[0] == 0) | (place[0] == EX - 1), 0.0, 1.0).astype(F32)
    keep_y = jnp.where((place[1] == 0) | (place[1] == EY - 1), 0.0, 1.0).astype(F32)
    v[...] = u[...]
    v[ax] = v[ax] + xin[...]
    v[7 - ax] = (v[7 - ax] + xout[...]) * keep_x
    for i in range(8):
        v[i, ay] = v[i, ay] + yin[i]
        v[i, 7 - ay] = (v[i, 7 - ay] + yout[i]) * keep_y
    v[7 - ax] = v[7 - ax] * keep_x
    lane, row = lane_iota(), row_iota()
    first, last = row == 0, row == 7
    keep_z = jnp.where((first & (lane == 0)) | (last & (lane == 127)), 0.0, 1.0).astype(F32)
    for i in range(8):
        for j in range(8):
            t = v[i, j]
            from_prev = pltpu.roll(pltpu.roll(t, 1, 1), 1, 0)
            from_next = pltpu.roll(pltpu.roll(t, 127, 1), 7, 0)
            t = t + jnp.where(first, from_prev, 0.0) + jnp.where(last, from_next, 0.0)
            v[i, j] = t * keep_z


def stiffness(u, cw, rolls, out):
    deriv = all_tables()["deriv"]
    for j in range(8):
        q = []
        vals = [u[i, j] for i in range(8)]
        for p in range(8):
            g = float(deriv[p, 0]) * vals[0]
            for i in range(1, 8):
                g = g + float(deriv[p, i]) * vals[i]
            q.append(g * cw[p, j])
        for i in range(8):
            r = float(deriv[0, i]) * q[0]
            for p in range(1, 8):
                r = r + float(deriv[p, i]) * q[p]
            out[i, j] = r
    for i in range(8):
        q = []
        vals = [u[i, j] for j in range(8)]
        for p in range(8):
            g = float(deriv[p, 0]) * vals[0]
            for j in range(1, 8):
                g = g + float(deriv[p, j]) * vals[j]
            q.append(g * (STRETCH[1] * cw[i, p]))
        for j in range(8):
            r = float(deriv[0, j]) * q[0]
            for p in range(1, 8):
                r = r + float(deriv[p, j]) * q[p]
            out[i, j] = out[i, j] + r
    for i in range(8):
        for j in range(8):
            t = u[i, j]
            g = rolls[0] * t
            for s in range(1, 8):
                g = g + rolls[s] * pltpu.roll(t, s, 0)
            q = g * cw[i, j]
            r = rolls[8] * q
            for s in range(1, 8):
                r = r + rolls[8 + s] * pltpu.roll(q, s, 0)
            out[i, j] = out[i, j] + r


def prolong_add(coarse, rolls, z_low_t, z_high_t, v):
    hat = all_tables()["hat"]
    low = dot(coarse, z_low_t[...])
    high = dot(coarse, z_high_t[...])
    h0, h1 = rolls[16], rolls[17]
    line = [h0 * low[r : r + 1] + h1 * high[r : r + 1] for r in range(4)]
    for j in range(8):
        near = float(hat[0, j]) * line[0] + float(hat[1, j]) * line[1]
        far = float(hat[0, j]) * line[2] + float(hat[1, j]) * line[3]
        for i in range(8):
            v[i, j] = v[i, j] + (float(hat[0, i]) * near + float(hat[1, i]) * far)


def total(a, b):
    return jnp.sum(a[...] * b[...], keepdims=True).reshape(1, 1)


def k_faces(place, u, inner, outer):
    put_x_faces(place, u, inner, outer)


def k_restrict(place, u, corner, z_low, z_high, rows):
    send_rows(restrict_rows(u, corner, z_low, z_high), rows)


def k_weight(place, coefficient, weight, cw):
    cw[...] = coefficient[...] * weight[...]


def k_y_faces(place, u, xin, xout, inner, outer):
    ax, ay = inner_x(place), inner_y(place)
    for face, at in ((inner, ay), (outer, 7 - ay)):
        for i in range(8):
            face[i] = u[i, at]
        face[ax] = face[ax] + xin[at]
        face[7 - ax] = face[7 - ax] + xout[at]


def k_local_solve(place, u, xin, xout, yin, yout, solve, v, h, hin, hout):
    assemble(place, u, xin, xout, yin, yout, v)
    h[...] = dot(solve[...], v[...].reshape(512, 128)).reshape(8, 8, 8, 128)
    put_x_faces(place, h, hin, hout)


def k_coarse(place, got, gather, inv_eig, own_x, own_y, out):
    modes = dot(gather[place[2]], got[...]) * inv_eig[...]
    mine = dot(own_x[place[0]] * own_y[place[1]], modes)
    sums = jnp.sum(got[...].reshape(4 * CHIPS // 8, 8, 128), axis=0)
    sums = sums + pltpu.roll(sums, 4, 0)
    out[...] = jnp.where(lane_iota() == 127, sums, mine)


def k_first(
    place, h, xin, xout, yin, yout, mine, theirs, f, cw, rolls, z_low_t, z_high_t, corner, z_low, z_high,
    s, g, gin, gout, rows,
):
    assemble(place, h, xin, xout, yin, yout, s)
    prolong_add(mine[0:4] + theirs[4:8], rolls, z_low_t, z_high_t, s)
    stiffness(s, cw, rolls, g)
    put_x_faces(place, g, gin, gout)
    modes = restrict_rows(g, corner, z_low, z_high)
    lane, row = lax.broadcasted_iota(jnp.int32, (4, 128), 1), lax.broadcasted_iota(jnp.int32, (4, 128), 0)
    sums = jnp.where(row == 0, total(f, s), jnp.where(row == 1, total(s, g), 0.0))
    send_rows(jnp.where(lane == 127, sums, modes), rows)


def k_second(
    place, h, xin, xout, yin, yout, mine, theirs, f, s0, g0, cw, rolls, z_low_t, z_high_t,
    s1, h1, gin, gout, rows, scalars, t,
):
    assemble(place, h, xin, xout, yin, yout, t)
    coarse = mine[0:4] + theirs[4:8]
    prolong_add(coarse, rolls, z_low_t, z_high_t, t)
    lane4 = lax.broadcasted_iota(jnp.int32, (4, 128), 1)
    known = jnp.sum(jnp.where(lane4 == 127, coarse, 0.0), axis=1, keepdims=True)
    energy, curve = known[0:1], known[1:2]
    step = energy / curve
    s1[...] = s0[...] - step * t[...]
    stiffness(s1, cw, rolls, h1)
    put_x_faces(place, h1, gin, gout)
    fresh = jnp.sum(s1[...] * (f[...] - step * g0[...]), keepdims=True).reshape(1, 1)
    sums = (fresh, total(s1, h1), total(s1, g0), total(s0, h1))
    lane = lane_iota()
    row = jnp.zeros((8, 128), F32)
    for n, value in enumerate(sums):
        row = jnp.where(lane == n, value, row)
    for n in range(2 * CHIPS // 8):
        rows[8 * n : 8 * n + 8] = row
    lane = lane_iota()
    scalars[...] = jnp.where(lane == 0, energy, jnp.where(lane == 1, curve, step))


def k_last(place, h, xin, xout, yin, yout, got, scalars, s0, s1, b, w, p, r):
    sums = jnp.sum(got[...], axis=0, keepdims=True)
    fresh, s1h1, s1g0, s0h1 = (sums[:, n : n + 1] for n in range(4))
    energy, curve, step0 = (scalars[0:1, n : n + 1] for n in range(3))
    beta = fresh / energy
    step1 = fresh / (s1h1 + beta * (s1g0 + s0h1) + beta * beta * curve)
    assemble(place, h, xin, xout, yin, yout, r)
    p[...] = step0 * s0[...] + step1 * (s1[...] + beta * s0[...])
    r[...] = (b[...] - step0 * w[...]) - step1 * (r[...] + beta * w[...])


CHIP_AXES = ("x", "y", "z")
ALL_AXES = ("x", "c", "y", "z")
SWAP = [(0, 1), (1, 0)]


def pairs(count, start):
    out = []
    for n in range(start, count - 1, 2):
        out += [(n, n + 1), (n + 1, n)]
    return out


def swap_x(inner, outer):
    return (
        lax.ppermute(inner, "c", SWAP),
        lax.ppermute(outer, ("x", "c"), pairs(EX, 1)),
    )


def swap_y(inner, outer):
    return (
        lax.ppermute(inner, ("y", "z"), pairs(EY, 0)),
        lax.ppermute(outer, ("y", "z"), pairs(EY, 1)),
    )


def share(rows):
    got = lax.all_to_all(rows.reshape(CHIPS, 4, 128), CHIP_AXES, 0, 0)
    return got.reshape(4 * CHIPS, 128)


def on_device(forcing, coefficient):
    tables = all_tables()
    tab = lambda *names: [jnp.asarray(tables[n]) for n in names]
    f = forcing.reshape(8, 8, 8, 128)
    coef = coefficient.reshape(8, 8, 8, 128)
    px = lax.axis_index(("x", "c")).astype(jnp.int32)
    py = lax.axis_index(("y", "z")).astype(jnp.int32)
    n = jnp.arange(4, dtype=jnp.int32)
    place = jnp.where(n == 0, px, jnp.where(n == 1, py, px & 1))

    def halo(u, inner, outer):
        xs = swap_x(inner, outer)
        ys = swap_y(*call(k_y_faces, (FACE, FACE), place, u, *xs, name="yfaces"))
        return xs + ys

    def coarse(rows):
        got = share(rows)
        mine = call(
            k_coarse, (SMALL,), place, got, *tab("gather", "inv_eig", "own_x", "own_y"), name="coarse"
        )[0]
        return mine, lax.ppermute(mine, "c", SWAP)

    def local(u, sides):
        return call(
            k_local_solve, (NODES, NODES, FACE, FACE), place, u, *sides, *tab("local_solve"), name="solve"
        )

    faces = call(k_faces, (FACE, FACE), place, f, name="faces")
    rows = call(k_restrict, (ROWS,), place, f, *tab("corner", "z_low", "z_high"), name="restrict")[0]
    cw = call(k_weight, (NODES,), place, coef, *tab("weight"), name="weight")[0]
    c0 = coarse(rows)
    b, h, hin, hout = local(f, halo(f, *faces))
    s0, g0, gin, gout, rows = call(
        k_first, (NODES, NODES, FACE, FACE, ROWS), place, h, *halo(h, hin, hout), *c0, f, cw,
        *tab("rolls", "z_low_t", "z_high_t", "corner", "z_low", "z_high"), name="first",
    )
    c1 = coarse(rows)
    w, h, hin, hout = local(g0, halo(g0, gin, gout))
    s1, h1, gin, gout, rows, scalars = call(
        k_second,
        (NODES, NODES, FACE, FACE, jax.ShapeDtypeStruct((2 * CHIPS, 128), F32), SMALL),
        place, h, *halo(h, hin, hout), *c1, f, s0, g0, cw, *tab("rolls", "z_low_t", "z_high_t"),
        scratch=(pltpu.VMEM((8, 8, 8, 128), F32),), name="second",
    )
    got = lax.all_to_all(rows.reshape(2 * CHIPS, 1, 128), ALL_AXES, 0, 0).reshape(2 * CHIPS, 128)
    p, r = call(
        k_last, (NODES, NODES), place, h1, *halo(h1, gin, gout), got, scalars, s0, s1, b, w, name="last"
    )
    return p.reshape(forcing.shape), r.reshape(forcing.shape)


def solution(mesh):
    fine = Mesh(mesh.devices.reshape(4, 2, 4, 8), ALL_AXES)
    spec = P(None, None, None, ("x", "c"), ("y", "z"), None)
    return jax.shard_map(
        on_device, mesh=fine, in_specs=(spec, spec), out_specs=(spec, spec), check_vma=False
    )
```

time: 858 us -> 151 us (0.18)
  waiting for transfers between devices: 521 us -> 26.6 us
  blocking collectives: 218 us -> 0 us
  Pallas kernels: 0 us -> 36.4 us
  starting transfers between devices: 55.4 us -> 77.6 us
  matrix products: 21.5 us -> 0 us
  between operations: 19.3 us -> 1.02 us
    psum x2 -> x0, waiting for transfers between devices: 480 us -> none  [coarse_part(): whole_grid = lax.psum(whole_grid, ('gx', 'gy'))]
    psum x3 -> x0, blocking collectives: 218 us -> none  [the longest x2 146 us: energy_sum(): return lax.psum(inner_sum(left, right), ('gx', 'gy'))]
    all_to_all x0 -> x3, starting transfers between devices: none -> 37.2 us  [the longest x2 26.7 us: share(): got = lax.all_to_all(rows.reshape(CHIPS, 4, 128), CHIP_AXES, 0, 0)]
    pallas_call x0 -> x15, Pallas kernels: none -> 36.4 us  [call(): pl.pallas_call(body, out_shape=outs, in_specs=[SMEM] + [VMEM] * len(args)...]
    dot_general x48 -> x0, matrix products: 21.5 us -> none  [contract(): return jnp.einsum(form, table, field, precision=lax.Precision.HIGHEST)]
    ppermute x20 -> x22, starting transfers between devices: 55.3 us -> 40.4 us  [the longest x5 24.1 us: swap_y(): lax.ppermute(outer, ('y', 'z'), pairs(EY, 1))]
    ppermute x20 -> x22, waiting for transfers between devices: 40.3 us -> 26.6 us  [the longest x5 16.1 us: swap_x(): lax.ppermute(outer, ('x', 'c'), pairs(EX, 1))]
  transfers between devices with their start and end apart: 22 -> 25, of which waited for: 15 -> 9; matrix products, arithmetic and copies ran while one was open for 2% -> 0% of each run, Pallas kernels for 0% -> 16%
where the time goes in v1:
time: 151 us; the launch traced here: 150 us
  starting transfers between devices  77.6 us (51%)
  Pallas kernels  36.4 us (24%)
  waiting for transfers between devices  26.6 us (18%)
  local copies, waits for them, and re-layouts  8.08 us (5%)
    pallas_call x15, Pallas kernels, call(): pl.pallas_call(body, out_shape=outs, in_specs=[SMEM] + [VMEM] * len(args)...  36.4 us
    all_to_all x2, starting transfers between devices, share(): got = lax.all_to_all(rows.reshape(CHIPS, 4, 128), CHIP_AXES, 0, 0)  26.7 us
    ppermute x5, starting transfers between devices, swap_y(): lax.ppermute(outer, ('y', 'z'), pairs(EY, 1))  24.1 us
    ppermute x5, waiting for transfers between devices, swap_x(): lax.ppermute(outer, ('x', 'c'), pairs(EX, 1))  16.1 us
    ppermute x5, starting transfers between devices, swap_x(): lax.ppermute(outer, ('x', 'c'), pairs(EX, 1))  11.1 us
    all_to_all x1, starting transfers between devices, on_device(): lax.all_to_all(rows.reshape(2 * CHIPS, 1, 128), ALL_AXES, 0, 0)  10.5 us
    ppermute x5, waiting for transfers between devices, swap_y(): lax.ppermute(outer, ('y', 'z'), pairs(EY, 1))  9.37 us
    unnamed x58, local copies, waits for them, and re-layouts  8.08 us
  transfers between devices with their start and end apart: 25, of which 9 were waited for; matrix products, arithmetic and copies ran while one was open for 0% of the time, Pallas kernels for 16%

profile of v1, /device:TPU:10, one launch (start us, length us, event | category | flops | bytes accessed | tf_op | source)
XLA Modules:
  0.0 150.3 jit_solution(10480986126349650743)
XLA Ops:
  0.6 0.6 compare_select_fusion.1.place
  1.2 2.3 %restrict.1 = f32[512,128]{1,0:T(8,128)} custom-call(s32[4]{0:T(128)} %compare_select_fusion.1.place, f32[8,8,8,128]{3,2,1,0:T(8,128)} %bitcast.16, f32[8,512]{1,0:T(8,128)} %constant.49.clone.corner, f32[128,128]{1,0:T(8,128)} %constant.50.clone.z_low, f32[128,128]{1,0:T(8,128)} %constant.51.clone.z_high.z_high_t), custom_call_target="tpu_custom_call" | custom-call | tf_op jit(solution)/shard_map/restrict/pallas_call | solution.py:164
  3.6 15.5 %all-to-all-start = ((f32[128,4,128]{2,1,0:T(4,128)}), f32[128,4,128]{2,1,0:T(4,128)S(1)}, u32[]{:S(2)}, u32[]{:S(2)}) async-start(f32[128,4,128]{2,1,0:T(4,128)} %bitcast.22), calls=%async_computation | async-start | bytes 524288 | tf_op jit(solution)/shard_map/all_to_all | solution.py:405
  19.0 1.6 %faces.1 = (f32[8,8,128]{2,1,0:T(8,128)}, f32[8,8,128]{2,1,0:T(8,128)}) custom-call(s32[4]{0:T(128)} %compare_select_fusion.1.place, f32[8,8,8,128]{3,2,1,0:T(8,128)} %bitcast.17), custom_call_target="tpu_custom_call" | custom-call | tf_op jit(solution)/shard_map/faces/pallas_call | solution.py:164
  20.6 0.0 collective-permute-start
  20.6 2.4 %collective-permute-start.1 = (f32[8,8,128]{2,1,0:T(8,128)}, f32[8,8,128]{2,1,0:T(8,128)S(1)}, u32[]{:S(2)}, u32[]{:S(2)}) collective-permute-start(f32[8,8,128]{2,1,0:T(8,128)} %get-tuple-element.36), channel_id=1, source_target_pairs={{32,64},{64,32},{96,128},{128,96},{160,192},{192,160},{33,65},{65,... | collective-permute-start | bytes 98312 | tf_op jit(solution)/shard_map/ppermute | solution.py:393
  23.1 3.1 %collective-permute-done.1.xout = f32[8,8,128]{2,1,0:T(8,128)S(1)} collective-permute-done((f32[8,8,128]{2,1,0:T(8,128)}, f32[8,8,128]{2,1,0:T(8,128)S(1)}, u32[]{:S(2)}, u32[]{:S(2)}) %collective-permute-start.1) | collective-permute-done | bytes 32800 | tf_op jit(solution)/shard_map/ppermute | solution.py:393
  26.2 0.6 copy-done.12
  26.8 1.6 %yfaces.5 = (f32[8,8,128]{2,1,0:T(8,128)}, f32[8,8,128]{2,1,0:T(8,128)}) custom-call(s32[4]{0:T(128)} %compare_select_fusion.1.place, f32[8,8,8,128]{3,2,1,0:T(8,128)} %bitcast.18, f32[8,8,128]{2,1,0:T(8,128)} %copy-done.9, f32[8,8,128]{2,1,0:T(8,128)} %copy-done.12), custom_call_target="tpu_custom_call" | custom-call | tf_op jit(solution)/shard_map/yfaces/pallas_call | solution.py:164
  28.4 1.5 collective-permute-start.2
  29.8 4.6 %collective-permute-start.3 = (f32[8,8,128]{2,1,0:T(8,128)}, f32[8,8,128]{2,1,0:T(8,128)S(1)}, u32[]{:S(2)}, u32[]{:S(2)}) collective-permute-start(f32[8,8,128]{2,1,0:T(8,128)} %get-tuple-element.38), channel_id=1, source_target_pairs={{1,2},{2,1},{3,4},{4,3},{5,6},{6,5},{7,8},{8,7},{9,10},{10,9},{11,... | collective-permute-start | bytes 98312 | tf_op jit(solution)/shard_map/ppermute | solution.py:400
  34.4 0.0 collective-permute-done.2.yin
  34.4 3.5 %collective-permute-done.3.yout = f32[8,8,128]{2,1,0:T(8,128)S(1)} collective-permute-done((f32[8,8,128]{2,1,0:T(8,128)}, f32[8,8,128]{2,1,0:T(8,128)S(1)}, u32[]{:S(2)}, u32[]{:S(2)}) %collective-permute-start.3) | collective-permute-done | bytes 32800 | tf_op jit(solution)/shard_map/ppermute | solution.py:400
  38.0 0.6 copy-done.22
  38.6 3.3 %solve.4 = (f32[8,8,8,128]{3,2,1,0:T(8,128)}, f32[8,8,8,128]{3,2,1,0:T(8,128)}, f32[8,8,128]{2,1,0:T(8,128)}, f32[8,8,128]{2,1,0:T(8,128)}) custom-call(s32[4]{0:T(128)} %compare_select_fusion.1.place, f32[8,8,8,128]{3,2,1,0:T(8,128)} %bitcast.19, f32[8,8,128]{2,1,0:T(8,128)} %copy-done.9, f32[8,8,128]{2,1,0:T(8,128)} %copy-done.12, ...), custom_call_target="tpu_custom_call" | custom-call | tf_op jit(solution)/shard_map/solve/pallas_call | solution.py:164
  41.9 0.0 collective-permute-start.4
  41.9 1.9 %collective-permute-start.5 = (f32[8,8,128]{2,1,0:T(8,128)}, f32[8,8,128]{2,1,0:T(8,128)S(1)}, u32[]{:S(2)}, u32[]{:S(2)}) collective-permute-start(f32[8,8,128]{2,1,0:T(8,128)} %get-tuple-element.41), channel_id=1, source_target_pairs={{32,64},{64,32},{96,128},{128,96},{160,192},{192,160},{33,65},{65,... | collective-permute-start | bytes 98312 | tf_op jit(solution)/shard_map/ppermute | solution.py:393
  43.8 3.5 %collective-permute-done.5.xout = f32[8,8,128]{2,1,0:T(8,128)S(1)} collective-permute-done((f32[8,8,128]{2,1,0:T(8,128)}, f32[8,8,128]{2,1,0:T(8,128)S(1)}, u32[]{:S(2)}, u32[]{:S(2)}) %collective-permute-start.5) | collective-permute-done | bytes 32800 | tf_op jit(solution)/shard_map/ppermute | solution.py:393
  47.3 0.6 copy-done.6
  47.9 1.6 %yfaces.6 = (f32[8,8,128]{2,1,0:T(8,128)}, f32[8,8,128]{2,1,0:T(8,128)}) custom-call(s32[4]{0:T(128)} %compare_select_fusion.1.place, f32[8,8,8,128]{3,2,1,0:T(8,128)} %get-tuple-element.39.u.h, f32[8,8,128]{2,1,0:T(8,128)} %copy-done.5, f32[8,8,128]{2,1,0:T(8,128)} %copy-done.6), custom_call_target="tpu_custom_call" | custom-call | tf_op jit(solution)/shard_map/yfaces/pallas_call | solution.py:164
  49.6 4.6 %collective-permute-start.7 = (f32[8,8,128]{2,1,0:T(8,128)}, f32[8,8,128]{2,1,0:T(8,128)S(1)}, u32[]{:S(2)}, u32[]{:S(2)}) collective-permute-start(f32[8,8,128]{2,1,0:T(8,128)} %get-tuple-element.43), channel_id=1, source_target_pairs={{1,2},{2,1},{3,4},{4,3},{5,6},{6,5},{7,8},{8,7},{9,10},{10,9},{11,... | collective-permute-start | bytes 98312 | tf_op jit(solution)/shard_map/ppermute | solution.py:400
  54.2 0.0 copy-start.1
  54.2 0.7 copy-done.1
  54.9 2.9 %coarse.2.mine = f32[8,128]{1,0:T(8,128)} custom-call(s32[4]{0:T(128)} %compare_select_fusion.1.place, f32[512,128]{1,0:T(8,128)} %bitcast.24, f32[2,224,512]{2,1,0:T(8,128)} %constant.53.clone.gather, f32[224,128]{1,0:T(8,128)} %constant.54.clone.inv_eig, f32[8,8,224]{2,1,0:T(8,128)} %constant.55.clone.own_x, f32[32,8,224]{2,1,0:T(8,128)} %constant.56.clone.own_y), custom_call_target="tpu_custom_call" | custom-call | tf_op jit(solution)/shard_map/coarse/pallas_call | solution.py:164
  57.7 0.2 collective-permute-start.8
  58.0 1.8 %weight.2.cw = f32[8,8,8,128]{3,2,1,0:T(8,128)} custom-call(s32[4]{0:T(128)} %compare_select_fusion.1.place, f32[8,8,8,128]{3,2,1,0:T(8,128)} %bitcast.27, f32[8,8,8,128]{3,2,1,0:T(8,128)} %constant.52.clone.weight), custom_call_target="tpu_custom_call" | custom-call | tf_op jit(solution)/shard_map/weight/pallas_call | solution.py:164
  59.8 0.6 copy-done.15
  60.3 0.0 copy-done.16
  60.4 0.6 copy-done.24
  60.9 3.9 %first.1 = (f32[8,8,8,128]{3,2,1,0:T(8,128)}, f32[8,8,8,128]{3,2,1,0:T(8,128)}, f32[8,8,128]{2,1,0:T(8,128)}, f32[8,8,128]{2,1,0:T(8,128)}, f32[512,128]{1,0:T(8,128)}) custom-call(s32[4]{0:T(128)} %compare_select_fusion.1.place, f32[8,8,8,128]{3,2,1,0:T(8,128)} %get-tuple-element.39.u.h, f32[8,8,128]{2,1,0:T(8,128)} %copy-done.5, f32[8,8,128]{2,1,0:T(8,128)} %copy-done.6, ...), custom_call_target="tpu_custom_call" | custom-call | tf_op jit(solution)/shard_map/first/pallas_call | solution.py:164
  64.9 11.3 %all-to-all-start.1 = ((f32[128,4,128]{2,1,0:T(4,128)}), f32[128,4,128]{2,1,0:T(4,128)S(1)}, u32[]{:S(2)}, u32[]{:S(2)}) async-start(f32[128,4,128]{2,1,0:T(4,128)} %bitcast.26), calls=%async_computation.1 | async-start | bytes 524288 | tf_op jit(solution)/shard_map/all_to_all | solution.py:405
  76.2 0.1 collective-permute-start.9
  76.3 2.4 %collective-permute-start.10 = (f32[8,8,128]{2,1,0:T(8,128)S(1)}, f32[8,8,128]{2,1,0:T(8,128)S(1)}, u32[]{:S(2)}, u32[]{:S(2)}) collective-permute-start(f32[8,8,128]{2,1,0:T(8,128)S(1)} %copy-done.27), channel_id=1, source_target_pairs={{32,64},{64,32},{96,128},{128,96},{160,192},{192,160},{33,65},{65,... | collective-permute-start | bytes 98312 | tf_op jit(solution)/shard_map/ppermute | solution.py:393
  78.7 3.2 %collective-permute-done.10.xout = f32[8,8,128]{2,1,0:T(8,128)S(1)} collective-permute-done((f32[8,8,128]{2,1,0:T(8,128)S(1)}, f32[8,8,128]{2,1,0:T(8,128)S(1)}, u32[]{:S(2)}, u32[]{:S(2)}) %collective-permute-start.10) | collective-permute-done | bytes 32800 | tf_op jit(solution)/shard_map/ppermute | solution.py:393
  81.9 0.6 copy-done.11
  82.5 1.6 %yfaces.7 = (f32[8,8,128]{2,1,0:T(8,128)}, f32[8,8,128]{2,1,0:T(8,128)}) custom-call(s32[4]{0:T(128)} %compare_select_fusion.1.place, f32[8,8,8,128]{3,2,1,0:T(8,128)} %get-tuple-element.44.u.g0, f32[8,8,128]{2,1,0:T(8,128)} %copy-done.10, f32[8,8,128]{2,1,0:T(8,128)} %copy-done.11), custom_call_target="tpu_custom_call" | custom-call | tf_op jit(solution)/shard_map/yfaces/pallas_call | solution.py:164
  84.1 1.3 collective-permute-start.11
  85.4 4.6 %collective-permute-start.12 = (f32[8,8,128]{2,1,0:T(8,128)}, f32[8,8,128]{2,1,0:T(8,128)S(1)}, u32[]{:S(2)}, u32[]{:S(2)}) collective-permute-start(f32[8,8,128]{2,1,0:T(8,128)} %get-tuple-element.48), channel_id=1, source_target_pairs={{1,2},{2,1},{3,4},{4,3},{5,6},{6,5},{7,8},{8,7},{9,10},{10,9},{11,... | collective-permute-start | bytes 98312 | tf_op jit(solution)/shard_map/ppermute | solution.py:400
  90.0 3.5 %collective-permute-done.12.yout = f32[8,8,128]{2,1,0:T(8,128)S(1)} collective-permute-done((f32[8,8,128]{2,1,0:T(8,128)}, f32[8,8,128]{2,1,0:T(8,128)S(1)}, u32[]{:S(2)}, u32[]{:S(2)}) %collective-permute-start.12) | collective-permute-done | bytes 32800 | tf_op jit(solution)/shard_map/ppermute | solution.py:400
  93.5 0.6 copy-done.21
  94.1 3.3 %solve.5 = (f32[8,8,8,128]{3,2,1,0:T(8,128)}, f32[8,8,8,128]{3,2,1,0:T(8,128)}, f32[8,8,128]{2,1,0:T(8,128)}, f32[8,8,128]{2,1,0:T(8,128)}) custom-call(s32[4]{0:T(128)} %compare_select_fusion.1.place, f32[8,8,8,128]{3,2,1,0:T(8,128)} %get-tuple-element.44.u.g0, f32[8,8,128]{2,1,0:T(8,128)} %copy-done.10, f32[8,8,128]{2,1,0:T(8,128)} %copy-done.11, ...), custom_call_target="tpu_custom_call" | custom-call | tf_op jit(solution)/shard_map/solve/pallas_call | solution.py:164
  97.4 1.9 %collective-permute-start.14 = (f32[8,8,128]{2,1,0:T(8,128)}, f32[8,8,128]{2,1,0:T(8,128)S(1)}, u32[]{:S(2)}, u32[]{:S(2)}) collective-permute-start(f32[8,8,128]{2,1,0:T(8,128)} %get-tuple-element.51), channel_id=1, source_target_pairs={{32,64},{64,32},{96,128},{128,96},{160,192},{192,160},{33,65},{65,... | collective-permute-start | bytes 98312 | tf_op jit(solution)/shard_map/ppermute | solution.py:393
  99.4 3.5 %collective-permute-done.14.xout = f32[8,8,128]{2,1,0:T(8,128)S(1)} collective-permute-done((f32[8,8,128]{2,1,0:T(8,128)}, f32[8,8,128]{2,1,0:T(8,128)S(1)}, u32[]{:S(2)}, u32[]{:S(2)}) %collective-permute-start.14) | collective-permute-done | bytes 32800 | tf_op jit(solution)/shard_map/ppermute | solution.py:393
  102.9 0.6 copy-done.4
  103.5 1.6 %yfaces.8 = (f32[8,8,128]{2,1,0:T(8,128)}, f32[8,8,128]{2,1,0:T(8,128)}) custom-call(s32[4]{0:T(128)} %compare_select_fusion.1.place, f32[8,8,8,128]{3,2,1,0:T(8,128)} %get-tuple-element.49.u.h, f32[8,8,128]{2,1,0:T(8,128)} %copy-done.3, f32[8,8,128]{2,1,0:T(8,128)} %copy-done.4), custom_call_target="tpu_custom_call" | custom-call | tf_op jit(solution)/shard_map/yfaces/pallas_call | solution.py:164
  105.1 4.6 %collective-permute-start.16 = (f32[8,8,128]{2,1,0:T(8,128)}, f32[8,8,128]{2,1,0:T(8,128)S(1)}, u32[]{:S(2)}, u32[]{:S(2)}) collective-permute-start(f32[8,8,128]{2,1,0:T(8,128)} %get-tuple-element.53), channel_id=1, source_target_pairs={{1,2},{2,1},{3,4},{4,3},{5,6},{6,5},{7,8},{8,7},{9,10},{10,9},{11,... | collective-permute-start | bytes 98312 | tf_op jit(solution)/shard_map/ppermute | solution.py:400
  109.8 0.7 copy-done
  110.5 2.9 %coarse.3.mine = f32[8,128]{1,0:T(8,128)} custom-call(s32[4]{0:T(128)} %compare_select_fusion.1.place, f32[512,128]{1,0:T(8,128)} %bitcast.23, f32[2,224,512]{2,1,0:T(8,128)} %constant.53.clone.gather, f32[224,128]{1,0:T(8,128)} %constant.54.clone.inv_eig, f32[8,8,224]{2,1,0:T(8,128)} %constant.55.clone.own_x, f32[32,8,224]{2,1,0:T(8,128)} %constant.56.clone.own_y), custom_call_target="tpu_custom_call" | custom-call | tf_op jit(solution)/shard_map/coarse/pallas_call | solution.py:164
  113.3 0.2 collective-permute-start.17
  113.6 1.1 collective-permute-done.17.theirs
  114.7 0.6 copy-done.23
  115.3 3.6 %second.1 = (f32[8,8,8,128]{3,2,1,0:T(8,128)}, f32[8,8,8,128]{3,2,1,0:T(8,128)}, f32[8,8,128]{2,1,0:T(8,128)}, f32[8,8,128]{2,1,0:T(8,128)}, f32[256,128]{1,0:T(8,128)}, /*index=5*/f32[8,128]{1,0:T(8,128)}) custom-call(s32[4]{0:T(128)} %compare_select_fusion.1.place, f32[8,8,8,128]{3,2,1,0:T(8,128)} %get-tuple-element.49.u.h, f32[8,8,128]{2,1,0:T(8,128)} %copy-done.3, ...), custom_call_target="tpu_custom_call" | custom-call | tf_op jit(solution)/shard_map/second/pallas_call | solution.py:164
  118.9 10.5 %all-to-all-start.2 = ((f32[256,1,128]{2,1,0:T(1,128)}), f32[256,1,128]{2,1,0:T(1,128)S(1)}, u32[]{:S(2)}, u32[]{:S(2)}) async-start(f32[256,1,128]{2,1,0:T(1,128)} %bitcast.28), calls=%async_computation.2 | async-start | bytes 262144 | tf_op jit(solution)/shard_map/all_to_all | solution.py:453
  129.4 0.2 collective-permute-start.18
  129.6 2.5 %collective-permute-start.19 = (f32[8,8,128]{2,1,0:T(8,128)S(1)}, f32[8,8,128]{2,1,0:T(8,128)S(1)}, u32[]{:S(2)}, u32[]{:S(2)}) collective-permute-start(f32[8,8,128]{2,1,0:T(8,128)S(1)} %copy-done.25), channel_id=1, source_target_pairs={{32,64},{64,32},{96,128},{128,96},{160,192},{192,160},{33,65},{65,... | collective-permute-start | bytes 98312 | tf_op jit(solution)/shard_map/ppermute | solution.py:393
  132.1 2.8 %collective-permute-done.19.xout = f32[8,8,128]{2,1,0:T(8,128)S(1)} collective-permute-done((f32[8,8,128]{2,1,0:T(8,128)S(1)}, f32[8,8,128]{2,1,0:T(8,128)S(1)}, u32[]{:S(2)}, u32[]{:S(2)}) %collective-permute-start.19) | collective-permute-done | bytes 32800 | tf_op jit(solution)/shard_map/ppermute | solution.py:393
  134.9 0.6 copy-done.8
  135.5 1.6 %yfaces.9 = (f32[8,8,128]{2,1,0:T(8,128)}, f32[8,8,128]{2,1,0:T(8,128)}) custom-call(s32[4]{0:T(128)} %compare_select_fusion.1.place, f32[8,8,8,128]{3,2,1,0:T(8,128)} %get-tuple-element.56.u.h, f32[8,8,128]{2,1,0:T(8,128)} %copy-done.7, f32[8,8,128]{2,1,0:T(8,128)} %copy-done.8), custom_call_target="tpu_custom_call" | custom-call | tf_op jit(solution)/shard_map/yfaces/pallas_call | solution.py:164
  137.2 1.7 %collective-permute-start.20 = (f32[8,8,128]{2,1,0:T(8,128)}, f32[8,8,128]{2,1,0:T(8,128)S(1)}, u32[]{:S(2)}, u32[]{:S(2)}) collective-permute-start(f32[8,8,128]{2,1,0:T(8,128)} %get-tuple-element.59), channel_id=1, source_target_pairs={{0,1},{1,0},{2,3},{3,2},{4,5},{5,4},{6,7},{7,6},{8,9},{9,8},{10,11... | collective-permute-start | bytes 98312 | tf_op jit(solution)/shard_map/ppermute | solution.py:399
  138.9 5.7 %collective-permute-start.21 = (f32[8,8,128]{2,1,0:T(8,128)}, f32[8,8,128]{2,1,0:T(8,128)S(1)}, u32[]{:S(2)}, u32[]{:S(2)}) collective-permute-start(f32[8,8,128]{2,1,0:T(8,128)} %get-tuple-element.60), channel_id=1, source_target_pairs={{1,2},{2,1},{3,4},{4,3},{5,6},{6,5},{7,8},{8,7},{9,10},{10,9},{11,... | collective-permute-start | bytes 98312 | tf_op jit(solution)/shard_map/ppermute | solution.py:400
  144.6 2.4 %collective-permute-done.21.yout = f32[8,8,128]{2,1,0:T(8,128)S(1)} collective-permute-done((f32[8,8,128]{2,1,0:T(8,128)}, f32[8,8,128]{2,1,0:T(8,128)S(1)}, u32[]{:S(2)}, u32[]{:S(2)}) %collective-permute-start.21) | collective-permute-done | bytes 32800 | tf_op jit(solution)/shard_map/ppermute | solution.py:400
  147.0 0.6 copy-done.18
  147.6 0.1 copy-done.2
  147.6 2.7 %last.1 = (f32[8,8,8,128]{3,2,1,0:T(8,128)}, f32[8,8,8,128]{3,2,1,0:T(8,128)}) custom-call(s32[4]{0:T(128)} %compare_select_fusion.1.place, f32[8,8,8,128]{3,2,1,0:T(8,128)} %get-tuple-element.56.u.h, f32[8,8,128]{2,1,0:T(8,128)} %copy-done.7, f32[8,8,128]{2,1,0:T(8,128)} %copy-done.8, f32[8,8,128]{2,1,0:T(8,128)} %copy-done.17, f32[8,8,128]{2,1,0:T(8,128)} %copy-done.18, ...), custom_call_target="tpu_custom_call" | custom-call | tf_op jit(solution)/shard_map/last/pallas_call | solution.py:164
  (60 shorter events, 0.1 us)
Async XLA Ops:
  3.6 50.6 %all-to-all-start = ((f32[128,4,128]{2,1,0:T(4,128)}), f32[128,4,128]{2,1,0:T(4,128)S(1)}, u32[]{:S(2)}, u32[]{:S(2)}) async-start(f32[128,4,128]{2,1,0:T(4,128)} %bitcast.22), calls=%async_computation | async-start | bytes 524288 | tf_op jit(solution)/shard_map/all_to_all | solution.py:405
  20.6 2.4 %collective-permute-start = (f32[8,8,128]{2,1,0:T(8,128)}, f32[8,8,128]{2,1,0:T(8,128)S(1)}, u32[]{:S(2)}, u32[]{:S(2)}) collective-permute-start(f32[8,8,128]{2,1,0:T(8,128)} %get-tuple-element.35), channel_id=1, source_target_pairs={{0,32},{32,0},{1,33},{33,1},{2,34},{34,2},{3,35},{35,3},{4,36},{36... | collective-permute-start | bytes 98312 | tf_op jit(solution)/shard_map/ppermute | solution.py:392
  20.6 5.5 %collective-permute-start.1 = (f32[8,8,128]{2,1,0:T(8,128)}, f32[8,8,128]{2,1,0:T(8,128)S(1)}, u32[]{:S(2)}, u32[]{:S(2)}) collective-permute-start(f32[8,8,128]{2,1,0:T(8,128)} %get-tuple-element.36), channel_id=1, source_target_pairs={{32,64},{64,32},{96,128},{128,96},{160,192},{192,160},{33,65},{65,... | collective-permute-start | bytes 98312 | tf_op jit(solution)/shard_map/ppermute | solution.py:393
  23.1 3.1 %copy-start.9 = (f32[8,8,128]{2,1,0:T(8,128)}, f32[8,8,128]{2,1,0:T(8,128)S(1)}, u32[]{:S(2)}) copy-start(f32[8,8,128]{2,1,0:T(8,128)S(1)} %collective-permute-done.xin) | copy-start | bytes 98308
  26.2 0.6 copy-start.12
  28.4 6.0 %collective-permute-start.2 = (f32[8,8,128]{2,1,0:T(8,128)}, f32[8,8,128]{2,1,0:T(8,128)S(1)}, u32[]{:S(2)}, u32[]{:S(2)}) collective-permute-start(f32[8,8,128]{2,1,0:T(8,128)} %get-tuple-element.37), channel_id=1, source_target_pairs={{0,1},{1,0},{2,3},{3,2},{4,5},{5,4},{6,7},{7,6},{8,9},{9,8},{10,11... | collective-permute-start | bytes 98312 | tf_op jit(solution)/shard_map/ppermute | solution.py:399
  29.8 8.1 %collective-permute-start.3 = (f32[8,8,128]{2,1,0:T(8,128)}, f32[8,8,128]{2,1,0:T(8,128)S(1)}, u32[]{:S(2)}, u32[]{:S(2)}) collective-permute-start(f32[8,8,128]{2,1,0:T(8,128)} %get-tuple-element.38), channel_id=1, source_target_pairs={{1,2},{2,1},{3,4},{4,3},{5,6},{6,5},{7,8},{8,7},{9,10},{10,9},{11,... | collective-permute-start | bytes 98312 | tf_op jit(solution)/shard_map/ppermute | solution.py:400
  34.4 3.5 %copy-start.20 = (f32[8,8,128]{2,1,0:T(8,128)}, f32[8,8,128]{2,1,0:T(8,128)S(1)}, u32[]{:S(2)}) copy-start(f32[8,8,128]{2,1,0:T(8,128)S(1)} %collective-permute-done.2.yin) | copy-start | bytes 98308
  38.0 0.6 copy-start.22
  41.9 1.9 %collective-permute-start.4 = (f32[8,8,128]{2,1,0:T(8,128)}, f32[8,8,128]{2,1,0:T(8,128)S(1)}, u32[]{:S(2)}, u32[]{:S(2)}) collective-permute-start(f32[8,8,128]{2,1,0:T(8,128)} %get-tuple-element.40), channel_id=1, source_target_pairs={{0,32},{32,0},{1,33},{33,1},{2,34},{34,2},{3,35},{35,3},{4,36},{36... | collective-permute-start | bytes 98312 | tf_op jit(solution)/shard_map/ppermute | solution.py:392
  41.9 5.4 %collective-permute-start.5 = (f32[8,8,128]{2,1,0:T(8,128)}, f32[8,8,128]{2,1,0:T(8,128)S(1)}, u32[]{:S(2)}, u32[]{:S(2)}) collective-permute-start(f32[8,8,128]{2,1,0:T(8,128)} %get-tuple-element.41), channel_id=1, source_target_pairs={{32,64},{64,32},{96,128},{128,96},{160,192},{192,160},{33,65},{65,... | collective-permute-start | bytes 98312 | tf_op jit(solution)/shard_map/ppermute | solution.py:393
  43.8 3.5 %copy-start.5 = (f32[8,8,128]{2,1,0:T(8,128)}, f32[8,8,128]{2,1,0:T(8,128)S(1)}, u32[]{:S(2)}) copy-start(f32[8,8,128]{2,1,0:T(8,128)S(1)} %collective-permute-done.4.xin) | copy-start | bytes 98308
  47.3 0.6 copy-start.6
  49.6 10.2 %collective-permute-start.6 = (f32[8,8,128]{2,1,0:T(8,128)}, f32[8,8,128]{2,1,0:T(8,128)S(1)}, u32[]{:S(2)}, u32[]{:S(2)}) collective-permute-start(f32[8,8,128]{2,1,0:T(8,128)} %get-tuple-element.42), channel_id=1, source_target_pairs={{0,1},{1,0},{2,3},{3,2},{4,5},{5,4},{6,7},{7,6},{8,9},{9,8},{10,11... | collective-permute-start | bytes 98312 | tf_op jit(solution)/shard_map/ppermute | solution.py:399
  49.6 10.2 %collective-permute-start.7 = (f32[8,8,128]{2,1,0:T(8,128)}, f32[8,8,128]{2,1,0:T(8,128)S(1)}, u32[]{:S(2)}, u32[]{:S(2)}) collective-permute-start(f32[8,8,128]{2,1,0:T(8,128)} %get-tuple-element.43), channel_id=1, source_target_pairs={{1,2},{2,1},{3,4},{4,3},{5,6},{6,5},{7,8},{8,7},{9,10},{10,9},{11,... | collective-permute-start | bytes 98312 | tf_op jit(solution)/shard_map/ppermute | solution.py:400
  54.2 0.7 copy-start.1
  57.7 2.0 %collective-permute-start.8 = (f32[8,128]{1,0:T(8,128)}, f32[8,128]{1,0:T(8,128)S(1)}, u32[]{:S(2)}, u32[]{:S(2)}) collective-permute-start(f32[8,128]{1,0:T(8,128)} %coarse.2.mine), channel_id=1, source_target_pairs={{0,32},{32,0},{1,33},{33,1},{2,34},{34,2},{3,35},{35,3},{4,36},{36... | collective-permute-start | bytes 12296 | tf_op jit(solution)/shard_map/ppermute | solution.py:429
  59.7 0.6 copy-start.15
  59.7 0.6 copy-start.16
  60.4 0.6 copy-start.24
  64.9 11.3 %copy-start.28 = (f32[8,8,128]{2,1,0:T(8,128)S(1)}, f32[8,8,128]{2,1,0:T(8,128)}, u32[]{:S(2)}) copy-start(f32[8,8,128]{2,1,0:T(8,128)} %get-tuple-element.45) | copy-start | bytes 98308
  64.9 11.4 %copy-start.27 = (f32[8,8,128]{2,1,0:T(8,128)S(1)}, f32[8,8,128]{2,1,0:T(8,128)}, u32[]{:S(2)}) copy-start(f32[8,8,128]{2,1,0:T(8,128)} %get-tuple-element.46) | copy-start | bytes 98308
  64.9 44.9 %all-to-all-start.1 = ((f32[128,4,128]{2,1,0:T(4,128)}), f32[128,4,128]{2,1,0:T(4,128)S(1)}, u32[]{:S(2)}, u32[]{:S(2)}) async-start(f32[128,4,128]{2,1,0:T(4,128)} %bitcast.26), calls=%async_computation.1 | async-start | bytes 524288 | tf_op jit(solution)/shard_map/all_to_all | solution.py:405
  76.2 2.5 %collective-permute-start.9 = (f32[8,8,128]{2,1,0:T(8,128)S(1)}, f32[8,8,128]{2,1,0:T(8,128)S(1)}, u32[]{:S(2)}, u32[]{:S(2)}) collective-permute-start(f32[8,8,128]{2,1,0:T(8,128)S(1)} %copy-done.28), channel_id=1, source_target_pairs={{0,32},{32,0},{1,33},{33,1},{2,34},{34,2},{3,35},{35,3},{4,36},{36... | collective-permute-start | bytes 98312 | tf_op jit(solution)/shard_map/ppermute | solution.py:392
  76.3 5.6 %collective-permute-start.10 = (f32[8,8,128]{2,1,0:T(8,128)S(1)}, f32[8,8,128]{2,1,0:T(8,128)S(1)}, u32[]{:S(2)}, u32[]{:S(2)}) collective-permute-start(f32[8,8,128]{2,1,0:T(8,128)S(1)} %copy-done.27), channel_id=1, source_target_pairs={{32,64},{64,32},{96,128},{128,96},{160,192},{192,160},{33,65},{65,... | collective-permute-start | bytes 98312 | tf_op jit(solution)/shard_map/ppermute | solution.py:393
  78.7 3.2 %copy-start.10 = (f32[8,8,128]{2,1,0:T(8,128)}, f32[8,8,128]{2,1,0:T(8,128)S(1)}, u32[]{:S(2)}) copy-start(f32[8,8,128]{2,1,0:T(8,128)S(1)} %collective-permute-done.9.xin) | copy-start | bytes 98308
  81.9 0.6 copy-start.11
  84.1 5.9 %collective-permute-start.11 = (f32[8,8,128]{2,1,0:T(8,128)}, f32[8,8,128]{2,1,0:T(8,128)S(1)}, u32[]{:S(2)}, u32[]{:S(2)}) collective-permute-start(f32[8,8,128]{2,1,0:T(8,128)} %get-tuple-element.47), channel_id=1, source_target_pairs={{0,1},{1,0},{2,3},{3,2},{4,5},{5,4},{6,7},{7,6},{8,9},{9,8},{10,11... | collective-permute-start | bytes 98312 | tf_op jit(solution)/shard_map/ppermute | solution.py:399
  85.4 8.1 %collective-permute-start.12 = (f32[8,8,128]{2,1,0:T(8,128)}, f32[8,8,128]{2,1,0:T(8,128)S(1)}, u32[]{:S(2)}, u32[]{:S(2)}) collective-permute-start(f32[8,8,128]{2,1,0:T(8,128)} %get-tuple-element.48), channel_id=1, source_target_pairs={{1,2},{2,1},{3,4},{4,3},{5,6},{6,5},{7,8},{8,7},{9,10},{10,9},{11,... | collective-permute-start | bytes 98312 | tf_op jit(solution)/shard_map/ppermute | solution.py:400
  90.0 3.5 %copy-start.19 = (f32[8,8,128]{2,1,0:T(8,128)}, f32[8,8,128]{2,1,0:T(8,128)S(1)}, u32[]{:S(2)}) copy-start(f32[8,8,128]{2,1,0:T(8,128)S(1)} %collective-permute-done.11.yin) | copy-start | bytes 98308
  93.5 0.6 copy-start.21
  97.4 1.9 %collective-permute-start.13 = (f32[8,8,128]{2,1,0:T(8,128)}, f32[8,8,128]{2,1,0:T(8,128)S(1)}, u32[]{:S(2)}, u32[]{:S(2)}) collective-permute-start(f32[8,8,128]{2,1,0:T(8,128)} %get-tuple-element.50), channel_id=1, source_target_pairs={{0,32},{32,0},{1,33},{33,1},{2,34},{34,2},{3,35},{35,3},{4,36},{36... | collective-permute-start | bytes 98312 | tf_op jit(solution)/shard_map/ppermute | solution.py:392
  97.4 5.4 %collective-permute-start.14 = (f32[8,8,128]{2,1,0:T(8,128)}, f32[8,8,128]{2,1,0:T(8,128)S(1)}, u32[]{:S(2)}, u32[]{:S(2)}) collective-permute-start(f32[8,8,128]{2,1,0:T(8,128)} %get-tuple-element.51), channel_id=1, source_target_pairs={{32,64},{64,32},{96,128},{128,96},{160,192},{192,160},{33,65},{65,... | collective-permute-start | bytes 98312 | tf_op jit(solution)/shard_map/ppermute | solution.py:393
  99.4 3.5 %copy-start.3 = (f32[8,8,128]{2,1,0:T(8,128)}, f32[8,8,128]{2,1,0:T(8,128)S(1)}, u32[]{:S(2)}) copy-start(f32[8,8,128]{2,1,0:T(8,128)S(1)} %collective-permute-done.13.xin) | copy-start | bytes 98308
  102.9 0.6 copy-start.4
  105.1 8.4 %collective-permute-start.15 = (f32[8,8,128]{2,1,0:T(8,128)}, f32[8,8,128]{2,1,0:T(8,128)S(1)}, u32[]{:S(2)}, u32[]{:S(2)}) collective-permute-start(f32[8,8,128]{2,1,0:T(8,128)} %get-tuple-element.52), channel_id=1, source_target_pairs={{0,1},{1,0},{2,3},{3,2},{4,5},{5,4},{6,7},{7,6},{8,9},{9,8},{10,11... | collective-permute-start | bytes 98312 | tf_op jit(solution)/shard_map/ppermute | solution.py:399
  105.1 8.4 %collective-permute-start.16 = (f32[8,8,128]{2,1,0:T(8,128)}, f32[8,8,128]{2,1,0:T(8,128)S(1)}, u32[]{:S(2)}, u32[]{:S(2)}) collective-permute-start(f32[8,8,128]{2,1,0:T(8,128)} %get-tuple-element.53), channel_id=1, source_target_pairs={{1,2},{2,1},{3,4},{4,3},{5,6},{6,5},{7,8},{8,7},{9,10},{10,9},{11,... | collective-permute-start | bytes 98312 | tf_op jit(solution)/shard_map/ppermute | solution.py:400
  109.7 0.7 copy-start
  113.3 1.4 collective-permute-start.17
  113.5 1.2 copy-start.13
  113.6 1.2 copy-start.14
  114.7 0.6 copy-start.23
  118.9 10.5 %copy-start.26 = (f32[8,8,128]{2,1,0:T(8,128)S(1)}, f32[8,8,128]{2,1,0:T(8,128)}, u32[]{:S(2)}) copy-start(f32[8,8,128]{2,1,0:T(8,128)} %get-tuple-element.57) | copy-start | bytes 98308
  118.9 10.7 %copy-start.25 = (f32[8,8,128]{2,1,0:T(8,128)S(1)}, f32[8,8,128]{2,1,0:T(8,128)}, u32[]{:S(2)}) copy-start(f32[8,8,128]{2,1,0:T(8,128)} %get-tuple-element.58) | copy-start | bytes 98308
  118.9 28.1 %all-to-all-start.2 = ((f32[256,1,128]{2,1,0:T(1,128)}), f32[256,1,128]{2,1,0:T(1,128)S(1)}, u32[]{:S(2)}, u32[]{:S(2)}) async-start(f32[256,1,128]{2,1,0:T(1,128)} %bitcast.28), calls=%async_computation.2 | async-start | bytes 262144 | tf_op jit(solution)/shard_map/all_to_all | solution.py:453
  129.4 2.7 %collective-permute-start.18 = (f32[8,8,128]{2,1,0:T(8,128)S(1)}, f32[8,8,128]{2,1,0:T(8,128)S(1)}, u32[]{:S(2)}, u32[]{:S(2)}) collective-permute-start(f32[8,8,128]{2,1,0:T(8,128)S(1)} %copy-done.26), channel_id=1, source_target_pairs={{0,32},{32,0},{1,33},{33,1},{2,34},{34,2},{3,35},{35,3},{4,36},{36... | collective-permute-start | bytes 98312 | tf_op jit(solution)/shard_map/ppermute | solution.py:392
  129.6 5.3 %collective-permute-start.19 = (f32[8,8,128]{2,1,0:T(8,128)S(1)}, f32[8,8,128]{2,1,0:T(8,128)S(1)}, u32[]{:S(2)}, u32[]{:S(2)}) collective-permute-start(f32[8,8,128]{2,1,0:T(8,128)S(1)} %copy-done.25), channel_id=1, source_target_pairs={{32,64},{64,32},{96,128},{128,96},{160,192},{192,160},{33,65},{65,... | collective-permute-start | bytes 98312 | tf_op jit(solution)/shard_map/ppermute | solution.py:393
  132.1 2.9 %copy-start.7 = (f32[8,8,128]{2,1,0:T(8,128)}, f32[8,8,128]{2,1,0:T(8,128)S(1)}, u32[]{:S(2)}) copy-start(f32[8,8,128]{2,1,0:T(8,128)S(1)} %collective-permute-done.18.xin) | copy-start | bytes 98308
  134.9 0.6 copy-start.8
  137.2 7.4 %collective-permute-start.20 = (f32[8,8,128]{2,1,0:T(8,128)}, f32[8,8,128]{2,1,0:T(8,128)S(1)}, u32[]{:S(2)}, u32[]{:S(2)}) collective-permute-start(f32[8,8,128]{2,1,0:T(8,128)} %get-tuple-element.59), channel_id=1, source_target_pairs={{0,1},{1,0},{2,3},{3,2},{4,5},{5,4},{6,7},{7,6},{8,9},{9,8},{10,11... | collective-permute-start | bytes 98312 | tf_op jit(solution)/shard_map/ppermute | solution.py:399
  138.9 8.1 %collective-permute-start.21 = (f32[8,8,128]{2,1,0:T(8,128)}, f32[8,8,128]{2,1,0:T(8,128)S(1)}, u32[]{:S(2)}, u32[]{:S(2)}) collective-permute-start(f32[8,8,128]{2,1,0:T(8,128)} %get-tuple-element.60), channel_id=1, source_target_pairs={{1,2},{2,1},{3,4},{4,3},{5,6},{6,5},{7,8},{8,7},{9,10},{10,9},{11,... | collective-permute-start | bytes 98312 | tf_op jit(solution)/shard_map/ppermute | solution.py:400
  144.6 2.4 %copy-start.17 = (f32[8,8,128]{2,1,0:T(8,128)}, f32[8,8,128]{2,1,0:T(8,128)S(1)}, u32[]{:S(2)}) copy-start(f32[8,8,128]{2,1,0:T(8,128)S(1)} %collective-permute-done.20.yin) | copy-start | bytes 98308
  147.0 0.6 copy-start.18
  147.0 0.7 copy-start.2

commit v2 on v1

v2 whole, which is shorter than its diff:
```python
import functools
import math

import jax
import jax.numpy as jnp
import numpy as np
from jax import lax
from jax.experimental import pallas as pl
from jax.experimental.pallas import tpu as pltpu
from jax.sharding import Mesh
from jax.sharding import PartitionSpec as P


EX = 8
EY = 32
EZ = 128
STRETCH = (1.0, 64.0, 1.0)
CHIPS = 128
MODES = (EX - 1) * (EY - 1)
MODES_PAD = 224
F32 = jnp.float32
BF16 = jnp.bfloat16


def legendre(order, x):
    before, now = 1.0, x
    for n in range(2, order + 1):
        before, now = now, ((2 * n - 1) * x * now - (n - 1) * before) / n
    return now


def gll_points():
    points = [-1.0]
    for n in range(1, 7):
        x = -math.cos(math.pi * n / 7.0)
        for _ in range(60):
            x = x - (legendre(8, x) - legendre(6, x)) / (15.0 * legendre(7, x))
        points.append(x)
    points.append(1.0)
    return points


@functools.lru_cache(maxsize=None)
def spectral_tables():
    nodes = gll_points()
    values = [legendre(7, x) for x in nodes]
    w = np.array([2.0 / (56.0 * v * v) for v in values])
    deriv = np.zeros((8, 8))
    for i in range(8):
        for j in range(8):
            if i != j:
                deriv[i, j] = values[i] / (values[j] * (nodes[i] - nodes[j]))
    deriv[0, 0] = -14.0
    deriv[7, 7] = 14.0
    stiff = deriv.T @ np.diag(w) @ deriv
    stiff[0, 0] *= 2.0
    stiff[7, 7] *= 2.0
    root = 1.0 / np.sqrt(w)
    lam, vec = np.linalg.eigh(root[:, None] * stiff * root[None, :])
    basis = root[:, None] * vec
    x = np.array(nodes)
    hat = np.stack([(1.0 - x) / 2.0, (1.0 + x) / 2.0])
    hat[0, 7] = 0.0
    hat[1, 0] = 0.0
    return w, deriv, basis, lam, hat


def sine_system(cells):
    n = np.arange(1, cells)
    table = math.sqrt(2.0 / cells) * np.sin(math.pi * ((n[:, None] * n[None, :]) % (2 * cells)) / cells)
    cosines = np.cos(math.pi * n / cells)
    return table, (2.0 - 2.0 * cosines) / 2.0, 2.0 * (4.0 + 2.0 * cosines) / 6.0


@functools.lru_cache(maxsize=None)
def all_tables():
    w, deriv, basis, lam, hat = spectral_tables()
    denom = (
        STRETCH[0] * lam[:, None, None] + STRETCH[1] * lam[None, :, None] + STRETCH[2] * lam[None, None, :]
    )
    big = np.kron(np.kron(basis, basis), basis)
    full = ((big / denom.reshape(1, 512)) @ big.T).reshape(8, 8, 8, 8, 8, 8)
    local_solve = []
    for si in (1.0, -1.0):
        for sj in (1.0, -1.0):
            t = full[:4, :4]
            t = 0.5 * (t[:, :, :, :4] + si * t[:, :, :, 7:3:-1])
            t = 0.5 * (t[:, :, :, :, :4] + sj * t[:, :, :, :, 7:3:-1])
            local_solve.append(t.reshape(128, 128))
    local_solve = np.stack(local_solve)
    tx, sx, mx = sine_system(EX)
    ty, sy, my = sine_system(EY)
    tz, sz, mz = sine_system(EZ)
    vx = np.zeros((EX + 1, EX - 1))
    vx[1:-1] = tx
    vy = np.zeros((EY + 1, EY - 1))
    vy[1:-1] = ty
    vz = np.zeros((EZ + 1, EZ))
    vz[1:-1, : EZ - 1] = tz
    z_low, z_high = vz[:-1], vz[1:]
    eig = (
        STRETCH[0] * sx[:, None, None] * my[None, :, None] * mz[None, None, :]
        + STRETCH[1] * mx[:, None, None] * sy[None, :, None] * mz[None, None, :]
        + STRETCH[2] * mx[:, None, None] * my[None, :, None] * sz[None, None, :]
    )
    inv_eig = np.zeros((MODES_PAD, EZ))
    inv_eig[:MODES, : EZ - 1] = (1.0 / eig).reshape(MODES, EZ - 1)
    part = np.zeros((MODES, EX // 2, EY, 2, 2))
    for a in range(2):
        for b in range(2):
            rows_x = vx[a : a + EX - 1 : 2]
            rows_y = vy[b : b + EY]
            part[:, :, :, a, b] = np.einsum("xm,yn->mnxy", rows_x, rows_y).reshape(MODES, EX // 2, EY)
    gather = np.zeros((MODES_PAD, 4 * CHIPS))
    gather[:MODES] = part.reshape(MODES, 4 * CHIPS)
    flip = np.array([1.0 if m % 2 == 0 else -1.0 for m in range(EX - 1)])
    own_x = np.zeros((EX, 8, MODES_PAD))
    for x in range(EX):
        for row in range(8):
            side, a = row // 4, row // 2 % 2
            sign = flip if x % 2 else 1.0
            own_x[x, row, :MODES] = np.repeat(sign * vx[(x ^ side) + a], EY - 1)
    own_y = np.zeros((EY + 8, MODES_PAD))
    own_y[: EY + 1, :MODES] = np.tile(vy, (1, EX - 1))
    lanes = np.ones((1, 128))
    roll_tables = np.zeros((19, 8, 128))
    for s in range(8):
        for r in range(8):
            roll_tables[s, r] = deriv[r, (r - s) % 8]
            roll_tables[8 + s, r] = deriv[(r - s) % 8, r]
    roll_tables[16] = hat[0][:, None] * lanes
    roll_tables[17] = hat[1][:, None] * lanes
    roll_tables[18] = w[:, None] * lanes
    f = lambda t: np.asarray(t, np.float32)

    def split(t):
        high = t.astype(BF16)
        return np.stack([high, (t - high.astype(np.float64)).astype(BF16)])

    return dict(
        deriv=f(deriv),
        hat=f(hat),
        local_solve=split(local_solve),
        z_in=split(np.concatenate([z_low, z_high], axis=1)),
        z_out=split(np.concatenate([z_low.T, z_high.T], axis=1)),
        inv_eig=f(inv_eig),
        gather=split(gather),
        own_x=f(own_x),
        own_y=f(own_y),
        rolls=f(roll_tables),
        weight=w,
    )


FACE = jax.ShapeDtypeStruct((8, 8, 128), F32)
FACES = (FACE,) * 4
NODES = jax.ShapeDtypeStruct((8, 8, 8, 128), F32)
ROWS = jax.ShapeDtypeStruct((4 * CHIPS, 128), F32)
SMALL = jax.ShapeDtypeStruct((8, 128), F32)
VMEM = pl.BlockSpec(memory_space=pltpu.VMEM)
SMEM = pl.BlockSpec(memory_space=pltpu.SMEM)


def call(body, outs, place, *args, scratch=(), specs=None):
    return pl.pallas_call(
        body,
        out_shape=outs,
        in_specs=[SMEM] + (specs or [VMEM] * len(args)),
        out_specs=[VMEM] * len(outs),
        scratch_shapes=list(scratch),
        compiler_params=pltpu.CompilerParams(vmem_limit_bytes=12 << 20),
    )(place, *args)


def parts(x):
    high = x.astype(jnp.bfloat16)
    return high, (x - high.astype(F32)).astype(jnp.bfloat16)


def dot(a, b):
    return jnp.dot(a, b, preferred_element_type=F32)


def table_dot(table, x):
    high, low = parts(x)
    return dot(table[0], high) + (dot(table[0], low) + dot(table[1], high))


def dot_table(x, table):
    high, low = parts(x)
    first = dot(jnp.concatenate([high, low], axis=0), table[0])
    return first[0:8] + (first[8:16] + dot(high, table[1]))


def inner_x(place):
    return 7 * (1 - (place[0] & 1))


def inner_y(place):
    return 7 * (1 - (place[1] & 1))


def put_faces(place, u, faces):
    xin, xout, yin, yout = faces
    ax, ay = inner_x(place), inner_y(place)
    xin[...] = u[ax]
    xout[...] = u[7 - ax]
    for i in range(8):
        yin[i] = u[i, ay]
        yout[i] = u[i, 7 - ay]


def lane_iota():
    return lax.broadcasted_iota(jnp.int32, (8, 128), 1)


def row_iota():
    return lax.broadcasted_iota(jnp.int32, (8, 128), 0)


def weighted(coefs, vals):
    out = None
    for c, v in zip(coefs, vals):
        if c != 0.0:
            t = v if c == 1.0 else float(c) * v
            out = t if out is None else out + t
    return out


def restrict_rows(place, u, rolls, z_in):
    hat = all_tables()["hat"]
    near = [[weighted(hat[b], [u[i, j] for j in range(8)]) for i in range(8)] for b in range(2)]
    corner = [[weighted(hat[a], near[b]) for b in range(2)] for a in range(2)]
    row = row_iota()
    odd = (place[0] & 1) == 1
    out = jnp.zeros((8, 128), F32)
    for c in range(2):
        for a in range(2):
            for b in range(2):
                line = jnp.sum(rolls[16 + c] * corner[a][b], axis=0, keepdims=True)
                at = jnp.where(odd, 4 * c + 2 * (1 - a) + b, 4 * c + 2 * a + b)
                out = jnp.where(row == at, line, out)
    modes = dot_table(out, z_in)
    return modes[0:4, 0:128] + modes[4:8, 128:256]


def send_rows(rows, out):
    pair = jnp.concatenate([rows, rows], axis=0)
    for t in range(4 * CHIPS // 8):
        out[8 * t : 8 * t + 8] = pair


def assemble(place, u, xin, xout, yin, yout, v):
    ax, ay = inner_x(place), inner_y(place)
    keep_x = jnp.where((place[0] == 0) | (place[0] == EX - 1), 0.0, 1.0).astype(F32)
    keep_y = jnp.where((place[1] == 0) | (place[1] == EY - 1), 0.0, 1.0).astype(F32)
    v[...] = u[...]
    v[ax] = v[ax] + xin[...]
    v[7 - ax] = (v[7 - ax] + xout[...]) * keep_x
    for i in range(8):
        v[i, ay] = v[i, ay] + yin[i]
        v[i, 7 - ay] = (v[i, 7 - ay] + yout[i]) * keep_y
    v[7 - ax] = v[7 - ax] * keep_x
    lane, row = lane_iota(), row_iota()
    first, last = row == 0, row == 7
    keep_z = jnp.where((first & (lane == 0)) | (last & (lane == 127)), 0.0, 1.0).astype(F32)
    for i in range(8):
        for j in range(8):
            t = v[i, j]
            from_prev = pltpu.roll(pltpu.roll(t, 1, 1), 1, 0)
            from_next = pltpu.roll(pltpu.roll(t, 127, 1), 7, 0)
            t = t + jnp.where(first, from_prev, 0.0) + jnp.where(last, from_next, 0.0)
            v[i, j] = t * keep_z


def lines(vals, weights, deriv):
    even = 0.5 * (deriv[:4, :4] + deriv[:4, 7:3:-1])
    odd = 0.5 * (deriv[:4, :4] - deriv[:4, 7:3:-1])
    sums = [vals[i] + vals[7 - i] for i in range(4)]
    difs = [vals[i] - vals[7 - i] for i in range(4)]
    u, v = [], []
    for p in range(4):
        e, o = weighted(even[p], sums), weighted(odd[p], difs)
        q, r = (o + e) * weights[p], (o - e) * weights[7 - p]
        u.append(q - r)
        v.append(q + r)
    out = [None] * 8
    for i in range(4):
        e, o = weighted(even[:, i], u), weighted(odd[:, i], v)
        out[i], out[7 - i] = e + o, e - o
    return out


def stiffness(u, cw, rolls, out):
    deriv = all_tables()["deriv"].astype(np.float64)
    for j in range(8):
        r = lines([u[i, j] for i in range(8)], [cw[i, j] for i in range(8)], deriv)
        for i in range(8):
            out[i, j] = r[i]
    for i in range(8):
        r = lines([u[i, j] for j in range(8)], [cw[i, j] for j in range(8)], deriv)
        for j in range(8):
            t = u[i, j]
            g = rolls[0] * t
            for s in range(1, 8):
                g = g + rolls[s] * pltpu.roll(t, s, 0)
            q = g * cw[i, j]
            k = rolls[8] * q
            for s in range(1, 8):
                k = k + rolls[8 + s] * pltpu.roll(q, s, 0)
            out[i, j] = out[i, j] + (STRETCH[1] * r[j] + k)


def prolong_add(coarse, rolls, z_out, v):
    hat = all_tables()["hat"]
    both = dot_table(coarse, z_out)
    low, high = both[:, 0:128], both[:, 128:256]
    h0, h1 = rolls[16], rolls[17]
    line = [h0 * low[r : r + 1] + h1 * high[r : r + 1] for r in range(4)]
    for j in range(8):
        near = float(hat[0, j]) * line[0] + float(hat[1, j]) * line[1]
        far = float(hat[0, j]) * line[2] + float(hat[1, j]) * line[3]
        for i in range(8):
            v[i, j] = v[i, j] + (float(hat[0, i]) * near + float(hat[1, i]) * far)


def total(a, b):
    return jnp.sum(a[...] * b[...], keepdims=True).reshape(1, 1)


def k_faces(place, u, xin, xout, yin, yout, sems):
    ax, ay = inner_x(place), inner_y(place)
    sources = (u.at[ax], u.at[7 - ax], u.at[:, ay], u.at[:, 7 - ay])
    copies = [
        pltpu.make_async_copy(source, face, sems.at[n])
        for n, (source, face) in enumerate(zip(sources, (xin, xout, yin, yout)))
    ]
    for copy in copies:
        copy.start()
    for copy in copies:
        copy.wait()


def k_restrict(place, u, coefficient, rolls, z_in, rows, cw):
    send_rows(restrict_rows(place, u, rolls, z_in), rows)
    w = all_tables()["weight"]
    for i in range(8):
        for j in range(8):
            cw[i, j] = coefficient[i, j] * (float(w[i] * w[j]) * rolls[18])


def k_local_solve(place, u, xin, xout, yin, yout, solve, v, h, *faces):
    assemble(place, u, xin, xout, yin, yout, v)
    out = []
    for si in range(2):
        for sj in range(2):
            block = []
            for i in range(4):
                for j in range(4):
                    near, far = v[i, j], v[7 - i, j]
                    near_j, far_j = v[i, 7 - j], v[7 - i, 7 - j]
                    left = near - far if si else near + far
                    right = near_j - far_j if si else near_j + far_j
                    block.append(left - right if sj else left + right)
            high, low = parts(jnp.concatenate(block, axis=0))
            t, t_low = solve[0, 2 * si + sj], solve[1, 2 * si + sj]
            out.append((dot(t, high) + (dot(t, low) + dot(t_low, high))).reshape(4, 4, 8, 128))
    for i in range(4):
        for j in range(4):
            pp, pm, mp, mm = (block[i, j] for block in out)
            a, b, c, d = pp + pm, pp - pm, mp + mm, mp - mm
            h[i, j] = a + c
            h[7 - i, j] = a - c
            h[i, 7 - j] = b + d
            h[7 - i, 7 - j] = b - d
    put_faces(place, h, faces)


def k_coarse(place, got, gather, inv_eig, own_x, own_y, out):
    core = place[2]
    size = CHIPS
    blocks = [got[pl.ds(pl.multiple_of(size * (n + core * (3 - 2 * n)), size), size)] for n in range(4)]
    modes = table_dot(gather, jnp.concatenate(blocks, axis=0)) * inv_eig[...]
    row = lax.broadcasted_iota(jnp.int32, (8, MODES_PAD), 0)
    low, high = own_y[pl.ds(place[1], 1)], own_y[pl.ds(place[1] + 1, 1)]
    own = own_x[place[0]] * jnp.where((row & 1) == 0, low, high)
    own_high, own_low = parts(own)
    high, low = parts(modes)
    first = dot(jnp.concatenate([own_high, own_low], axis=0), high)
    mine = first[0:8] + (first[8:16] + dot(own_high, low))
    sums = jnp.sum(got[...].reshape(4 * CHIPS // 8, 8, 128), axis=0)
    sums = sums + pltpu.roll(sums, 4, 0)
    out[...] = jnp.where(lane_iota() == 127, sums, mine)


def both_halves(mine, theirs):
    return mine[...] + pltpu.roll(theirs[...], 4, 0)


def k_first(
    place, h, xin, xout, yin, yout, mine, theirs, f, cw, rolls, z_out, z_in, s, g, rows, *faces
):
    assemble(place, h, xin, xout, yin, yout, s)
    prolong_add(both_halves(mine, theirs), rolls, z_out, s)
    stiffness(s, cw, rolls, g)
    put_faces(place, g, faces)
    modes = restrict_rows(place, g, rolls, z_in)
    lane, row = lax.broadcasted_iota(jnp.int32, (4, 128), 1), lax.broadcasted_iota(jnp.int32, (4, 128), 0)
    sums = jnp.where(row == 0, total(f, s), jnp.where(row == 1, total(s, g), 0.0))
    send_rows(jnp.where(lane == 127, sums, modes), rows)


def k_second(
    place, h, xin, xout, yin, yout, mine, theirs, f, s0, g0, cw, rolls, z_out,
    s1, h1, rows, scalars, *rest,
):
    faces, t = rest[:4], rest[4]
    assemble(place, h, xin, xout, yin, yout, t)
    coarse = both_halves(mine, theirs)
    prolong_add(coarse, rolls, z_out, t)
    lane = lane_iota()
    known = jnp.sum(jnp.where(lane == 127, coarse, 0.0), axis=1, keepdims=True)
    energy, curve = known[0:1], known[1:2]
    step = energy / curve
    s1[...] = s0[...] - step * t[...]
    stiffness(s1, cw, rolls, h1)
    put_faces(place, h1, faces)
    fresh = jnp.sum(s1[...] * (f[...] - step * g0[...]), keepdims=True).reshape(1, 1)
    sums = (fresh, total(s1, h1), total(s1, g0), total(s0, h1))
    row = jnp.zeros((8, 128), F32)
    for n, value in enumerate(sums):
        row = jnp.where(lane == n, value, row)
    for n in range(2 * CHIPS // 8):
        rows[8 * n : 8 * n + 8] = row
    scalars[...] = jnp.where(lane == 0, energy, jnp.where(lane == 1, curve, step))


def k_last(place, h, xin, xout, yin, yout, got, scalars, s0, s1, b, w, p, r):
    sums = jnp.sum(got[...], axis=0, keepdims=True)
    fresh, s1h1, s1g0, s0h1 = (sums[:, n : n + 1] for n in range(4))
    energy, curve, step0 = (scalars[0:1, n : n + 1] for n in range(3))
    beta = fresh / energy
    step1 = fresh / (s1h1 + beta * (s1g0 + s0h1) + beta * beta * curve)
    assemble(place, h, xin, xout, yin, yout, r)
    p[...] = step0 * s0[...] + step1 * (s1[...] + beta * s0[...])
    r[...] = (b[...] - step0 * w[...]) - step1 * (r[...] + beta * w[...])


CHIP_AXES = ("x", "y", "z")
ALL_AXES = ("x", "c", "y", "z")
SWAP = [(0, 1), (1, 0)]


def pairs(count, start):
    out = []
    for n in range(start, count, 2):
        out += [(n, (n + 1) % count), ((n + 1) % count, n)]
    return out


def swap_x(inner, outer):
    far = lax.ppermute(outer, ("x", "c"), pairs(EX, 1))
    near = lax.ppermute(inner, "c", SWAP)
    return near, far


def swap_y(inner, outer):
    far = lax.ppermute(outer, ("y", "z"), pairs(EY, 1))
    near = lax.ppermute(inner, ("y", "z"), pairs(EY, 0))
    return near, far


def share(rows):
    got = lax.all_to_all(rows.reshape(CHIPS, 4, 128), CHIP_AXES, 0, 0)
    return got.reshape(4 * CHIPS, 128)


def on_device(forcing, coefficient):
    tables = all_tables()
    tab = lambda *names: [jnp.asarray(tables[n]) for n in names]
    f = forcing.reshape(8, 8, 8, 128)
    coef = coefficient.reshape(8, 8, 8, 128)
    px = lax.axis_index(("x", "c")).astype(jnp.int32)
    py = lax.axis_index(("y", "z")).astype(jnp.int32)
    n = jnp.arange(4, dtype=jnp.int32)
    place = jnp.where(n == 0, px, jnp.where(n == 1, py, px & 1))

    inside = jnp.arange(8, dtype=jnp.int32)[:, None, None] == 7 * (1 - (px & 1))
    outside = jnp.arange(8, dtype=jnp.int32)[:, None, None] == 7 * (px & 1)
    even = (py & 1) == 0

    def y_face(raw, last, xin, xout):
        near = jnp.where(last, xin[7], xin[0])[None]
        far = jnp.where(last, xout[7], xout[0])[None]
        return raw + jnp.where(inside, near, jnp.where(outside, far, 0.0))

    def halo(xin, xout, yin, yout):
        xs = swap_x(xin, xout)
        ys = swap_y(y_face(yin, even, *xs), y_face(yout, ~even, *xs))
        return xs + ys

    def coarse(rows):
        got = share(rows)
        mine = call(k_coarse, (SMALL,), place, got, *tab("gather", "inv_eig", "own_x", "own_y"))[0]
        return mine, lax.ppermute(mine, "c", SWAP)

    def local(u, sides):
        out = call(k_local_solve, (NODES, NODES) + FACES, place, u, *sides, *tab("local_solve"))
        return out[0], out[1], out[2:]

    faces = call(
        k_faces, FACES, place, f,
        specs=[pl.BlockSpec(memory_space=pl.ANY)], scratch=(pltpu.SemaphoreType.DMA((4,)),),
    )
    rows, cw = call(k_restrict, (ROWS, NODES), place, f, coef, *tab("rolls", "z_in"))
    c0 = coarse(rows)
    b, h, faces = local(f, halo(*faces))
    s0, g0, rows, *faces1 = call(
        k_first, (NODES, NODES, ROWS) + FACES, place, h, *halo(*faces), *c0, f, cw,
        *tab("rolls", "z_out", "z_in"),
    )
    c1 = coarse(rows)
    w, h, faces = local(g0, halo(*faces1))
    s1, h1, rows, scalars, *faces1 = call(
        k_second,
        (NODES, NODES, jax.ShapeDtypeStruct((2 * CHIPS, 128), F32), SMALL) + FACES,
        place, h, *halo(*faces), *c1, f, s0, g0, cw, *tab("rolls", "z_out"),
        scratch=(pltpu.VMEM((8, 8, 8, 128), F32),),
    )
    got = lax.all_to_all(rows.reshape(2 * CHIPS, 1, 128), ALL_AXES, 0, 0).reshape(2 * CHIPS, 128)
    sides = halo(*faces1)
    p, r = call(k_last, (NODES, NODES), place, h1, *sides, got, scalars, s0, s1, b, w)
    return p.reshape(forcing.shape), r.reshape(forcing.shape)


def solution(mesh):
    fine = Mesh(mesh.devices.reshape(4, 2, 4, 8), ALL_AXES)
    spec = P(None, None, None, ("x", "c"), ("y", "z"), None)
    return jax.shard_map(
        on_device, mesh=fine, in_specs=(spec, spec), out_specs=(spec, spec), check_vma=False
    )
```

time: 151 us -> 115 us (0.76)
  the two profiles are of different devices: /device:TPU:10 before, /device:TPU:1 now
where the time goes in v2:
time: 115 us
  starting transfers between devices  58.5 us (51%)
  waiting for transfers between devices  39.7 us (35%)
  Pallas kernels  13.1 us (11%)
  local copies, waits for them, and re-layouts  1.94 us (2%)
    ppermute x5, starting transfers between devices, swap_y(): far = lax.ppermute(outer, ('y', 'z'), pairs(EY, 1))  22.3 us
    all_to_all x2, starting transfers between devices, share(): got = lax.all_to_all(rows.reshape(CHIPS, 4, 128), CHIP_AXES, 0, 0)  14.1 us
    pallas_call x9, Pallas kernels, call(): pl.pallas_call(body, out_shape=outs, in_specs=[SMEM] + (specs or [VMEM] *...  13.1 us
    ppermute x5, waiting for transfers between devices, swap_x(): far = lax.ppermute(outer, ('x', 'c'), pairs(EX, 1))  12.4 us
    all_to_all x2, waiting for transfers between devices, share(): got = lax.all_to_all(rows.reshape(CHIPS, 4, 128), CHIP_AXES, 0, 0)  12.1 us
    ppermute x5, starting transfers between devices, swap_x(): near = lax.ppermute(inner, 'c', SWAP)  9.3 us
    ppermute x5, waiting for transfers between devices, swap_y(): far = lax.ppermute(outer, ('y', 'z'), pairs(EY, 1))  8.6 us
    all_to_all x1, starting transfers between devices, on_device(): lax.all_to_all(rows.reshape(2 * CHIPS, 1, 128), ALL_AXES, 0, 0)  5.17 us
  transfers between devices with their start and end apart: 25, of which 16 were waited for; matrix products, arithmetic and copies ran while one was open for 0% of the time, Pallas kernels for 3%

profile of v2, /device:TPU:1, one launch (start us, length us, event | category | flops | bytes accessed | tf_op | source)
XLA Modules:
  0.0 114.5 jit_solution(9188831833471401231)
XLA Ops:
  0.7 0.0 copy-start
  0.7 0.9 copy-done
  1.6 0.7 shard_map.113
  2.3 3.3 %collective-permute-start = (f32[8,8,128]{2,1,0:T(8,128)S(1)}, f32[8,8,128]{2,1,0:T(8,128)S(1)}, u32[]{:S(2)}, u32[]{:S(2)}) collective-permute-start(f32[8,8,128]{2,1,0:T(8,128)S(1)} %get-tuple-element.37), channel_id=1, source_target_pairs={{0,32},{32,0},{1,33},{33,1},{2,34},{34,2},{3,35},{35,3},{4,36},{36... | collective-permute-start | bytes 98312 | tf_op jit(solution)/shard_map/ppermute | solution.py:463
  5.6 0.0 collective-permute-start.1
  5.6 0.9 collective-permute-done.xin
  6.5 2.5 %collective-permute-done.1.xout = f32[8,8,128]{2,1,0:T(8,128)S(1)} collective-permute-done((f32[8,8,128]{2,1,0:T(8,128)S(1)}, f32[8,8,128]{2,1,0:T(8,128)S(1)}, u32[]{:S(2)}, u32[]{:S(2)}) %collective-permute-start.1) | collective-permute-done | bytes 32800 | tf_op jit(solution)/shard_map/ppermute | solution.py:462
  8.9 0.1 select_add_fusion.8
  9.0 6.4 %collective-permute-start.3 = (f32[8,8,128]{2,1,0:T(8,128)S(1)}, f32[8,8,128]{2,1,0:T(8,128)S(1)}, u32[]{:S(2)}, u32[]{:S(2)}) collective-permute-start(f32[8,8,128]{2,1,0:T(8,128)S(1)} %get-tuple-element.104), channel_id=1, source_target_pairs={{1,2},{2,1},{3,4},{4,3},{5,6},{6,5},{7,8},{8,7},{9,10},{10,9},{11,... | collective-permute-start | bytes 98312 | tf_op jit(solution)/shard_map/ppermute | solution.py:468
  15.4 1.3 %collective-permute-done.3.yout = f32[8,8,128]{2,1,0:T(8,128)S(1)} collective-permute-done((f32[8,8,128]{2,1,0:T(8,128)S(1)}, f32[8,8,128]{2,1,0:T(8,128)S(1)}, u32[]{:S(2)}, u32[]{:S(2)}) %collective-permute-start.3) | collective-permute-done | bytes 32800 | tf_op jit(solution)/shard_map/ppermute | solution.py:468
  16.7 1.8 %collective-permute-done.2.yin = f32[8,8,128]{2,1,0:T(8,128)S(1)} collective-permute-done((f32[8,8,128]{2,1,0:T(8,128)S(1)}, f32[8,8,128]{2,1,0:T(8,128)S(1)}, u32[]{:S(2)}, u32[]{:S(2)}) %collective-permute-start.2) | collective-permute-done | bytes 32800 | tf_op jit(solution)/shard_map/ppermute | solution.py:469
  18.5 0.9 copy-done.3
  19.5 1.1 shard_map.114
  20.5 2.5 %collective-permute-start.4 = (f32[8,8,128]{2,1,0:T(8,128)S(1)}, f32[8,8,128]{2,1,0:T(8,128)S(1)}, u32[]{:S(2)}, u32[]{:S(2)}) collective-permute-start(f32[8,8,128]{2,1,0:T(8,128)S(1)} %get-tuple-element.42), channel_id=1, source_target_pairs={{0,32},{32,0},{1,33},{33,1},{2,34},{34,2},{3,35},{35,3},{4,36},{36... | collective-permute-start | bytes 98312 | tf_op jit(solution)/shard_map/ppermute | solution.py:463
  23.1 1.4 %shard_map.115 = (f32[512,128]{1,0:T(8,128)}, f32[8,8,8,128]{3,2,1,0:T(8,128)S(1)}) custom-call(s32[4]{0:T(128)S(1)} %compare_select_fusion.1.place, f32[8,8,8,128]{3,2,1,0:T(8,128)S(1)} %bitcast.58, f32[8,8,8,128]{3,2,1,0:T(8,128)S(1)} %bitcast.64, f32[19,8,128]{2,1,0:T(8,128)S(1)} %copy-done.5, bf16[2,128,256]{2,1,0:T(8,128)(2,1)S(1)} %copy-done.7), custom_call_target="tpu_custom_call" | custom-call | tf_op jit(solution)/shard_map/pallas_call | solution.py:165
  24.5 7.9 %all-to-all-start = ((f32[128,4,128]{2,1,0:T(4,128)}), f32[128,4,128]{2,1,0:T(4,128)S(1)}, u32[]{:S(2)}, u32[]{:S(2)}) async-start(f32[128,4,128]{2,1,0:T(4,128)} %bitcast.10), calls=%async_computation | async-start | bytes 524288 | tf_op jit(solution)/shard_map/all_to_all | solution.py:474
  32.5 0.0 copy-start.8
  32.5 1.4 %collective-permute-start.5 = (f32[8,8,128]{2,1,0:T(8,128)S(1)}, f32[8,8,128]{2,1,0:T(8,128)S(1)}, u32[]{:S(2)}, u32[]{:S(2)}) collective-permute-start(f32[8,8,128]{2,1,0:T(8,128)S(1)} %get-tuple-element.43), channel_id=1, source_target_pairs={{32,64},{64,32},{96,128},{128,96},{160,192},{192,160},{224,0},{0,2... | collective-permute-start | bytes 98312 | tf_op jit(solution)/shard_map/ppermute | solution.py:462
  33.9 0.0 collective-permute-done.4.xin
  33.9 2.5 %collective-permute-done.5.xout = f32[8,8,128]{2,1,0:T(8,128)S(1)} collective-permute-done((f32[8,8,128]{2,1,0:T(8,128)S(1)}, f32[8,8,128]{2,1,0:T(8,128)S(1)}, u32[]{:S(2)}, u32[]{:S(2)}) %collective-permute-start.5) | collective-permute-done | bytes 32800 | tf_op jit(solution)/shard_map/ppermute | solution.py:462
  36.4 0.1 select_add_fusion.6
  36.5 4.6 %collective-permute-start.7 = (f32[8,8,128]{2,1,0:T(8,128)S(1)}, f32[8,8,128]{2,1,0:T(8,128)S(1)}, u32[]{:S(2)}, u32[]{:S(2)}) collective-permute-start(f32[8,8,128]{2,1,0:T(8,128)S(1)} %get-tuple-element.102), channel_id=1, source_target_pairs={{1,2},{2,1},{3,4},{4,3},{5,6},{6,5},{7,8},{8,7},{9,10},{10,9},{11,... | collective-permute-start | bytes 98312 | tf_op jit(solution)/shard_map/ppermute | solution.py:468
  41.1 0.0 collective-permute-start.6
  41.1 5.7 %all-to-all-done = f32[128,4,128]{2,1,0:T(4,128)S(1)} async-done(((f32[128,4,128]{2,1,0:T(4,128)}), f32[128,4,128]{2,1,0:T(4,128)S(1)}, u32[]{:S(2)}, u32[]{:S(2)}) %all-to-all-start) | async-done | bytes 262176 | tf_op jit(solution)/shard_map/all_to_all | solution.py:474
  46.8 0.0 copy-start.6
  46.8 1.0 shard_map.116.mine
  47.8 1.7 %collective-permute-start.8 = (f32[8,128]{1,0:T(8,128)S(1)}, f32[8,128]{1,0:T(8,128)S(1)}, u32[]{:S(2)}, u32[]{:S(2)}) collective-permute-start(f32[8,128]{1,0:T(8,128)S(1)} %shard_map.116.mine), channel_id=1, source_target_pairs={{0,32},{32,0},{1,33},{33,1},{2,34},{34,2},{3,35},{35,3},{4,36},{36... | collective-permute-start | bytes 12296 | tf_op jit(solution)/shard_map/ppermute | solution.py:505
  49.6 0.8 collective-permute-done.8.theirs
  50.4 2.5 %shard_map.117 = (f32[8,8,8,128]{3,2,1,0:T(8,128)S(1)}, f32[8,8,8,128]{3,2,1,0:T(8,128)S(1)}, f32[512,128]{1,0:T(8,128)}, f32[8,8,128]{2,1,0:T(8,128)S(1)}, f32[...) custom-call(s32[4]{0:T(128)S(1)} %compare_select_fusion.1.place, ...), custom_call_target="tpu_custom_call" | custom-call | tf_op jit(solution)/shard_map/pallas_call | solution.py:165
  52.9 0.3 collective-permute-start.9
  53.2 0.0 collective-permute-start.10
  53.2 0.9 collective-permute-done.9.xin
  54.1 2.5 %collective-permute-done.10.xout = f32[8,8,128]{2,1,0:T(8,128)S(1)} collective-permute-done((f32[8,8,128]{2,1,0:T(8,128)S(1)}, f32[8,8,128]{2,1,0:T(8,128)S(1)}, u32[]{:S(2)}, u32[]{:S(2)}) %collective-permute-start.10) | collective-permute-done | bytes 32800 | tf_op jit(solution)/shard_map/ppermute | solution.py:462
  56.6 0.1 select_add_fusion.4
  56.7 0.2 collective-permute-start.12
  56.9 0.2 collective-permute-start.11
  57.2 5.7 %collective-permute-done.12.yout = f32[8,8,128]{2,1,0:T(8,128)S(1)} collective-permute-done((f32[8,8,128]{2,1,0:T(8,128)S(1)}, f32[8,8,128]{2,1,0:T(8,128)S(1)}, u32[]{:S(2)}, u32[]{:S(2)}) %collective-permute-start.12) | collective-permute-done | bytes 32800 | tf_op jit(solution)/shard_map/ppermute | solution.py:468
  62.9 0.0 collective-permute-done.11.yin
  62.9 1.1 shard_map.118
  63.9 2.8 %collective-permute-start.13 = (f32[8,8,128]{2,1,0:T(8,128)S(1)}, f32[8,8,128]{2,1,0:T(8,128)S(1)}, u32[]{:S(2)}, u32[]{:S(2)}) collective-permute-start(f32[8,8,128]{2,1,0:T(8,128)S(1)} %get-tuple-element.54), channel_id=1, source_target_pairs={{0,32},{32,0},{1,33},{33,1},{2,34},{34,2},{3,35},{35,3},{4,36},{36... | collective-permute-start | bytes 98312 | tf_op jit(solution)/shard_map/ppermute | solution.py:463
  66.7 6.2 %all-to-all-start.1 = ((f32[128,4,128]{2,1,0:T(4,128)}), f32[128,4,128]{2,1,0:T(4,128)S(1)}, u32[]{:S(2)}, u32[]{:S(2)}) async-start(f32[128,4,128]{2,1,0:T(4,128)} %bitcast.20), calls=%async_computation.1 | async-start | bytes 524288 | tf_op jit(solution)/shard_map/all_to_all | solution.py:474
  72.9 0.9 collective-permute-start.14
  73.9 0.0 collective-permute-done.13.xin
  73.9 3.0 %collective-permute-done.14.xout = f32[8,8,128]{2,1,0:T(8,128)S(1)} collective-permute-done((f32[8,8,128]{2,1,0:T(8,128)S(1)}, f32[8,8,128]{2,1,0:T(8,128)S(1)}, u32[]{:S(2)}, u32[]{:S(2)}) %collective-permute-start.14) | collective-permute-done | bytes 32800 | tf_op jit(solution)/shard_map/ppermute | solution.py:462
  76.8 0.1 select_add_fusion.2
  76.9 4.1 %collective-permute-start.16 = (f32[8,8,128]{2,1,0:T(8,128)S(1)}, f32[8,8,128]{2,1,0:T(8,128)S(1)}, u32[]{:S(2)}, u32[]{:S(2)}) collective-permute-start(f32[8,8,128]{2,1,0:T(8,128)S(1)} %get-tuple-element.98), channel_id=1, source_target_pairs={{1,2},{2,1},{3,4},{4,3},{5,6},{6,5},{7,8},{8,7},{9,10},{10,9},{11,... | collective-permute-start | bytes 98312 | tf_op jit(solution)/shard_map/ppermute | solution.py:468
  81.0 6.4 %all-to-all-done.1 = f32[128,4,128]{2,1,0:T(4,128)S(1)} async-done(((f32[128,4,128]{2,1,0:T(4,128)}), f32[128,4,128]{2,1,0:T(4,128)S(1)}, u32[]{:S(2)}, u32[]{:S(2)}) %all-to-all-start.1) | async-done | bytes 262176 | tf_op jit(solution)/shard_map/all_to_all | solution.py:474
  87.4 1.0 shard_map.119.mine
  88.4 1.5 %collective-permute-start.17 = (f32[8,128]{1,0:T(8,128)S(1)}, f32[8,128]{1,0:T(8,128)S(1)}, u32[]{:S(2)}, u32[]{:S(2)}) collective-permute-start(f32[8,128]{1,0:T(8,128)S(1)} %shard_map.119.mine), channel_id=1, source_target_pairs={{0,32},{32,0},{1,33},{33,1},{2,34},{34,2},{3,35},{35,3},{4,36},{36... | collective-permute-start | bytes 12296 | tf_op jit(solution)/shard_map/ppermute | solution.py:505
  90.0 0.0 collective-permute-done.16.yout
  90.0 0.0 collective-permute-done.15.yin
  90.0 0.8 collective-permute-done.17.theirs
  90.8 2.5 %shard_map.120 = (f32[8,8,8,128]{3,2,1,0:T(8,128)S(1)}, f32[8,8,8,128]{3,2,1,0:T(8,128)S(1)}, f32[256,128]{1,0:T(8,128)}, f32[8,128]{1,0:T(8,128)S(1)}, f32[8,8,...) custom-call(s32[4]{0:T(128)S(1)} %compare_select_fusion.1.place, ...), custom_call_target="tpu_custom_call" | custom-call | tf_op jit(solution)/shard_map/pallas_call | solution.py:165
  93.3 0.3 collective-permute-start.18
  93.7 5.2 %all-to-all-start.2 = ((f32[256,1,128]{2,1,0:T(1,128)}), f32[256,1,128]{2,1,0:T(1,128)S(1)}, u32[]{:S(2)}, u32[]{:S(2)}) async-start(f32[256,1,128]{2,1,0:T(1,128)} %bitcast.27), calls=%async_computation.2 | async-start | bytes 262144 | tf_op jit(solution)/shard_map/all_to_all | solution.py:530
  98.8 1.7 %collective-permute-start.19 = (f32[8,8,128]{2,1,0:T(8,128)S(1)}, f32[8,8,128]{2,1,0:T(8,128)S(1)}, u32[]{:S(2)}, u32[]{:S(2)}) collective-permute-start(f32[8,8,128]{2,1,0:T(8,128)S(1)} %get-tuple-element.62), channel_id=1, source_target_pairs={{32,64},{64,32},{96,128},{128,96},{160,192},{192,160},{224,0},{0,2... | collective-permute-start | bytes 98312 | tf_op jit(solution)/shard_map/ppermute | solution.py:462
  100.6 2.0 %collective-permute-done.19.xout = f32[8,8,128]{2,1,0:T(8,128)S(1)} collective-permute-done((f32[8,8,128]{2,1,0:T(8,128)S(1)}, f32[8,8,128]{2,1,0:T(8,128)S(1)}, u32[]{:S(2)}, u32[]{:S(2)}) %collective-permute-start.19) | collective-permute-done | bytes 32800 | tf_op jit(solution)/shard_map/ppermute | solution.py:462
  102.6 0.1 select_add_fusion
  102.7 6.9 %collective-permute-start.21 = (f32[8,8,128]{2,1,0:T(8,128)S(1)}, f32[8,8,128]{2,1,0:T(8,128)S(1)}, u32[]{:S(2)}, u32[]{:S(2)}) collective-permute-start(f32[8,8,128]{2,1,0:T(8,128)S(1)} %get-tuple-element.96), channel_id=1, source_target_pairs={{1,2},{2,1},{3,4},{4,3},{5,6},{6,5},{7,8},{8,7},{9,10},{10,9},{11,... | collective-permute-start | bytes 98312 | tf_op jit(solution)/shard_map/ppermute | solution.py:468
  109.7 0.0 collective-permute-start.20
  109.7 1.6 %collective-permute-done.21.yout = f32[8,8,128]{2,1,0:T(8,128)S(1)} collective-permute-done((f32[8,8,128]{2,1,0:T(8,128)S(1)}, f32[8,8,128]{2,1,0:T(8,128)S(1)}, u32[]{:S(2)}, u32[]{:S(2)}) %collective-permute-start.21) | collective-permute-done | bytes 32800 | tf_op jit(solution)/shard_map/ppermute | solution.py:468
  111.3 1.5 %collective-permute-done.20.yin = f32[8,8,128]{2,1,0:T(8,128)S(1)} collective-permute-done((f32[8,8,128]{2,1,0:T(8,128)S(1)}, f32[8,8,128]{2,1,0:T(8,128)S(1)}, u32[]{:S(2)}, u32[]{:S(2)}) %collective-permute-start.20) | collective-permute-done | bytes 32800 | tf_op jit(solution)/shard_map/ppermute | solution.py:469
  112.7 0.0 all-to-all-done.2
  112.7 1.8 %shard_map.121 = (f32[8,8,8,128]{3,2,1,0:T(8,128)}, f32[8,8,8,128]{3,2,1,0:T(8,128)}) custom-call(s32[4]{0:T(128)S(1)} %compare_select_fusion.1.place, f32[8,8,8,128]{3,2,1,0:T(8,128)S(1)} %get-tuple-element.60.h, f32[8,8,128]{2,1,0:T(8,128)S(1)} %collective-permute-done.18.xin, f32[8,8,128]{2,1,0:T(8,128)S(1)} %collective-permute-done.19.xout, ...), custom_call_target="tpu_custom_call" | custom-call | tf_op jit(solution)/shard_map/pallas_call | solution.py:165
  (36 shorter events, 0.1 us)
Async XLA Ops:
  0.7 1.0 copy-start
  1.6 16.9 %copy-start.1 = (f32[8,8,8,1,1,128]{5,4,3,2,1,0:T(1,128)S(1)}, f32[8,8,8,1,1,128]{5,4,3,2,1,0:T(1,128)}, u32[]{:S(2)}) copy-start(f32[8,8,8,1,1,128]{5,4,3,2,1,0:T(1,128)} %param.10) | copy-start | bytes 786436
  2.3 4.1 %collective-permute-start = (f32[8,8,128]{2,1,0:T(8,128)S(1)}, f32[8,8,128]{2,1,0:T(8,128)S(1)}, u32[]{:S(2)}, u32[]{:S(2)}) collective-permute-start(f32[8,8,128]{2,1,0:T(8,128)S(1)} %get-tuple-element.37), channel_id=1, source_target_pairs={{0,32},{32,0},{1,33},{33,1},{2,34},{34,2},{3,35},{35,3},{4,36},{36... | collective-permute-start | bytes 98312 | tf_op jit(solution)/shard_map/ppermute | solution.py:463
  5.6 3.3 %collective-permute-start.1 = (f32[8,8,128]{2,1,0:T(8,128)S(1)}, f32[8,8,128]{2,1,0:T(8,128)S(1)}, u32[]{:S(2)}, u32[]{:S(2)}) collective-permute-start(f32[8,8,128]{2,1,0:T(8,128)S(1)} %get-tuple-element.38), channel_id=1, source_target_pairs={{32,64},{64,32},{96,128},{128,96},{160,192},{192,160},{224,0},{0,2... | collective-permute-start | bytes 98312 | tf_op jit(solution)/shard_map/ppermute | solution.py:462
  9.0 7.7 %collective-permute-start.3 = (f32[8,8,128]{2,1,0:T(8,128)S(1)}, f32[8,8,128]{2,1,0:T(8,128)S(1)}, u32[]{:S(2)}, u32[]{:S(2)}) collective-permute-start(f32[8,8,128]{2,1,0:T(8,128)S(1)} %get-tuple-element.104), channel_id=1, source_target_pairs={{1,2},{2,1},{3,4},{4,3},{5,6},{6,5},{7,8},{8,7},{9,10},{10,9},{11,... | collective-permute-start | bytes 98312 | tf_op jit(solution)/shard_map/ppermute | solution.py:468
  15.4 3.1 %collective-permute-start.2 = (f32[8,8,128]{2,1,0:T(8,128)S(1)}, f32[8,8,128]{2,1,0:T(8,128)S(1)}, u32[]{:S(2)}, u32[]{:S(2)}) collective-permute-start(f32[8,8,128]{2,1,0:T(8,128)S(1)} %get-tuple-element.105), channel_id=1, source_target_pairs={{0,1},{1,0},{2,3},{3,2},{4,5},{5,4},{6,7},{7,6},{8,9},{9,8},{10,11... | collective-permute-start | bytes 98312 | tf_op jit(solution)/shard_map/ppermute | solution.py:469
  18.5 1.0 copy-start.3
  19.4 3.6 %copy-start.5 = (f32[19,8,128]{2,1,0:T(8,128)S(1)}, f32[19,8,128]{2,1,0:T(8,128)}, u32[]{:S(2)}) copy-start(f32[19,8,128]{2,1,0:T(8,128)} %constant.48.clone.rolls) | copy-start | bytes 233476
  19.5 3.6 %copy-start.7 = (bf16[2,128,256]{2,1,0:T(8,128)(2,1)S(1)}, bf16[2,128,256]{2,1,0:T(8,128)(2,1)}, u32[]{:S(2)}) copy-start(bf16[2,128,256]{2,1,0:T(8,128)(2,1)} %constant.49.clone.z_in) | copy-start | bytes 393220
  19.5 3.6 %copy-start.10 = (f32[8,8,8,1,1,128]{5,4,3,2,1,0:T(1,128)S(1)}, f32[8,8,8,1,1,128]{5,4,3,2,1,0:T(1,128)}, u32[]{:S(2)}) copy-start(f32[8,8,8,1,1,128]{5,4,3,2,1,0:T(1,128)} %param.11) | copy-start | bytes 786436
  20.5 13.4 %collective-permute-start.4 = (f32[8,8,128]{2,1,0:T(8,128)S(1)}, f32[8,8,128]{2,1,0:T(8,128)S(1)}, u32[]{:S(2)}, u32[]{:S(2)}) collective-permute-start(f32[8,8,128]{2,1,0:T(8,128)S(1)} %get-tuple-element.42), channel_id=1, source_target_pairs={{0,32},{32,0},{1,33},{33,1},{2,34},{34,2},{3,35},{35,3},{4,36},{36... | collective-permute-start | bytes 98312 | tf_op jit(solution)/shard_map/ppermute | solution.py:463
  24.5 22.3 %copy-start.2 = (bf16[2,224,512]{2,1,0:T(8,128)(2,1)S(1)}, bf16[2,224,512]{2,1,0:T(8,128)(2,1)}, u32[]{:S(2)}) copy-start(bf16[2,224,512]{2,1,0:T(8,128)(2,1)} %constant.50.clone.gather) | copy-start | bytes 1376260
  24.5 22.3 %copy-start.11 = (f32[40,224]{1,0:T(8,128)S(1)}, f32[40,224]{1,0:T(8,128)}, u32[]{:S(2)}) copy-start(f32[40,224]{1,0:T(8,128)} %constant.53.clone.own_y) | copy-start | bytes 107524
  24.5 22.3 %all-to-all-start = ((f32[128,4,128]{2,1,0:T(4,128)}), f32[128,4,128]{2,1,0:T(4,128)S(1)}, u32[]{:S(2)}, u32[]{:S(2)}) async-start(f32[128,4,128]{2,1,0:T(4,128)} %bitcast.10), calls=%async_computation | async-start | bytes 524288 | tf_op jit(solution)/shard_map/all_to_all | solution.py:474
  32.5 14.3 %copy-start.8 = (f32[224,128]{1,0:T(8,128)S(1)}, f32[224,128]{1,0:T(8,128)}, u32[]{:S(2)}) copy-start(f32[224,128]{1,0:T(8,128)} %constant.51.clone.inv_eig) | copy-start | bytes 344068
  32.5 3.9 %collective-permute-start.5 = (f32[8,8,128]{2,1,0:T(8,128)S(1)}, f32[8,8,128]{2,1,0:T(8,128)S(1)}, u32[]{:S(2)}, u32[]{:S(2)}) collective-permute-start(f32[8,8,128]{2,1,0:T(8,128)S(1)} %get-tuple-element.43), channel_id=1, source_target_pairs={{32,64},{64,32},{96,128},{128,96},{160,192},{192,160},{224,0},{0,2... | collective-permute-start | bytes 98312 | tf_op jit(solution)/shard_map/ppermute | solution.py:462
  36.4 10.4 %copy-start.9 = (f32[8,8,224]{2,1,0:T(8,128)S(1)}, f32[8,8,224]{2,1,0:T(8,128)}, u32[]{:S(2)}) copy-start(f32[8,8,224]{2,1,0:T(8,128)} %constant.52.clone.own_x) | copy-start | bytes 172036
  36.5 13.1 %collective-permute-start.7 = (f32[8,8,128]{2,1,0:T(8,128)S(1)}, f32[8,8,128]{2,1,0:T(8,128)S(1)}, u32[]{:S(2)}, u32[]{:S(2)}) collective-permute-start(f32[8,8,128]{2,1,0:T(8,128)S(1)} %get-tuple-element.102), channel_id=1, source_target_pairs={{1,2},{2,1},{3,4},{4,3},{5,6},{6,5},{7,8},{8,7},{9,10},{10,9},{11,... | collective-permute-start | bytes 98312 | tf_op jit(solution)/shard_map/ppermute | solution.py:468
  41.1 8.4 %collective-permute-start.6 = (f32[8,8,128]{2,1,0:T(8,128)S(1)}, f32[8,8,128]{2,1,0:T(8,128)S(1)}, u32[]{:S(2)}, u32[]{:S(2)}) collective-permute-start(f32[8,8,128]{2,1,0:T(8,128)S(1)} %get-tuple-element.103), channel_id=1, source_target_pairs={{0,1},{1,0},{2,3},{3,2},{4,5},{5,4},{6,7},{7,6},{8,9},{9,8},{10,11... | collective-permute-start | bytes 98312 | tf_op jit(solution)/shard_map/ppermute | solution.py:469
  46.8 3.6 %copy-start.6 = (bf16[2,128,256]{2,1,0:T(8,128)(2,1)S(1)}, bf16[2,128,256]{2,1,0:T(8,128)(2,1)}, u32[]{:S(2)}) copy-start(bf16[2,128,256]{2,1,0:T(8,128)(2,1)} %constant.55.clone.z_out) | copy-start | bytes 393220
  47.8 2.6 %collective-permute-start.8 = (f32[8,128]{1,0:T(8,128)S(1)}, f32[8,128]{1,0:T(8,128)S(1)}, u32[]{:S(2)}, u32[]{:S(2)}) collective-permute-start(f32[8,128]{1,0:T(8,128)S(1)} %shard_map.116.mine), channel_id=1, source_target_pairs={{0,32},{32,0},{1,33},{33,1},{2,34},{34,2},{3,35},{35,3},{4,36},{36... | collective-permute-start | bytes 12296 | tf_op jit(solution)/shard_map/ppermute | solution.py:505
  50.4 12.5 %copy-start.4 = (bf16[2,4,128,128]{3,2,1,0:T(8,128)(2,1)S(1)}, bf16[2,4,128,128]{3,2,1,0:T(8,128)(2,1)}, u32[]{:S(2)}) copy-start(bf16[2,4,128,128]{3,2,1,0:T(8,128)(2,1)} %constant.54.clone.solve) | copy-start | bytes 786436
  52.9 1.2 %collective-permute-start.9 = (f32[8,8,128]{2,1,0:T(8,128)S(1)}, f32[8,8,128]{2,1,0:T(8,128)S(1)}, u32[]{:S(2)}, u32[]{:S(2)}) collective-permute-start(f32[8,8,128]{2,1,0:T(8,128)S(1)} %get-tuple-element.49), channel_id=1, source_target_pairs={{0,32},{32,0},{1,33},{33,1},{2,34},{34,2},{3,35},{35,3},{4,36},{36... | collective-permute-start | bytes 98312 | tf_op jit(solution)/shard_map/ppermute | solution.py:463
  53.2 3.3 %collective-permute-start.10 = (f32[8,8,128]{2,1,0:T(8,128)S(1)}, f32[8,8,128]{2,1,0:T(8,128)S(1)}, u32[]{:S(2)}, u32[]{:S(2)}) collective-permute-start(f32[8,8,128]{2,1,0:T(8,128)S(1)} %get-tuple-element.50), channel_id=1, source_target_pairs={{32,64},{64,32},{96,128},{128,96},{160,192},{192,160},{224,0},{0,2... | collective-permute-start | bytes 98312 | tf_op jit(solution)/shard_map/ppermute | solution.py:462
  56.7 6.2 %collective-permute-start.12 = (f32[8,8,128]{2,1,0:T(8,128)S(1)}, f32[8,8,128]{2,1,0:T(8,128)S(1)}, u32[]{:S(2)}, u32[]{:S(2)}) collective-permute-start(f32[8,8,128]{2,1,0:T(8,128)S(1)} %get-tuple-element.100), channel_id=1, source_target_pairs={{1,2},{2,1},{3,4},{4,3},{5,6},{6,5},{7,8},{8,7},{9,10},{10,9},{11,... | collective-permute-start | bytes 98312 | tf_op jit(solution)/shard_map/ppermute | solution.py:468
  56.9 5.9 %collective-permute-start.11 = (f32[8,8,128]{2,1,0:T(8,128)S(1)}, f32[8,8,128]{2,1,0:T(8,128)S(1)}, u32[]{:S(2)}, u32[]{:S(2)}) collective-permute-start(f32[8,8,128]{2,1,0:T(8,128)S(1)} %get-tuple-element.101), channel_id=1, source_target_pairs={{0,1},{1,0},{2,3},{3,2},{4,5},{5,4},{6,7},{7,6},{8,9},{9,8},{10,11... | collective-permute-start | bytes 98312 | tf_op jit(solution)/shard_map/ppermute | solution.py:469
  63.9 9.9 %collective-permute-start.13 = (f32[8,8,128]{2,1,0:T(8,128)S(1)}, f32[8,8,128]{2,1,0:T(8,128)S(1)}, u32[]{:S(2)}, u32[]{:S(2)}) collective-permute-start(f32[8,8,128]{2,1,0:T(8,128)S(1)} %get-tuple-element.54), channel_id=1, source_target_pairs={{0,32},{32,0},{1,33},{33,1},{2,34},{34,2},{3,35},{35,3},{4,36},{36... | collective-permute-start | bytes 98312 | tf_op jit(solution)/shard_map/ppermute | solution.py:463
  66.7 20.7 %all-to-all-start.1 = ((f32[128,4,128]{2,1,0:T(4,128)}), f32[128,4,128]{2,1,0:T(4,128)S(1)}, u32[]{:S(2)}, u32[]{:S(2)}) async-start(f32[128,4,128]{2,1,0:T(4,128)} %bitcast.20), calls=%async_computation.1 | async-start | bytes 524288 | tf_op jit(solution)/shard_map/all_to_all | solution.py:474
  72.9 3.9 %collective-permute-start.14 = (f32[8,8,128]{2,1,0:T(8,128)S(1)}, f32[8,8,128]{2,1,0:T(8,128)S(1)}, u32[]{:S(2)}, u32[]{:S(2)}) collective-permute-start(f32[8,8,128]{2,1,0:T(8,128)S(1)} %get-tuple-element.55), channel_id=1, source_target_pairs={{32,64},{64,32},{96,128},{128,96},{160,192},{192,160},{224,0},{0,2... | collective-permute-start | bytes 98312 | tf_op jit(solution)/shard_map/ppermute | solution.py:462
  76.9 13.0 %collective-permute-start.16 = (f32[8,8,128]{2,1,0:T(8,128)S(1)}, f32[8,8,128]{2,1,0:T(8,128)S(1)}, u32[]{:S(2)}, u32[]{:S(2)}) collective-permute-start(f32[8,8,128]{2,1,0:T(8,128)S(1)} %get-tuple-element.98), channel_id=1, source_target_pairs={{1,2},{2,1},{3,4},{4,3},{5,6},{6,5},{7,8},{8,7},{9,10},{10,9},{11,... | collective-permute-start | bytes 98312 | tf_op jit(solution)/shard_map/ppermute | solution.py:468
  81.0 9.0 %collective-permute-start.15 = (f32[8,8,128]{2,1,0:T(8,128)S(1)}, f32[8,8,128]{2,1,0:T(8,128)S(1)}, u32[]{:S(2)}, u32[]{:S(2)}) collective-permute-start(f32[8,8,128]{2,1,0:T(8,128)S(1)} %get-tuple-element.99), channel_id=1, source_target_pairs={{0,1},{1,0},{2,3},{3,2},{4,5},{5,4},{6,7},{7,6},{8,9},{9,8},{10,11... | collective-permute-start | bytes 98312 | tf_op jit(solution)/shard_map/ppermute | solution.py:469
  88.4 2.4 %collective-permute-start.17 = (f32[8,128]{1,0:T(8,128)S(1)}, f32[8,128]{1,0:T(8,128)S(1)}, u32[]{:S(2)}, u32[]{:S(2)}) collective-permute-start(f32[8,128]{1,0:T(8,128)S(1)} %shard_map.119.mine), channel_id=1, source_target_pairs={{0,32},{32,0},{1,33},{33,1},{2,34},{34,2},{3,35},{35,3},{4,36},{36... | collective-permute-start | bytes 12296 | tf_op jit(solution)/shard_map/ppermute | solution.py:505
  93.3 7.3 %collective-permute-start.18 = (f32[8,8,128]{2,1,0:T(8,128)S(1)}, f32[8,8,128]{2,1,0:T(8,128)S(1)}, u32[]{:S(2)}, u32[]{:S(2)}) collective-permute-start(f32[8,8,128]{2,1,0:T(8,128)S(1)} %get-tuple-element.61), channel_id=1, source_target_pairs={{0,32},{32,0},{1,33},{33,1},{2,34},{34,2},{3,35},{35,3},{4,36},{36... | collective-permute-start | bytes 98312 | tf_op jit(solution)/shard_map/ppermute | solution.py:463
  93.7 19.1 %all-to-all-start.2 = ((f32[256,1,128]{2,1,0:T(1,128)}), f32[256,1,128]{2,1,0:T(1,128)S(1)}, u32[]{:S(2)}, u32[]{:S(2)}) async-start(f32[256,1,128]{2,1,0:T(1,128)} %bitcast.27), calls=%async_computation.2 | async-start | bytes 262144 | tf_op jit(solution)/shard_map/all_to_all | solution.py:530
  98.8 3.8 %collective-permute-start.19 = (f32[8,8,128]{2,1,0:T(8,128)S(1)}, f32[8,8,128]{2,1,0:T(8,128)S(1)}, u32[]{:S(2)}, u32[]{:S(2)}) collective-permute-start(f32[8,8,128]{2,1,0:T(8,128)S(1)} %get-tuple-element.62), channel_id=1, source_target_pairs={{32,64},{64,32},{96,128},{128,96},{160,192},{192,160},{224,0},{0,2... | collective-permute-start | bytes 98312 | tf_op jit(solution)/shard_map/ppermute | solution.py:462
  102.7 8.5 %collective-permute-start.21 = (f32[8,8,128]{2,1,0:T(8,128)S(1)}, f32[8,8,128]{2,1,0:T(8,128)S(1)}, u32[]{:S(2)}, u32[]{:S(2)}) collective-permute-start(f32[8,8,128]{2,1,0:T(8,128)S(1)} %get-tuple-element.96), channel_id=1, source_target_pairs={{1,2},{2,1},{3,4},{4,3},{5,6},{6,5},{7,8},{8,7},{9,10},{10,9},{11,... | collective-permute-start | bytes 98312 | tf_op jit(solution)/shard_map/ppermute | solution.py:468
  109.7 3.1 %collective-permute-start.20 = (f32[8,8,128]{2,1,0:T(8,128)S(1)}, f32[8,8,128]{2,1,0:T(8,128)S(1)}, u32[]{:S(2)}, u32[]{:S(2)}) collective-permute-start(f32[8,8,128]{2,1,0:T(8,128)S(1)} %get-tuple-element.97), channel_id=1, source_target_pairs={{0,1},{1,0},{2,3},{3,2},{4,5},{5,4},{6,7},{7,6},{8,9},{9,8},{10,11... | collective-permute-start | bytes 98312 | tf_op jit(solution)/shard_map/ppermute | solution.py:469

commit v3 on v2

--- a/solution.py
+++ b/solution.py
@@ -341,8 +341,11 @@
         copy.wait()
 
 
-def k_restrict(place, u, coefficient, rolls, z_in, rows, cw):
+def k_restrict(place, u, rolls, z_in, rows):
     send_rows(restrict_rows(place, u, rolls, z_in), rows)
+
+
+def k_weight(place, coefficient, rolls, cw):
     w = all_tables()["weight"]
     for i in range(8):
         for j in range(8):
@@ -451,22 +454,29 @@
 SWAP = [(0, 1), (1, 0)]
 
 
-def pairs(count, start):
+def swaps(along_x, start):
     out = []
-    for n in range(start, count, 2):
-        out += [(n, (n + 1) % count), ((n + 1) % count, n)]
+    for x in range(EX):
+        for y in range(EY):
+            n, count = (x, EX) if along_x else (y, EY)
+            other = (n - start ^ 1) + start
+            if 0 <= other < count:
+                to = (other, y) if along_x else (x, other)
+            else:
+                to = (x, y ^ 1) if along_x else (x ^ 1, y)
+            out.append((x * EY + y, to[0] * EY + to[1]))
     return out
 
 
 def swap_x(inner, outer):
-    far = lax.ppermute(outer, ("x", "c"), pairs(EX, 1))
+    far = lax.ppermute(outer, ALL_AXES, swaps(True, 1))
     near = lax.ppermute(inner, "c", SWAP)
     return near, far
 
 
 def swap_y(inner, outer):
-    far = lax.ppermute(outer, ("y", "z"), pairs(EY, 1))
-    near = lax.ppermute(inner, ("y", "z"), pairs(EY, 0))
+    far = lax.ppermute(outer, ALL_AXES, swaps(False, 1))
+    near = lax.ppermute(inner, ALL_AXES, swaps(False, 0))
     return near, far
 
 
@@ -510,9 +520,12 @@
 
     faces = call(
         k_faces, FACES, place, f,
-        specs=[pl.BlockSpec(memory_space=pl.ANY)], scratch=(pltpu.SemaphoreType.DMA((4,)),),
-    )
-    rows, cw = call(k_restrict, (ROWS, NODES), place, f, coef, *tab("rolls", "z_in"))
+        specs=[pl.BlockSpec(memory_space=pltpu.HBM)], scratch=(pltpu.SemaphoreType.DMA((4,)),),
+    )
+    f_later, xin = lax.optimization_barrier((f, faces[0]))
+    faces = (xin, *faces[1:])
+    rows = call(k_restrict, (ROWS,), place, f_later, *tab("rolls", "z_in"))[0]
+    cw = call(k_weight, (NODES,), place, coef, *tab("rolls"))[0]
     c0 = coarse(rows)
     b, h, faces = local(f, halo(*faces))
     s0, g0, rows, *faces1 = call(

time: 115 us -> 112 us (0.974)
  starting transfers between devices: 58.5 us -> 54.8 us
    ppermute x15, starting transfers between devices: 26.6 us -> 17 us  [the longest x5 11.1 us: swap_y(): far = lax.ppermute(outer, ALL_AXES, swaps(False, 1))]
    all_to_all x2, starting transfers between devices: 14.1 us -> 22 us  [share(): got = lax.all_to_all(rows.reshape(CHIPS, 4, 128), CHIP_AXES, 0, 0)]
    ppermute x15, waiting for transfers between devices: 24.3 us -> 19.8 us  [the longest x5 12.8 us: swap_x(): far = lax.ppermute(outer, ALL_AXES, swaps(True, 1))]
    all_to_all x1, waiting for transfers between devices: 0.01 us -> 3.58 us  [on_device(): lax.all_to_all(rows.reshape(2 * CHIPS, 1, 128), ALL_AXES, 0, 0)]
    ppermute x5, starting transfers between devices: 9.3 us -> 6.76 us  [swap_x(): near = lax.ppermute(inner, 'c', SWAP)]
    all_to_all x2, waiting for transfers between devices: 12.1 us -> 13.5 us  [share(): got = lax.all_to_all(rows.reshape(CHIPS, 4, 128), CHIP_AXES, 0, 0)]
    pallas_call x9 -> x10, Pallas kernels: 13.1 us -> 13.7 us  [call(): pl.pallas_call(body, out_shape=outs, in_specs=[SMEM] + (specs or [VMEM] *...]
  transfers between devices with their start and end apart: 25 -> 25, of which waited for: 16 -> 17; matrix products, arithmetic and copies ran while one was open for 0% -> 0% of each run, Pallas kernels for 3% -> 4%
where the time goes in v3:
time: 112 us; the launch traced here: 111 us
  starting transfers between devices  54.8 us (49%)
  waiting for transfers between devices  39.7 us (35%)
  Pallas kernels  13.7 us (12%)
  local copies, waits for them, and re-layouts  2.02 us (2%)
    all_to_all x2, starting transfers between devices, share(): got = lax.all_to_all(rows.reshape(CHIPS, 4, 128), CHIP_AXES, 0, 0)  22 us
    pallas_call x10, Pallas kernels, call(): pl.pallas_call(body, out_shape=outs, in_specs=[SMEM] + (specs or [VMEM] *...  13.7 us
    all_to_all x2, waiting for transfers between devices, share(): got = lax.all_to_all(rows.reshape(CHIPS, 4, 128), CHIP_AXES, 0, 0)  13.5 us
    ppermute x5, waiting for transfers between devices, swap_x(): far = lax.ppermute(outer, ALL_AXES, swaps(True, 1))  12.8 us
    ppermute x5, starting transfers between devices, swap_y(): far = lax.ppermute(outer, ALL_AXES, swaps(False, 1))  11.1 us
    ppermute x5, starting transfers between devices, swap_x(): near = lax.ppermute(inner, 'c', SWAP)  6.76 us
    ppermute x5, waiting for transfers between devices, swap_y(): near = lax.ppermute(inner, ALL_AXES, swaps(False, 0))  5.7 us
    all_to_all x1, starting transfers between devices, on_device(): lax.all_to_all(rows.reshape(2 * CHIPS, 1, 128), ALL_AXES, 0, 0)  5.17 us
  transfers between devices with their start and end apart: 25, of which 17 were waited for; matrix products, arithmetic and copies ran while one was open for 0% of the time, Pallas kernels for 4%

profile of v3, /device:TPU:1, one launch (start us, length us, event | category | flops | bytes accessed | tf_op | source)
XLA Modules:
  0.0 111.5 jit_solution(5354784641158709255)
XLA Ops:
  0.7 0.0 copy-start
  0.7 0.9 copy-done
  1.6 0.7 shard_map.113
  2.3 3.3 %collective-permute-start = (f32[8,8,128]{2,1,0:T(8,128)S(1)}, f32[8,8,128]{2,1,0:T(8,128)S(1)}, u32[]{:S(2)}, u32[]{:S(2)}) collective-permute-start(f32[8,8,128]{2,1,0:T(8,128)S(1)} %get-tuple-element.38), channel_id=1, source_target_pairs={{0,32},{32,0},{1,33},{33,1},{2,34},{34,2},{3,35},{35,3},{4,36},{36... | collective-permute-start | bytes 98312 | tf_op jit(solution)/shard_map/ppermute | solution.py:473
  5.6 0.8 collective-permute-done.xin
  6.5 2.8 %collective-permute-done.1.xout = f32[8,8,128]{2,1,0:T(8,128)S(1)} collective-permute-done((f32[8,8,128]{2,1,0:T(8,128)S(1)}, f32[8,8,128]{2,1,0:T(8,128)S(1)}, u32[]{:S(2)}, u32[]{:S(2)}) %collective-permute-start.1) | collective-permute-done | bytes 32800 | tf_op jit(solution)/shard_map/ppermute | solution.py:472
  9.2 0.1 select_add_fusion.8
  9.3 0.5 collective-permute-start.3
  9.8 1.2 %collective-permute-start.2 = (f32[8,8,128]{2,1,0:T(8,128)S(1)}, f32[8,8,128]{2,1,0:T(8,128)S(1)}, u32[]{:S(2)}, u32[]{:S(2)}) collective-permute-start(f32[8,8,128]{2,1,0:T(8,128)S(1)} %get-tuple-element.105), channel_id=1, source_target_pairs={{0,1},{1,0},{2,3},{3,2},{4,5},{5,4},{6,7},{7,6},{8,9},{9,8},{10,11... | collective-permute-start | bytes 98312 | tf_op jit(solution)/shard_map/ppermute | solution.py:479
  11.0 0.0 collective-permute-done.3.yout
  11.0 1.6 %collective-permute-done.2.yin = f32[8,8,128]{2,1,0:T(8,128)S(1)} collective-permute-done((f32[8,8,128]{2,1,0:T(8,128)S(1)}, f32[8,8,128]{2,1,0:T(8,128)S(1)}, u32[]{:S(2)}, u32[]{:S(2)}) %collective-permute-start.2) | collective-permute-done | bytes 32800 | tf_op jit(solution)/shard_map/ppermute | solution.py:479
  12.6 0.9 copy-done.4
  13.5 1.1 shard_map.114
  14.6 1.3 %collective-permute-start.4 = (f32[8,8,128]{2,1,0:T(8,128)S(1)}, f32[8,8,128]{2,1,0:T(8,128)S(1)}, u32[]{:S(2)}, u32[]{:S(2)}) collective-permute-start(f32[8,8,128]{2,1,0:T(8,128)S(1)} %get-tuple-element.43), channel_id=1, source_target_pairs={{0,32},{32,0},{1,33},{33,1},{2,34},{34,2},{3,35},{35,3},{4,36},{36... | collective-permute-start | bytes 98312 | tf_op jit(solution)/shard_map/ppermute | solution.py:473
  15.9 1.4 %shard_map.115 = f32[512,128]{1,0:T(8,128)} custom-call(s32[4]{0:T(128)S(1)} %compare_select_fusion.1.place, f32[8,8,8,128]{3,2,1,0:T(8,128)S(1)} %bitcast.58, f32[19,8,128]{2,1,0:T(8,128)S(1)} %copy-done.3, bf16[2,128,256]{2,1,0:T(8,128)(2,1)S(1)} %copy-done.7), custom_call_target="tpu_custom_call" | custom-call | tf_op jit(solution)/shard_map/pallas_call | solution.py:165
  17.4 14.5 %all-to-all-start = ((f32[128,4,128]{2,1,0:T(4,128)}), f32[128,4,128]{2,1,0:T(4,128)S(1)}, u32[]{:S(2)}, u32[]{:S(2)}) async-start(f32[128,4,128]{2,1,0:T(4,128)} %bitcast.9), calls=%async_computation | async-start | bytes 524288 | tf_op jit(solution)/shard_map/all_to_all | solution.py:484
  31.9 0.0 copy-start.8
  31.9 1.2 %collective-permute-start.5 = (f32[8,8,128]{2,1,0:T(8,128)S(1)}, f32[8,8,128]{2,1,0:T(8,128)S(1)}, u32[]{:S(2)}, u32[]{:S(2)}) collective-permute-start(f32[8,8,128]{2,1,0:T(8,128)S(1)} %get-tuple-element.44), channel_id=1, source_target_pairs={{0,1},{1,0},{2,3},{3,2},{4,5},{5,4},{6,7},{7,6},{8,9},{9,8},{10,11... | collective-permute-start | bytes 98312 | tf_op jit(solution)/shard_map/ppermute | solution.py:472
  33.1 0.0 collective-permute-done.4.xin
  33.1 2.7 %collective-permute-done.5.xout = f32[8,8,128]{2,1,0:T(8,128)S(1)} collective-permute-done((f32[8,8,128]{2,1,0:T(8,128)S(1)}, f32[8,8,128]{2,1,0:T(8,128)S(1)}, u32[]{:S(2)}, u32[]{:S(2)}) %collective-permute-start.5) | collective-permute-done | bytes 32800 | tf_op jit(solution)/shard_map/ppermute | solution.py:472
  35.8 0.1 select_add_fusion.6
  35.9 3.7 %collective-permute-start.7 = (f32[8,8,128]{2,1,0:T(8,128)S(1)}, f32[8,8,128]{2,1,0:T(8,128)S(1)}, u32[]{:S(2)}, u32[]{:S(2)}) collective-permute-start(f32[8,8,128]{2,1,0:T(8,128)S(1)} %get-tuple-element.102), channel_id=1, source_target_pairs={{0,32},{1,2},{2,1},{3,4},{4,3},{5,6},{6,5},{7,8},{8,7},{9,10},{10,... | collective-permute-start | bytes 98312 | tf_op jit(solution)/shard_map/ppermute | solution.py:478
  39.6 0.0 collective-permute-start.6
  39.6 6.7 %all-to-all-done = f32[128,4,128]{2,1,0:T(4,128)S(1)} async-done(((f32[128,4,128]{2,1,0:T(4,128)}), f32[128,4,128]{2,1,0:T(4,128)S(1)}, u32[]{:S(2)}, u32[]{:S(2)}) %all-to-all-start) | async-done | bytes 262176 | tf_op jit(solution)/shard_map/all_to_all | solution.py:484
  46.3 0.0 copy-start.10
  46.3 1.0 shard_map.116.mine
  47.3 2.0 %collective-permute-start.8 = (f32[8,128]{1,0:T(8,128)S(1)}, f32[8,128]{1,0:T(8,128)S(1)}, u32[]{:S(2)}, u32[]{:S(2)}) collective-permute-start(f32[8,128]{1,0:T(8,128)S(1)} %shard_map.116.mine), channel_id=1, source_target_pairs={{0,32},{32,0},{1,33},{33,1},{2,34},{34,2},{3,35},{35,3},{4,36},{36... | collective-permute-start | bytes 12296 | tf_op jit(solution)/shard_map/ppermute | solution.py:515
  49.3 0.6 shard_map.117.cw
  49.9 0.0 collective-permute-done.6.yin
  49.9 0.2 collective-permute-done.8.theirs
  50.1 0.1 copy-done.6
  50.2 2.5 %shard_map.118 = (f32[8,8,8,128]{3,2,1,0:T(8,128)S(1)}, f32[8,8,8,128]{3,2,1,0:T(8,128)S(1)}, f32[512,128]{1,0:T(8,128)}, f32[8,8,128]{2,1,0:T(8,128)S(1)}, f32[...) custom-call(s32[4]{0:T(128)S(1)} %compare_select_fusion.1.place, ...), custom_call_target="tpu_custom_call" | custom-call | tf_op jit(solution)/shard_map/pallas_call | solution.py:165
  52.7 0.3 collective-permute-start.9
  53.0 0.9 collective-permute-done.9.xin
  54.0 2.7 %collective-permute-done.10.xout = f32[8,8,128]{2,1,0:T(8,128)S(1)} collective-permute-done((f32[8,8,128]{2,1,0:T(8,128)S(1)}, f32[8,8,128]{2,1,0:T(8,128)S(1)}, u32[]{:S(2)}, u32[]{:S(2)}) %collective-permute-start.10) | collective-permute-done | bytes 32800 | tf_op jit(solution)/shard_map/ppermute | solution.py:472
  56.7 0.1 select_add_fusion.4
  56.7 0.6 collective-permute-start.12
  57.4 0.0 collective-permute-start.11
  57.4 0.9 collective-permute-done.12.yout
  58.2 1.9 %collective-permute-done.11.yin = f32[8,8,128]{2,1,0:T(8,128)S(1)} collective-permute-done((f32[8,8,128]{2,1,0:T(8,128)S(1)}, f32[8,8,128]{2,1,0:T(8,128)S(1)}, u32[]{:S(2)}, u32[]{:S(2)}) %collective-permute-start.11) | collective-permute-done | bytes 32800 | tf_op jit(solution)/shard_map/ppermute | solution.py:479
  60.1 1.1 shard_map.119
  61.2 1.5 %collective-permute-start.13 = (f32[8,8,128]{2,1,0:T(8,128)S(1)}, f32[8,8,128]{2,1,0:T(8,128)S(1)}, u32[]{:S(2)}, u32[]{:S(2)}) collective-permute-start(f32[8,8,128]{2,1,0:T(8,128)S(1)} %get-tuple-element.54), channel_id=1, source_target_pairs={{0,32},{32,0},{1,33},{33,1},{2,34},{34,2},{3,35},{35,3},{4,36},{36... | collective-permute-start | bytes 98312 | tf_op jit(solution)/shard_map/ppermute | solution.py:473
  62.7 7.5 %all-to-all-start.1 = ((f32[128,4,128]{2,1,0:T(4,128)}), f32[128,4,128]{2,1,0:T(4,128)S(1)}, u32[]{:S(2)}, u32[]{:S(2)}) async-start(f32[128,4,128]{2,1,0:T(4,128)} %bitcast.20), calls=%async_computation.1 | async-start | bytes 524288 | tf_op jit(solution)/shard_map/all_to_all | solution.py:484
  70.2 1.2 %collective-permute-start.14 = (f32[8,8,128]{2,1,0:T(8,128)S(1)}, f32[8,8,128]{2,1,0:T(8,128)S(1)}, u32[]{:S(2)}, u32[]{:S(2)}) collective-permute-start(f32[8,8,128]{2,1,0:T(8,128)S(1)} %get-tuple-element.55), channel_id=1, source_target_pairs={{0,1},{1,0},{2,3},{3,2},{4,5},{5,4},{6,7},{7,6},{8,9},{9,8},{10,11... | collective-permute-start | bytes 98312 | tf_op jit(solution)/shard_map/ppermute | solution.py:472
  71.5 2.7 %collective-permute-done.14.xout = f32[8,8,128]{2,1,0:T(8,128)S(1)} collective-permute-done((f32[8,8,128]{2,1,0:T(8,128)S(1)}, f32[8,8,128]{2,1,0:T(8,128)S(1)}, u32[]{:S(2)}, u32[]{:S(2)}) %collective-permute-start.14) | collective-permute-done | bytes 32800 | tf_op jit(solution)/shard_map/ppermute | solution.py:472
  74.1 0.1 select_add_fusion.2
  74.2 3.7 %collective-permute-start.16 = (f32[8,8,128]{2,1,0:T(8,128)S(1)}, f32[8,8,128]{2,1,0:T(8,128)S(1)}, u32[]{:S(2)}, u32[]{:S(2)}) collective-permute-start(f32[8,8,128]{2,1,0:T(8,128)S(1)} %get-tuple-element.98), channel_id=1, source_target_pairs={{0,32},{1,2},{2,1},{3,4},{4,3},{5,6},{6,5},{7,8},{8,7},{9,10},{10,... | collective-permute-start | bytes 98312 | tf_op jit(solution)/shard_map/ppermute | solution.py:478
  77.9 0.0 collective-permute-start.15
  77.9 6.7 %all-to-all-done.1 = f32[128,4,128]{2,1,0:T(4,128)S(1)} async-done(((f32[128,4,128]{2,1,0:T(4,128)}), f32[128,4,128]{2,1,0:T(4,128)S(1)}, u32[]{:S(2)}, u32[]{:S(2)}) %all-to-all-start.1) | async-done | bytes 262176 | tf_op jit(solution)/shard_map/all_to_all | solution.py:484
  84.7 1.0 shard_map.120.mine
  85.7 2.0 %collective-permute-start.17 = (f32[8,128]{1,0:T(8,128)S(1)}, f32[8,128]{1,0:T(8,128)S(1)}, u32[]{:S(2)}, u32[]{:S(2)}) collective-permute-start(f32[8,128]{1,0:T(8,128)S(1)} %shard_map.120.mine), channel_id=1, source_target_pairs={{0,32},{32,0},{1,33},{33,1},{2,34},{34,2},{3,35},{35,3},{4,36},{36... | collective-permute-start | bytes 12296 | tf_op jit(solution)/shard_map/ppermute | solution.py:515
  87.6 0.8 collective-permute-done.17.theirs
  88.5 2.5 %shard_map.121 = (f32[8,8,8,128]{3,2,1,0:T(8,128)S(1)}, f32[8,8,8,128]{3,2,1,0:T(8,128)S(1)}, f32[256,128]{1,0:T(8,128)}, f32[8,128]{1,0:T(8,128)S(1)}, f32[8,8,...) custom-call(s32[4]{0:T(128)S(1)} %compare_select_fusion.1.place, ...), custom_call_target="tpu_custom_call" | custom-call | tf_op jit(solution)/shard_map/pallas_call | solution.py:165
  91.0 0.3 collective-permute-start.18
  91.3 5.2 %all-to-all-start.2 = ((f32[256,1,128]{2,1,0:T(1,128)}), f32[256,1,128]{2,1,0:T(1,128)S(1)}, u32[]{:S(2)}, u32[]{:S(2)}) async-start(f32[256,1,128]{2,1,0:T(1,128)} %bitcast.27), calls=%async_computation.2 | async-start | bytes 262144 | tf_op jit(solution)/shard_map/all_to_all | solution.py:543
  96.5 1.7 %collective-permute-start.19 = (f32[8,8,128]{2,1,0:T(8,128)S(1)}, f32[8,8,128]{2,1,0:T(8,128)S(1)}, u32[]{:S(2)}, u32[]{:S(2)}) collective-permute-start(f32[8,8,128]{2,1,0:T(8,128)S(1)} %get-tuple-element.62), channel_id=1, source_target_pairs={{0,1},{1,0},{2,3},{3,2},{4,5},{5,4},{6,7},{7,6},{8,9},{9,8},{10,11... | collective-permute-start | bytes 98312 | tf_op jit(solution)/shard_map/ppermute | solution.py:472
  98.2 2.0 %collective-permute-done.19.xout = f32[8,8,128]{2,1,0:T(8,128)S(1)} collective-permute-done((f32[8,8,128]{2,1,0:T(8,128)S(1)}, f32[8,8,128]{2,1,0:T(8,128)S(1)}, u32[]{:S(2)}, u32[]{:S(2)}) %collective-permute-start.19) | collective-permute-done | bytes 32800 | tf_op jit(solution)/shard_map/ppermute | solution.py:472
  100.3 0.1 select_add_fusion
  100.4 2.7 %collective-permute-start.21 = (f32[8,8,128]{2,1,0:T(8,128)S(1)}, f32[8,8,128]{2,1,0:T(8,128)S(1)}, u32[]{:S(2)}, u32[]{:S(2)}) collective-permute-start(f32[8,8,128]{2,1,0:T(8,128)S(1)} %get-tuple-element.96), channel_id=1, source_target_pairs={{0,32},{1,2},{2,1},{3,4},{4,3},{5,6},{6,5},{7,8},{8,7},{9,10},{10,... | collective-permute-start | bytes 98312 | tf_op jit(solution)/shard_map/ppermute | solution.py:478
  103.0 0.5 collective-permute-start.20
  103.5 0.4 collective-permute-done.21.yout
  103.9 2.2 %collective-permute-done.20.yin = f32[8,8,128]{2,1,0:T(8,128)S(1)} collective-permute-done((f32[8,8,128]{2,1,0:T(8,128)S(1)}, f32[8,8,128]{2,1,0:T(8,128)S(1)}, u32[]{:S(2)}, u32[]{:S(2)}) %collective-permute-start.20) | collective-permute-done | bytes 32800 | tf_op jit(solution)/shard_map/ppermute | solution.py:479
  106.1 3.6 %all-to-all-done.2 = f32[256,1,128]{2,1,0:T(1,128)S(1)} async-done(((f32[256,1,128]{2,1,0:T(1,128)}), f32[256,1,128]{2,1,0:T(1,128)S(1)}, u32[]{:S(2)}, u32[]{:S(2)}) %all-to-all-start.2) | async-done | bytes 131104 | tf_op jit(solution)/shard_map/all_to_all | solution.py:543
  109.7 1.8 %shard_map.122 = (f32[8,8,8,128]{3,2,1,0:T(8,128)}, f32[8,8,8,128]{3,2,1,0:T(8,128)}) custom-call(s32[4]{0:T(128)S(1)} %compare_select_fusion.1.place, f32[8,8,8,128]{3,2,1,0:T(8,128)S(1)} %get-tuple-element.60.h, f32[8,8,128]{2,1,0:T(8,128)S(1)} %collective-permute-done.18.xin, f32[8,8,128]{2,1,0:T(8,128)S(1)} %collective-permute-done.19.xout, ...), custom_call_target="tpu_custom_call" | custom-call | tf_op jit(solution)/shard_map/pallas_call | solution.py:165
  (38 shorter events, 0.1 us)
Async XLA Ops:
  0.7 1.0 copy-start
  1.6 11.0 %copy-start.1 = (f32[8,8,8,1,1,128]{5,4,3,2,1,0:T(1,128)S(1)}, f32[8,8,8,1,1,128]{5,4,3,2,1,0:T(1,128)}, u32[]{:S(2)}) copy-start(f32[8,8,8,1,1,128]{5,4,3,2,1,0:T(1,128)} %param.10) | copy-start | bytes 786436
  2.3 4.1 %collective-permute-start = (f32[8,8,128]{2,1,0:T(8,128)S(1)}, f32[8,8,128]{2,1,0:T(8,128)S(1)}, u32[]{:S(2)}, u32[]{:S(2)}) collective-permute-start(f32[8,8,128]{2,1,0:T(8,128)S(1)} %get-tuple-element.38), channel_id=1, source_target_pairs={{0,32},{32,0},{1,33},{33,1},{2,34},{34,2},{3,35},{35,3},{4,36},{36... | collective-permute-start | bytes 98312 | tf_op jit(solution)/shard_map/ppermute | solution.py:473
  5.6 3.6 %collective-permute-start.1 = (f32[8,8,128]{2,1,0:T(8,128)S(1)}, f32[8,8,128]{2,1,0:T(8,128)S(1)}, u32[]{:S(2)}, u32[]{:S(2)}) collective-permute-start(f32[8,8,128]{2,1,0:T(8,128)S(1)} %get-tuple-element.39), channel_id=1, source_target_pairs={{0,1},{1,0},{2,3},{3,2},{4,5},{5,4},{6,7},{7,6},{8,9},{9,8},{10,11... | collective-permute-start | bytes 98312 | tf_op jit(solution)/shard_map/ppermute | solution.py:472
  9.3 1.7 %collective-permute-start.3 = (f32[8,8,128]{2,1,0:T(8,128)S(1)}, f32[8,8,128]{2,1,0:T(8,128)S(1)}, u32[]{:S(2)}, u32[]{:S(2)}) collective-permute-start(f32[8,8,128]{2,1,0:T(8,128)S(1)} %get-tuple-element.104), channel_id=1, source_target_pairs={{0,32},{1,2},{2,1},{3,4},{4,3},{5,6},{6,5},{7,8},{8,7},{9,10},{10,... | collective-permute-start | bytes 98312 | tf_op jit(solution)/shard_map/ppermute | solution.py:478
  9.8 6.2 %copy-start.3 = (f32[19,8,128]{2,1,0:T(8,128)S(1)}, f32[19,8,128]{2,1,0:T(8,128)}, u32[]{:S(2)}) copy-start(f32[19,8,128]{2,1,0:T(8,128)} %constant.48.clone.rolls) | copy-start | bytes 233476
  9.8 2.8 %collective-permute-start.2 = (f32[8,8,128]{2,1,0:T(8,128)S(1)}, f32[8,8,128]{2,1,0:T(8,128)S(1)}, u32[]{:S(2)}, u32[]{:S(2)}) collective-permute-start(f32[8,8,128]{2,1,0:T(8,128)S(1)} %get-tuple-element.105), channel_id=1, source_target_pairs={{0,1},{1,0},{2,3},{3,2},{4,5},{5,4},{6,7},{7,6},{8,9},{9,8},{10,11... | collective-permute-start | bytes 98312 | tf_op jit(solution)/shard_map/ppermute | solution.py:479
  12.6 1.0 copy-start.4
  13.5 2.4 %copy-start.7 = (bf16[2,128,256]{2,1,0:T(8,128)(2,1)S(1)}, bf16[2,128,256]{2,1,0:T(8,128)(2,1)}, u32[]{:S(2)}) copy-start(bf16[2,128,256]{2,1,0:T(8,128)(2,1)} %constant.49.clone.z_in) | copy-start | bytes 393220
  14.6 18.5 %collective-permute-start.4 = (f32[8,8,128]{2,1,0:T(8,128)S(1)}, f32[8,8,128]{2,1,0:T(8,128)S(1)}, u32[]{:S(2)}, u32[]{:S(2)}) collective-permute-start(f32[8,8,128]{2,1,0:T(8,128)S(1)} %get-tuple-element.43), channel_id=1, source_target_pairs={{0,32},{32,0},{1,33},{33,1},{2,34},{34,2},{3,35},{35,3},{4,36},{36... | collective-permute-start | bytes 98312 | tf_op jit(solution)/shard_map/ppermute | solution.py:473
  17.4 28.9 %copy-start.2 = (bf16[2,224,512]{2,1,0:T(8,128)(2,1)S(1)}, bf16[2,224,512]{2,1,0:T(8,128)(2,1)}, u32[]{:S(2)}) copy-start(bf16[2,224,512]{2,1,0:T(8,128)(2,1)} %constant.50.clone.gather) | copy-start | bytes 1376260
  17.4 28.9 %copy-start.11 = (f32[40,224]{1,0:T(8,128)S(1)}, f32[40,224]{1,0:T(8,128)}, u32[]{:S(2)}) copy-start(f32[40,224]{1,0:T(8,128)} %constant.53.clone.own_y) | copy-start | bytes 107524
  17.4 28.9 %all-to-all-start = ((f32[128,4,128]{2,1,0:T(4,128)}), f32[128,4,128]{2,1,0:T(4,128)S(1)}, u32[]{:S(2)}, u32[]{:S(2)}) async-start(f32[128,4,128]{2,1,0:T(4,128)} %bitcast.9), calls=%async_computation | async-start | bytes 524288 | tf_op jit(solution)/shard_map/all_to_all | solution.py:484
  31.9 14.5 %copy-start.8 = (f32[224,128]{1,0:T(8,128)S(1)}, f32[224,128]{1,0:T(8,128)}, u32[]{:S(2)}) copy-start(f32[224,128]{1,0:T(8,128)} %constant.51.clone.inv_eig) | copy-start | bytes 344068
  31.9 3.9 %collective-permute-start.5 = (f32[8,8,128]{2,1,0:T(8,128)S(1)}, f32[8,8,128]{2,1,0:T(8,128)S(1)}, u32[]{:S(2)}, u32[]{:S(2)}) collective-permute-start(f32[8,8,128]{2,1,0:T(8,128)S(1)} %get-tuple-element.44), channel_id=1, source_target_pairs={{0,1},{1,0},{2,3},{3,2},{4,5},{5,4},{6,7},{7,6},{8,9},{9,8},{10,11... | collective-permute-start | bytes 98312 | tf_op jit(solution)/shard_map/ppermute | solution.py:472
  35.8 10.5 %copy-start.9 = (f32[8,8,224]{2,1,0:T(8,128)S(1)}, f32[8,8,224]{2,1,0:T(8,128)}, u32[]{:S(2)}) copy-start(f32[8,8,224]{2,1,0:T(8,128)} %constant.52.clone.own_x) | copy-start | bytes 172036
  35.9 14.0 %collective-permute-start.7 = (f32[8,8,128]{2,1,0:T(8,128)S(1)}, f32[8,8,128]{2,1,0:T(8,128)S(1)}, u32[]{:S(2)}, u32[]{:S(2)}) collective-permute-start(f32[8,8,128]{2,1,0:T(8,128)S(1)} %get-tuple-element.102), channel_id=1, source_target_pairs={{0,32},{1,2},{2,1},{3,4},{4,3},{5,6},{6,5},{7,8},{8,7},{9,10},{10,... | collective-permute-start | bytes 98312 | tf_op jit(solution)/shard_map/ppermute | solution.py:478
  39.6 10.3 %collective-permute-start.6 = (f32[8,8,128]{2,1,0:T(8,128)S(1)}, f32[8,8,128]{2,1,0:T(8,128)S(1)}, u32[]{:S(2)}, u32[]{:S(2)}) collective-permute-start(f32[8,8,128]{2,1,0:T(8,128)S(1)} %get-tuple-element.103), channel_id=1, source_target_pairs={{0,1},{1,0},{2,3},{3,2},{4,5},{5,4},{6,7},{7,6},{8,9},{9,8},{10,11... | collective-permute-start | bytes 98312 | tf_op jit(solution)/shard_map/ppermute | solution.py:479
  46.3 3.0 %copy-start.10 = (f32[8,8,8,1,1,128]{5,4,3,2,1,0:T(1,128)S(1)}, f32[8,8,8,1,1,128]{5,4,3,2,1,0:T(1,128)}, u32[]{:S(2)}) copy-start(f32[8,8,8,1,1,128]{5,4,3,2,1,0:T(1,128)} %param.11) | copy-start | bytes 786436
  47.3 2.8 %collective-permute-start.8 = (f32[8,128]{1,0:T(8,128)S(1)}, f32[8,128]{1,0:T(8,128)S(1)}, u32[]{:S(2)}, u32[]{:S(2)}) collective-permute-start(f32[8,128]{1,0:T(8,128)S(1)} %shard_map.116.mine), channel_id=1, source_target_pairs={{0,32},{32,0},{1,33},{33,1},{2,34},{34,2},{3,35},{35,3},{4,36},{36... | collective-permute-start | bytes 12296 | tf_op jit(solution)/shard_map/ppermute | solution.py:515
  49.3 0.9 copy-start.6
  50.2 9.9 %copy-start.5 = (bf16[2,4,128,128]{3,2,1,0:T(8,128)(2,1)S(1)}, bf16[2,4,128,128]{3,2,1,0:T(8,128)(2,1)}, u32[]{:S(2)}) copy-start(bf16[2,4,128,128]{3,2,1,0:T(8,128)(2,1)} %constant.54.clone.solve) | copy-start | bytes 786436
  52.7 1.2 %collective-permute-start.9 = (f32[8,8,128]{2,1,0:T(8,128)S(1)}, f32[8,8,128]{2,1,0:T(8,128)S(1)}, u32[]{:S(2)}, u32[]{:S(2)}) collective-permute-start(f32[8,8,128]{2,1,0:T(8,128)S(1)} %get-tuple-element.49), channel_id=1, source_target_pairs={{0,32},{32,0},{1,33},{33,1},{2,34},{34,2},{3,35},{35,3},{4,36},{36... | collective-permute-start | bytes 98312 | tf_op jit(solution)/shard_map/ppermute | solution.py:473
  53.0 3.6 %collective-permute-start.10 = (f32[8,8,128]{2,1,0:T(8,128)S(1)}, f32[8,8,128]{2,1,0:T(8,128)S(1)}, u32[]{:S(2)}, u32[]{:S(2)}) collective-permute-start(f32[8,8,128]{2,1,0:T(8,128)S(1)} %get-tuple-element.50), channel_id=1, source_target_pairs={{0,1},{1,0},{2,3},{3,2},{4,5},{5,4},{6,7},{7,6},{8,9},{9,8},{10,11... | collective-permute-start | bytes 98312 | tf_op jit(solution)/shard_map/ppermute | solution.py:472
  56.7 1.5 %collective-permute-start.12 = (f32[8,8,128]{2,1,0:T(8,128)S(1)}, f32[8,8,128]{2,1,0:T(8,128)S(1)}, u32[]{:S(2)}, u32[]{:S(2)}) collective-permute-start(f32[8,8,128]{2,1,0:T(8,128)S(1)} %get-tuple-element.100), channel_id=1, source_target_pairs={{0,32},{1,2},{2,1},{3,4},{4,3},{5,6},{6,5},{7,8},{8,7},{9,10},{10,... | collective-permute-start | bytes 98312 | tf_op jit(solution)/shard_map/ppermute | solution.py:478
  57.4 2.8 %collective-permute-start.11 = (f32[8,8,128]{2,1,0:T(8,128)S(1)}, f32[8,8,128]{2,1,0:T(8,128)S(1)}, u32[]{:S(2)}, u32[]{:S(2)}) collective-permute-start(f32[8,8,128]{2,1,0:T(8,128)S(1)} %get-tuple-element.101), channel_id=1, source_target_pairs={{0,1},{1,0},{2,3},{3,2},{4,5},{5,4},{6,7},{7,6},{8,9},{9,8},{10,11... | collective-permute-start | bytes 98312 | tf_op jit(solution)/shard_map/ppermute | solution.py:479
  61.2 10.3 %collective-permute-start.13 = (f32[8,8,128]{2,1,0:T(8,128)S(1)}, f32[8,8,128]{2,1,0:T(8,128)S(1)}, u32[]{:S(2)}, u32[]{:S(2)}) collective-permute-start(f32[8,8,128]{2,1,0:T(8,128)S(1)} %get-tuple-element.54), channel_id=1, source_target_pairs={{0,32},{32,0},{1,33},{33,1},{2,34},{34,2},{3,35},{35,3},{4,36},{36... | collective-permute-start | bytes 98312 | tf_op jit(solution)/shard_map/ppermute | solution.py:473
  62.7 21.9 %all-to-all-start.1 = ((f32[128,4,128]{2,1,0:T(4,128)}), f32[128,4,128]{2,1,0:T(4,128)S(1)}, u32[]{:S(2)}, u32[]{:S(2)}) async-start(f32[128,4,128]{2,1,0:T(4,128)} %bitcast.20), calls=%async_computation.1 | async-start | bytes 524288 | tf_op jit(solution)/shard_map/all_to_all | solution.py:484
  70.2 3.9 %collective-permute-start.14 = (f32[8,8,128]{2,1,0:T(8,128)S(1)}, f32[8,8,128]{2,1,0:T(8,128)S(1)}, u32[]{:S(2)}, u32[]{:S(2)}) collective-permute-start(f32[8,8,128]{2,1,0:T(8,128)S(1)} %get-tuple-element.55), channel_id=1, source_target_pairs={{0,1},{1,0},{2,3},{3,2},{4,5},{5,4},{6,7},{7,6},{8,9},{9,8},{10,11... | collective-permute-start | bytes 98312 | tf_op jit(solution)/shard_map/ppermute | solution.py:472
  74.2 13.4 %collective-permute-start.16 = (f32[8,8,128]{2,1,0:T(8,128)S(1)}, f32[8,8,128]{2,1,0:T(8,128)S(1)}, u32[]{:S(2)}, u32[]{:S(2)}) collective-permute-start(f32[8,8,128]{2,1,0:T(8,128)S(1)} %get-tuple-element.98), channel_id=1, source_target_pairs={{0,32},{1,2},{2,1},{3,4},{4,3},{5,6},{6,5},{7,8},{8,7},{9,10},{10,... | collective-permute-start | bytes 98312 | tf_op jit(solution)/shard_map/ppermute | solution.py:478
  77.9 9.7 %collective-permute-start.15 = (f32[8,8,128]{2,1,0:T(8,128)S(1)}, f32[8,8,128]{2,1,0:T(8,128)S(1)}, u32[]{:S(2)}, u32[]{:S(2)}) collective-permute-start(f32[8,8,128]{2,1,0:T(8,128)S(1)} %get-tuple-element.99), channel_id=1, source_target_pairs={{0,1},{1,0},{2,3},{3,2},{4,5},{5,4},{6,7},{7,6},{8,9},{9,8},{10,11... | collective-permute-start | bytes 98312 | tf_op jit(solution)/shard_map/ppermute | solution.py:479
  85.7 2.8 %collective-permute-start.17 = (f32[8,128]{1,0:T(8,128)S(1)}, f32[8,128]{1,0:T(8,128)S(1)}, u32[]{:S(2)}, u32[]{:S(2)}) collective-permute-start(f32[8,128]{1,0:T(8,128)S(1)} %shard_map.120.mine), channel_id=1, source_target_pairs={{0,32},{32,0},{1,33},{33,1},{2,34},{34,2},{3,35},{35,3},{4,36},{36... | collective-permute-start | bytes 12296 | tf_op jit(solution)/shard_map/ppermute | solution.py:515
  91.0 7.3 %collective-permute-start.18 = (f32[8,8,128]{2,1,0:T(8,128)S(1)}, f32[8,8,128]{2,1,0:T(8,128)S(1)}, u32[]{:S(2)}, u32[]{:S(2)}) collective-permute-start(f32[8,8,128]{2,1,0:T(8,128)S(1)} %get-tuple-element.61), channel_id=1, source_target_pairs={{0,32},{32,0},{1,33},{33,1},{2,34},{34,2},{3,35},{35,3},{4,36},{36... | collective-permute-start | bytes 98312 | tf_op jit(solution)/shard_map/ppermute | solution.py:473
  91.3 18.4 %all-to-all-start.2 = ((f32[256,1,128]{2,1,0:T(1,128)}), f32[256,1,128]{2,1,0:T(1,128)S(1)}, u32[]{:S(2)}, u32[]{:S(2)}) async-start(f32[256,1,128]{2,1,0:T(1,128)} %bitcast.27), calls=%async_computation.2 | async-start | bytes 262144 | tf_op jit(solution)/shard_map/all_to_all | solution.py:543
  96.5 3.8 %collective-permute-start.19 = (f32[8,8,128]{2,1,0:T(8,128)S(1)}, f32[8,8,128]{2,1,0:T(8,128)S(1)}, u32[]{:S(2)}, u32[]{:S(2)}) collective-permute-start(f32[8,8,128]{2,1,0:T(8,128)S(1)} %get-tuple-element.62), channel_id=1, source_target_pairs={{0,1},{1,0},{2,3},{3,2},{4,5},{5,4},{6,7},{7,6},{8,9},{9,8},{10,11... | collective-permute-start | bytes 98312 | tf_op jit(solution)/shard_map/ppermute | solution.py:472
  100.4 3.5 %collective-permute-start.21 = (f32[8,8,128]{2,1,0:T(8,128)S(1)}, f32[8,8,128]{2,1,0:T(8,128)S(1)}, u32[]{:S(2)}, u32[]{:S(2)}) collective-permute-start(f32[8,8,128]{2,1,0:T(8,128)S(1)} %get-tuple-element.96), channel_id=1, source_target_pairs={{0,32},{1,2},{2,1},{3,4},{4,3},{5,6},{6,5},{7,8},{8,7},{9,10},{10,... | collective-permute-start | bytes 98312 | tf_op jit(solution)/shard_map/ppermute | solution.py:478
  103.0 3.1 %collective-permute-start.20 = (f32[8,8,128]{2,1,0:T(8,128)S(1)}, f32[8,8,128]{2,1,0:T(8,128)S(1)}, u32[]{:S(2)}, u32[]{:S(2)}) collective-permute-start(f32[8,8,128]{2,1,0:T(8,128)S(1)} %get-tuple-element.97), channel_id=1, source_target_pairs={{0,1},{1,0},{2,3},{3,2},{4,5},{5,4},{6,7},{7,6},{8,9},{9,8},{10,11... | collective-permute-start | bytes 98312 | tf_op jit(solution)/shard_map/ppermute | solution.py:479

commit v4 on v3

--- a/solution.py
+++ b/solution.py
@@ -158,18 +158,26 @@
 ROWS = jax.ShapeDtypeStruct((4 * CHIPS, 128), F32)
 SMALL = jax.ShapeDtypeStruct((8, 128), F32)
 VMEM = pl.BlockSpec(memory_space=pltpu.VMEM)
-SMEM = pl.BlockSpec(memory_space=pltpu.SMEM)
-
-
-def call(body, outs, place, *args, scratch=(), specs=None):
+
+
+def where_am_i():
+    x = lax.axis_index("x") * 2 + lax.axis_index("c")
+    y = lax.axis_index("y") * 8 + lax.axis_index("z")
+    return x.astype(jnp.int32), y.astype(jnp.int32), (x & 1).astype(jnp.int32)
+
+
+def call(body, outs, *args, scratch=(), specs=None):
+    def placed(*refs):
+        body(where_am_i(), *refs)
+
     return pl.pallas_call(
-        body,
+        placed,
         out_shape=outs,
-        in_specs=[SMEM] + (specs or [VMEM] * len(args)),
+        in_specs=specs or [VMEM] * len(args),
         out_specs=[VMEM] * len(outs),
         scratch_shapes=list(scratch),
         compiler_params=pltpu.CompilerParams(vmem_limit_bytes=12 << 20),
-    )(place, *args)
+    )(*args)
 
 
 def parts(x):
@@ -490,11 +498,7 @@
     tab = lambda *names: [jnp.asarray(tables[n]) for n in names]
     f = forcing.reshape(8, 8, 8, 128)
     coef = coefficient.reshape(8, 8, 8, 128)
-    px = lax.axis_index(("x", "c")).astype(jnp.int32)
-    py = lax.axis_index(("y", "z")).astype(jnp.int32)
-    n = jnp.arange(4, dtype=jnp.int32)
-    place = jnp.where(n == 0, px, jnp.where(n == 1, py, px & 1))
-
+    px, py, _ = where_am_i()
     inside = jnp.arange(8, dtype=jnp.int32)[:, None, None] == 7 * (1 - (px & 1))
     outside = jnp.arange(8, dtype=jnp.int32)[:, None, None] == 7 * (px & 1)
     even = (py & 1) == 0
@@ -511,25 +515,25 @@
 
     def coarse(rows):
         got = share(rows)
-        mine = call(k_coarse, (SMALL,), place, got, *tab("gather", "inv_eig", "own_x", "own_y"))[0]
+        mine = call(k_coarse, (SMALL,), got, *tab("gather", "inv_eig", "own_x", "own_y"))[0]
         return mine, lax.ppermute(mine, "c", SWAP)
 
     def local(u, sides):
-        out = call(k_local_solve, (NODES, NODES) + FACES, place, u, *sides, *tab("local_solve"))
+        out = call(k_local_solve, (NODES, NODES) + FACES, u, *sides, *tab("local_solve"))
         return out[0], out[1], out[2:]
 
     faces = call(
-        k_faces, FACES, place, f,
+        k_faces, FACES, f,
         specs=[pl.BlockSpec(memory_space=pltpu.HBM)], scratch=(pltpu.SemaphoreType.DMA((4,)),),
     )
     f_later, xin = lax.optimization_barrier((f, faces[0]))
     faces = (xin, *faces[1:])
-    rows = call(k_restrict, (ROWS,), place, f_later, *tab("rolls", "z_in"))[0]
-    cw = call(k_weight, (NODES,), place, coef, *tab("rolls"))[0]
+    rows = call(k_restrict, (ROWS,), f_later, *tab("rolls", "z_in"))[0]
+    cw = call(k_weight, (NODES,), coef, *tab("rolls"))[0]
     c0 = coarse(rows)
     b, h, faces = local(f, halo(*faces))
     s0, g0, rows, *faces1 = call(
-        k_first, (NODES, NODES, ROWS) + FACES, place, h, *halo(*faces), *c0, f, cw,
+        k_first, (NODES, NODES, ROWS) + FACES, h, *halo(*faces), *c0, f, cw,
         *tab("rolls", "z_out", "z_in"),
     )
     c1 = coarse(rows)
@@ -537,12 +541,12 @@
     s1, h1, rows, scalars, *faces1 = call(
         k_second,
         (NODES, NODES, jax.ShapeDtypeStruct((2 * CHIPS, 128), F32), SMALL) + FACES,
-        place, h, *halo(*faces), *c1, f, s0, g0, cw, *tab("rolls", "z_out"),
+        h, *halo(*faces), *c1, f, s0, g0, cw, *tab("rolls", "z_out"),
         scratch=(pltpu.VMEM((8, 8, 8, 128), F32),),
     )
     got = lax.all_to_all(rows.reshape(2 * CHIPS, 1, 128), ALL_AXES, 0, 0).reshape(2 * CHIPS, 128)
     sides = halo(*faces1)
-    p, r = call(k_last, (NODES, NODES), place, h1, *sides, got, scalars, s0, s1, b, w)
+    p, r = call(k_last, (NODES, NODES), h1, *sides, got, scalars, s0, s1, b, w)
     return p.reshape(forcing.shape), r.reshape(forcing.shape)
 
 

time: 112 us -> 107 us (0.955)
  Pallas kernels: 13.7 us -> 8.2 us
    pallas_call x10, Pallas kernels: 13.7 us -> 8.2 us  [call(): pl.pallas_call(placed, out_shape=outs, in_specs=specs or [VMEM] * len(arg...]
  transfers between devices with their start and end apart: 25 -> 25, of which waited for: 17 -> 17; matrix products, arithmetic and copies ran while one was open for 0% -> 0% of each run, Pallas kernels for 4% -> 2%
where the time goes in v4:
time: 107 us; the launch traced here: 106 us
  starting transfers between devices  55.2 us (52%)
  waiting for transfers between devices  39.8 us (37%)
  Pallas kernels  8.2 us (8%)
  local copies, waits for them, and re-layouts  2.02 us (2%)
    all_to_all x2, starting transfers between devices, share(): got = lax.all_to_all(rows.reshape(CHIPS, 4, 128), CHIP_AXES, 0, 0)  21.9 us
    all_to_all x2, waiting for transfers between devices, share(): got = lax.all_to_all(rows.reshape(CHIPS, 4, 128), CHIP_AXES, 0, 0)  13.4 us
    ppermute x5, waiting for transfers between devices, swap_x(): far = lax.ppermute(outer, ALL_AXES, swaps(True, 1))  12.6 us
    ppermute x5, starting transfers between devices, swap_y(): far = lax.ppermute(outer, ALL_AXES, swaps(False, 1))  10.9 us
    pallas_call x10, Pallas kernels, call(): pl.pallas_call(placed, out_shape=outs, in_specs=specs or [VMEM] * len(arg...  8.2 us
    ppermute x5, starting transfers between devices, swap_x(): near = lax.ppermute(inner, 'c', SWAP)  6.96 us
    ppermute x5, waiting for transfers between devices, swap_y(): near = lax.ppermute(inner, ALL_AXES, swaps(False, 0))  5.7 us
    all_to_all x1, starting transfers between devices, on_device(): lax.all_to_all(rows.reshape(2 * CHIPS, 1, 128), ALL_AXES, 0, 0)  5.21 us
  transfers between devices with their start and end apart: 25, of which 17 were waited for; matrix products, arithmetic and copies ran while one was open for 0% of the time, Pallas kernels for 2%

profile of v4, /device:TPU:1, one launch (start us, length us, event | category | flops | bytes accessed | tf_op | source)
XLA Modules:
  0.0 106.5 jit_solution(1222126092459291745)
XLA Ops:
  0.6 0.9 copy-done
  1.6 0.1 shard_map.113
  1.7 3.3 %collective-permute-start = (f32[8,8,128]{2,1,0:T(8,128)S(1)}, f32[8,8,128]{2,1,0:T(8,128)S(1)}, u32[]{:S(2)}, u32[]{:S(2)}) collective-permute-start(f32[8,8,128]{2,1,0:T(8,128)S(1)} %get-tuple-element.38), channel_id=1, source_target_pairs={{0,32},{32,0},{1,33},{33,1},{2,34},{34,2},{3,35},{35,3},{4,36},{36... | collective-permute-start | bytes 98312 | tf_op jit(solution)/shard_map/ppermute | solution.py:481
  5.0 0.9 collective-permute-done.refs_1_
  5.9 2.8 %collective-permute-done.1.refs_2_ = f32[8,8,128]{2,1,0:T(8,128)S(1)} collective-permute-done((f32[8,8,128]{2,1,0:T(8,128)S(1)}, f32[8,8,128]{2,1,0:T(8,128)S(1)}, u32[]{:S(2)}, u32[]{:S(2)}) %collective-permute-start.1) | collective-permute-done | bytes 32800 | tf_op jit(solution)/shard_map/ppermute | solution.py:480
  8.6 0.1 select_add_fusion.8
  8.7 0.5 collective-permute-start.3
  9.2 1.2 %collective-permute-start.2 = (f32[8,8,128]{2,1,0:T(8,128)S(1)}, f32[8,8,128]{2,1,0:T(8,128)S(1)}, u32[]{:S(2)}, u32[]{:S(2)}) collective-permute-start(f32[8,8,128]{2,1,0:T(8,128)S(1)} %get-tuple-element.105), channel_id=1, source_target_pairs={{0,1},{1,0},{2,3},{3,2},{4,5},{5,4},{6,7},{7,6},{8,9},{9,8},{10,11... | collective-permute-start | bytes 98312 | tf_op jit(solution)/shard_map/ppermute | solution.py:487
  10.4 0.0 collective-permute-done.3.refs_4_
  10.4 1.6 %collective-permute-done.2.refs_3_ = f32[8,8,128]{2,1,0:T(8,128)S(1)} collective-permute-done((f32[8,8,128]{2,1,0:T(8,128)S(1)}, f32[8,8,128]{2,1,0:T(8,128)S(1)}, u32[]{:S(2)}, u32[]{:S(2)}) %collective-permute-start.2) | collective-permute-done | bytes 32800 | tf_op jit(solution)/shard_map/ppermute | solution.py:487
  12.0 0.9 copy-done.4
  12.9 0.5 shard_map.114
  13.5 1.4 %collective-permute-start.4 = (f32[8,8,128]{2,1,0:T(8,128)S(1)}, f32[8,8,128]{2,1,0:T(8,128)S(1)}, u32[]{:S(2)}, u32[]{:S(2)}) collective-permute-start(f32[8,8,128]{2,1,0:T(8,128)S(1)} %get-tuple-element.43), channel_id=1, source_target_pairs={{0,32},{32,0},{1,33},{33,1},{2,34},{34,2},{3,35},{35,3},{4,36},{36... | collective-permute-start | bytes 98312 | tf_op jit(solution)/shard_map/ppermute | solution.py:481
  14.8 0.9 shard_map.115
  15.7 14.5 %all-to-all-start = ((f32[128,4,128]{2,1,0:T(4,128)}), f32[128,4,128]{2,1,0:T(4,128)S(1)}, u32[]{:S(2)}, u32[]{:S(2)}) async-start(f32[128,4,128]{2,1,0:T(4,128)} %bitcast.9), calls=%async_computation | async-start | bytes 524288 | tf_op jit(solution)/shard_map/all_to_all | solution.py:492
  30.2 0.0 copy-start.8
  30.2 1.5 %collective-permute-start.5 = (f32[8,8,128]{2,1,0:T(8,128)S(1)}, f32[8,8,128]{2,1,0:T(8,128)S(1)}, u32[]{:S(2)}, u32[]{:S(2)}) collective-permute-start(f32[8,8,128]{2,1,0:T(8,128)S(1)} %get-tuple-element.44), channel_id=1, source_target_pairs={{0,1},{1,0},{2,3},{3,2},{4,5},{5,4},{6,7},{7,6},{8,9},{9,8},{10,11... | collective-permute-start | bytes 98312 | tf_op jit(solution)/shard_map/ppermute | solution.py:480
  31.7 2.4 %collective-permute-done.5.refs_2_ = f32[8,8,128]{2,1,0:T(8,128)S(1)} collective-permute-done((f32[8,8,128]{2,1,0:T(8,128)S(1)}, f32[8,8,128]{2,1,0:T(8,128)S(1)}, u32[]{:S(2)}, u32[]{:S(2)}) %collective-permute-start.5) | collective-permute-done | bytes 32800 | tf_op jit(solution)/shard_map/ppermute | solution.py:480
  34.1 0.1 select_add_fusion.6
  34.2 3.7 %collective-permute-start.7 = (f32[8,8,128]{2,1,0:T(8,128)S(1)}, f32[8,8,128]{2,1,0:T(8,128)S(1)}, u32[]{:S(2)}, u32[]{:S(2)}) collective-permute-start(f32[8,8,128]{2,1,0:T(8,128)S(1)} %get-tuple-element.102), channel_id=1, source_target_pairs={{0,32},{1,2},{2,1},{3,4},{4,3},{5,6},{6,5},{7,8},{8,7},{9,10},{10,... | collective-permute-start | bytes 98312 | tf_op jit(solution)/shard_map/ppermute | solution.py:486
  37.9 6.6 %all-to-all-done = f32[128,4,128]{2,1,0:T(4,128)S(1)} async-done(((f32[128,4,128]{2,1,0:T(4,128)}), f32[128,4,128]{2,1,0:T(4,128)S(1)}, u32[]{:S(2)}, u32[]{:S(2)}) %all-to-all-start) | async-done | bytes 262176 | tf_op jit(solution)/shard_map/all_to_all | solution.py:492
  44.5 0.0 copy-start.9
  44.5 0.5 shard_map.116.refs_5_
  45.0 2.1 %collective-permute-start.8 = (f32[8,128]{1,0:T(8,128)S(1)}, f32[8,128]{1,0:T(8,128)S(1)}, u32[]{:S(2)}, u32[]{:S(2)}) collective-permute-start(f32[8,128]{1,0:T(8,128)S(1)} %shard_map.116.refs_5_), channel_id=1, source_target_pairs={{0,32},{32,0},{1,33},{33,1},{2,34},{34,2},{3,35},{35,3},{4,36},{36... | collective-permute-start | bytes 12296 | tf_op jit(solution)/shard_map/ppermute | solution.py:519
  47.1 0.0 collective-permute-done.6.refs_3_
  47.1 0.8 collective-permute-done.8.refs_6_
  47.9 0.1 copy-done.6
  48.0 2.0 %shard_map.118 = (f32[8,8,8,128]{3,2,1,0:T(8,128)S(1)}, f32[8,8,8,128]{3,2,1,0:T(8,128)S(1)}, f32[512,128]{1,0:T(8,128)}, f32[8,8,128]{2,1,0:T(8,128)S(1)}, f32[...) custom-call(f32[8,8,8,128]{3,2,1,0:T(8,128)S(1)} %get-tuple-element.42.refs_0_, ...), custom_call_target="tpu_custom_call" | custom-call | tf_op jit(solution)/shard_map/pallas_call | solution.py:173
  50.0 0.4 collective-permute-start.9
  50.4 0.0 collective-permute-start.10
  50.4 0.9 collective-permute-done.9.refs_1_
  51.3 2.7 %collective-permute-done.10.refs_2_ = f32[8,8,128]{2,1,0:T(8,128)S(1)} collective-permute-done((f32[8,8,128]{2,1,0:T(8,128)S(1)}, f32[8,8,128]{2,1,0:T(8,128)S(1)}, u32[]{:S(2)}, u32[]{:S(2)}) %collective-permute-start.10) | collective-permute-done | bytes 32800 | tf_op jit(solution)/shard_map/ppermute | solution.py:480
  54.0 0.1 select_add_fusion.4
  54.1 0.5 collective-permute-start.12
  54.6 0.0 collective-permute-start.11
  54.6 0.9 collective-permute-done.12.refs_4_
  55.5 1.9 %collective-permute-done.11.refs_3_ = f32[8,8,128]{2,1,0:T(8,128)S(1)} collective-permute-done((f32[8,8,128]{2,1,0:T(8,128)S(1)}, f32[8,8,128]{2,1,0:T(8,128)S(1)}, u32[]{:S(2)}, u32[]{:S(2)}) %collective-permute-start.11) | collective-permute-done | bytes 32800 | tf_op jit(solution)/shard_map/ppermute | solution.py:487
  57.4 0.5 shard_map.119
  57.9 1.5 %collective-permute-start.13 = (f32[8,8,128]{2,1,0:T(8,128)S(1)}, f32[8,8,128]{2,1,0:T(8,128)S(1)}, u32[]{:S(2)}, u32[]{:S(2)}) collective-permute-start(f32[8,8,128]{2,1,0:T(8,128)S(1)} %get-tuple-element.54), channel_id=1, source_target_pairs={{0,32},{32,0},{1,33},{33,1},{2,34},{34,2},{3,35},{35,3},{4,36},{36... | collective-permute-start | bytes 98312 | tf_op jit(solution)/shard_map/ppermute | solution.py:481
  59.4 7.5 %all-to-all-start.1 = ((f32[128,4,128]{2,1,0:T(4,128)}), f32[128,4,128]{2,1,0:T(4,128)S(1)}, u32[]{:S(2)}, u32[]{:S(2)}) async-start(f32[128,4,128]{2,1,0:T(4,128)} %bitcast.20), calls=%async_computation.1 | async-start | bytes 524288 | tf_op jit(solution)/shard_map/all_to_all | solution.py:492
  66.9 1.2 %collective-permute-start.14 = (f32[8,8,128]{2,1,0:T(8,128)S(1)}, f32[8,8,128]{2,1,0:T(8,128)S(1)}, u32[]{:S(2)}, u32[]{:S(2)}) collective-permute-start(f32[8,8,128]{2,1,0:T(8,128)S(1)} %get-tuple-element.55), channel_id=1, source_target_pairs={{0,1},{1,0},{2,3},{3,2},{4,5},{5,4},{6,7},{7,6},{8,9},{9,8},{10,11... | collective-permute-start | bytes 98312 | tf_op jit(solution)/shard_map/ppermute | solution.py:480
  68.1 2.7 %collective-permute-done.14.refs_2_ = f32[8,8,128]{2,1,0:T(8,128)S(1)} collective-permute-done((f32[8,8,128]{2,1,0:T(8,128)S(1)}, f32[8,8,128]{2,1,0:T(8,128)S(1)}, u32[]{:S(2)}, u32[]{:S(2)}) %collective-permute-start.14) | collective-permute-done | bytes 32800 | tf_op jit(solution)/shard_map/ppermute | solution.py:480
  70.8 0.1 select_add_fusion.2
  70.9 3.7 %collective-permute-start.16 = (f32[8,8,128]{2,1,0:T(8,128)S(1)}, f32[8,8,128]{2,1,0:T(8,128)S(1)}, u32[]{:S(2)}, u32[]{:S(2)}) collective-permute-start(f32[8,8,128]{2,1,0:T(8,128)S(1)} %get-tuple-element.98), channel_id=1, source_target_pairs={{0,32},{1,2},{2,1},{3,4},{4,3},{5,6},{6,5},{7,8},{8,7},{9,10},{10,... | collective-permute-start | bytes 98312 | tf_op jit(solution)/shard_map/ppermute | solution.py:486
  74.6 0.0 collective-permute-start.15
  74.6 6.7 %all-to-all-done.1 = f32[128,4,128]{2,1,0:T(4,128)S(1)} async-done(((f32[128,4,128]{2,1,0:T(4,128)}), f32[128,4,128]{2,1,0:T(4,128)S(1)}, u32[]{:S(2)}, u32[]{:S(2)}) %all-to-all-start.1) | async-done | bytes 262176 | tf_op jit(solution)/shard_map/all_to_all | solution.py:492
  81.3 0.4 shard_map.120.refs_5_
  81.8 2.0 %collective-permute-start.17 = (f32[8,128]{1,0:T(8,128)S(1)}, f32[8,128]{1,0:T(8,128)S(1)}, u32[]{:S(2)}, u32[]{:S(2)}) collective-permute-start(f32[8,128]{1,0:T(8,128)S(1)} %shard_map.120.refs_5_), channel_id=1, source_target_pairs={{0,32},{32,0},{1,33},{33,1},{2,34},{34,2},{3,35},{35,3},{4,36},{36... | collective-permute-start | bytes 12296 | tf_op jit(solution)/shard_map/ppermute | solution.py:519
  83.8 0.0 collective-permute-done.16.refs_4_
  83.8 0.0 collective-permute-done.15.refs_3_
  83.8 0.8 collective-permute-done.17.refs_6_
  84.6 1.9 %shard_map.121 = (f32[8,8,8,128]{3,2,1,0:T(8,128)S(1)}, f32[8,8,8,128]{3,2,1,0:T(8,128)S(1)}, f32[256,128]{1,0:T(8,128)}, f32[8,128]{1,0:T(8,128)S(1)}, f32[8,8,...) custom-call(f32[8,8,8,128]{3,2,1,0:T(8,128)S(1)} %get-tuple-element.53.refs_0_, ...), custom_call_target="tpu_custom_call" | custom-call | tf_op jit(solution)/shard_map/pallas_call | solution.py:173
  86.5 0.3 collective-permute-start.18
  86.9 5.2 %all-to-all-start.2 = ((f32[256,1,128]{2,1,0:T(1,128)}), f32[256,1,128]{2,1,0:T(1,128)S(1)}, u32[]{:S(2)}, u32[]{:S(2)}) async-start(f32[256,1,128]{2,1,0:T(1,128)} %bitcast.27), calls=%async_computation.2 | async-start | bytes 262144 | tf_op jit(solution)/shard_map/all_to_all | solution.py:547
  92.1 1.7 %collective-permute-start.19 = (f32[8,8,128]{2,1,0:T(8,128)S(1)}, f32[8,8,128]{2,1,0:T(8,128)S(1)}, u32[]{:S(2)}, u32[]{:S(2)}) collective-permute-start(f32[8,8,128]{2,1,0:T(8,128)S(1)} %get-tuple-element.62), channel_id=1, source_target_pairs={{0,1},{1,0},{2,3},{3,2},{4,5},{5,4},{6,7},{7,6},{8,9},{9,8},{10,11... | collective-permute-start | bytes 98312 | tf_op jit(solution)/shard_map/ppermute | solution.py:480
  93.8 0.0 collective-permute-done.18.refs_1_
  93.8 2.1 %collective-permute-done.19.refs_2_ = f32[8,8,128]{2,1,0:T(8,128)S(1)} collective-permute-done((f32[8,8,128]{2,1,0:T(8,128)S(1)}, f32[8,8,128]{2,1,0:T(8,128)S(1)}, u32[]{:S(2)}, u32[]{:S(2)}) %collective-permute-start.19) | collective-permute-done | bytes 32800 | tf_op jit(solution)/shard_map/ppermute | solution.py:480
  95.9 0.1 select_add_fusion
  96.0 2.6 %collective-permute-start.21 = (f32[8,8,128]{2,1,0:T(8,128)S(1)}, f32[8,8,128]{2,1,0:T(8,128)S(1)}, u32[]{:S(2)}, u32[]{:S(2)}) collective-permute-start(f32[8,8,128]{2,1,0:T(8,128)S(1)} %get-tuple-element.96), channel_id=1, source_target_pairs={{0,32},{1,2},{2,1},{3,4},{4,3},{5,6},{6,5},{7,8},{8,7},{9,10},{10,... | collective-permute-start | bytes 98312 | tf_op jit(solution)/shard_map/ppermute | solution.py:486
  98.6 0.5 collective-permute-start.20
  99.1 0.4 collective-permute-done.21.refs_4_
  99.4 2.2 %collective-permute-done.20.refs_3_ = f32[8,8,128]{2,1,0:T(8,128)S(1)} collective-permute-done((f32[8,8,128]{2,1,0:T(8,128)S(1)}, f32[8,8,128]{2,1,0:T(8,128)S(1)}, u32[]{:S(2)}, u32[]{:S(2)}) %collective-permute-start.20) | collective-permute-done | bytes 32800 | tf_op jit(solution)/shard_map/ppermute | solution.py:487
  101.6 3.6 %all-to-all-done.2 = f32[256,1,128]{2,1,0:T(1,128)S(1)} async-done(((f32[256,1,128]{2,1,0:T(1,128)}), f32[256,1,128]{2,1,0:T(1,128)S(1)}, u32[]{:S(2)}, u32[]{:S(2)}) %all-to-all-start.2) | async-done | bytes 131104 | tf_op jit(solution)/shard_map/all_to_all | solution.py:547
  105.2 1.3 %shard_map.122 = (f32[8,8,8,128]{3,2,1,0:T(8,128)}, f32[8,8,8,128]{3,2,1,0:T(8,128)}) custom-call(f32[8,8,8,128]{3,2,1,0:T(8,128)S(1)} %get-tuple-element.60.refs_0_, f32[8,8,128]{2,1,0:T(8,128)S(1)} %collective-permute-done.18.refs_1_, f32[8,8,128]{2,1,0:T(8,128)S(1)} %collective-permute-done.19.refs_2_, f32[8,8,128]{2,1,0:T(8,128)S(1)} %collective-permute-done.20.refs_3_, ...), custom_call_target="tpu_custom_call" | custom-call | tf_op jit(solution)/shard_map/pallas_call | solution.py:173
  (36 shorter events, 0.1 us)
Async XLA Ops:
  0.6 1.0 copy-start
  1.6 10.4 %copy-start.1 = (f32[8,8,8,1,1,128]{5,4,3,2,1,0:T(1,128)S(1)}, f32[8,8,8,1,1,128]{5,4,3,2,1,0:T(1,128)}, u32[]{:S(2)}) copy-start(f32[8,8,8,1,1,128]{5,4,3,2,1,0:T(1,128)} %param.10) | copy-start | bytes 786436
  1.7 4.1 %collective-permute-start = (f32[8,8,128]{2,1,0:T(8,128)S(1)}, f32[8,8,128]{2,1,0:T(8,128)S(1)}, u32[]{:S(2)}, u32[]{:S(2)}) collective-permute-start(f32[8,8,128]{2,1,0:T(8,128)S(1)} %get-tuple-element.38), channel_id=1, source_target_pairs={{0,32},{32,0},{1,33},{33,1},{2,34},{34,2},{3,35},{35,3},{4,36},{36... | collective-permute-start | bytes 98312 | tf_op jit(solution)/shard_map/ppermute | solution.py:481
  5.0 3.6 %collective-permute-start.1 = (f32[8,8,128]{2,1,0:T(8,128)S(1)}, f32[8,8,128]{2,1,0:T(8,128)S(1)}, u32[]{:S(2)}, u32[]{:S(2)}) collective-permute-start(f32[8,8,128]{2,1,0:T(8,128)S(1)} %get-tuple-element.39), channel_id=1, source_target_pairs={{0,1},{1,0},{2,3},{3,2},{4,5},{5,4},{6,7},{7,6},{8,9},{9,8},{10,11... | collective-permute-start | bytes 98312 | tf_op jit(solution)/shard_map/ppermute | solution.py:480
  8.7 1.7 %collective-permute-start.3 = (f32[8,8,128]{2,1,0:T(8,128)S(1)}, f32[8,8,128]{2,1,0:T(8,128)S(1)}, u32[]{:S(2)}, u32[]{:S(2)}) collective-permute-start(f32[8,8,128]{2,1,0:T(8,128)S(1)} %get-tuple-element.104), channel_id=1, source_target_pairs={{0,32},{1,2},{2,1},{3,4},{4,3},{5,6},{6,5},{7,8},{8,7},{9,10},{10,... | collective-permute-start | bytes 98312 | tf_op jit(solution)/shard_map/ppermute | solution.py:486
  9.2 5.6 %copy-start.3 = (f32[19,8,128]{2,1,0:T(8,128)S(1)}, f32[19,8,128]{2,1,0:T(8,128)}, u32[]{:S(2)}) copy-start(f32[19,8,128]{2,1,0:T(8,128)} %constant.46.clone.refs_1_.refs_9_.refs_11_) | copy-start | bytes 233476
  9.2 2.8 %collective-permute-start.2 = (f32[8,8,128]{2,1,0:T(8,128)S(1)}, f32[8,8,128]{2,1,0:T(8,128)S(1)}, u32[]{:S(2)}, u32[]{:S(2)}) collective-permute-start(f32[8,8,128]{2,1,0:T(8,128)S(1)} %get-tuple-element.105), channel_id=1, source_target_pairs={{0,1},{1,0},{2,3},{3,2},{4,5},{5,4},{6,7},{7,6},{8,9},{9,8},{10,11... | collective-permute-start | bytes 98312 | tf_op jit(solution)/shard_map/ppermute | solution.py:487
  12.0 1.0 copy-start.4
  12.9 1.9 %copy-start.7 = (bf16[2,128,256]{2,1,0:T(8,128)(2,1)S(1)}, bf16[2,128,256]{2,1,0:T(8,128)(2,1)}, u32[]{:S(2)}) copy-start(bf16[2,128,256]{2,1,0:T(8,128)(2,1)} %constant.47.clone.refs_2_.refs_11_) | copy-start | bytes 393220
  13.5 18.2 %collective-permute-start.4 = (f32[8,8,128]{2,1,0:T(8,128)S(1)}, f32[8,8,128]{2,1,0:T(8,128)S(1)}, u32[]{:S(2)}, u32[]{:S(2)}) collective-permute-start(f32[8,8,128]{2,1,0:T(8,128)S(1)} %get-tuple-element.43), channel_id=1, source_target_pairs={{0,32},{32,0},{1,33},{33,1},{2,34},{34,2},{3,35},{35,3},{4,36},{36... | collective-permute-start | bytes 98312 | tf_op jit(solution)/shard_map/ppermute | solution.py:481
  15.7 28.8 %copy-start.2 = (bf16[2,224,512]{2,1,0:T(8,128)(2,1)S(1)}, bf16[2,224,512]{2,1,0:T(8,128)(2,1)}, u32[]{:S(2)}) copy-start(bf16[2,224,512]{2,1,0:T(8,128)(2,1)} %constant.48.clone.refs_1_) | copy-start | bytes 1376260
  15.7 28.8 %copy-start.11 = (f32[40,224]{1,0:T(8,128)S(1)}, f32[40,224]{1,0:T(8,128)}, u32[]{:S(2)}) copy-start(f32[40,224]{1,0:T(8,128)} %constant.51.clone.refs_4_) | copy-start | bytes 107524
  15.7 28.8 %all-to-all-start = ((f32[128,4,128]{2,1,0:T(4,128)}), f32[128,4,128]{2,1,0:T(4,128)S(1)}, u32[]{:S(2)}, u32[]{:S(2)}) async-start(f32[128,4,128]{2,1,0:T(4,128)} %bitcast.9), calls=%async_computation | async-start | bytes 524288 | tf_op jit(solution)/shard_map/all_to_all | solution.py:492
  30.2 14.3 %copy-start.8 = (f32[224,128]{1,0:T(8,128)S(1)}, f32[224,128]{1,0:T(8,128)}, u32[]{:S(2)}) copy-start(f32[224,128]{1,0:T(8,128)} %constant.49.clone.refs_2_) | copy-start | bytes 344068
  30.2 3.9 %collective-permute-start.5 = (f32[8,8,128]{2,1,0:T(8,128)S(1)}, f32[8,8,128]{2,1,0:T(8,128)S(1)}, u32[]{:S(2)}, u32[]{:S(2)}) collective-permute-start(f32[8,8,128]{2,1,0:T(8,128)S(1)} %get-tuple-element.44), channel_id=1, source_target_pairs={{0,1},{1,0},{2,3},{3,2},{4,5},{5,4},{6,7},{7,6},{8,9},{9,8},{10,11... | collective-permute-start | bytes 98312 | tf_op jit(solution)/shard_map/ppermute | solution.py:480
  34.1 10.4 %copy-start.10 = (f32[8,8,224]{2,1,0:T(8,128)S(1)}, f32[8,8,224]{2,1,0:T(8,128)}, u32[]{:S(2)}) copy-start(f32[8,8,224]{2,1,0:T(8,128)} %constant.50.clone.refs_3_) | copy-start | bytes 172036
  34.2 12.9 %collective-permute-start.7 = (f32[8,8,128]{2,1,0:T(8,128)S(1)}, f32[8,8,128]{2,1,0:T(8,128)S(1)}, u32[]{:S(2)}, u32[]{:S(2)}) collective-permute-start(f32[8,8,128]{2,1,0:T(8,128)S(1)} %get-tuple-element.102), channel_id=1, source_target_pairs={{0,32},{1,2},{2,1},{3,4},{4,3},{5,6},{6,5},{7,8},{8,7},{9,10},{10,... | collective-permute-start | bytes 98312 | tf_op jit(solution)/shard_map/ppermute | solution.py:486
  37.9 9.2 %collective-permute-start.6 = (f32[8,8,128]{2,1,0:T(8,128)S(1)}, f32[8,8,128]{2,1,0:T(8,128)S(1)}, u32[]{:S(2)}, u32[]{:S(2)}) collective-permute-start(f32[8,8,128]{2,1,0:T(8,128)S(1)} %get-tuple-element.103), channel_id=1, source_target_pairs={{0,1},{1,0},{2,3},{3,2},{4,5},{5,4},{6,7},{7,6},{8,9},{9,8},{10,11... | collective-permute-start | bytes 98312 | tf_op jit(solution)/shard_map/ppermute | solution.py:487
  44.5 2.6 %copy-start.9 = (f32[8,8,8,1,1,128]{5,4,3,2,1,0:T(1,128)S(1)}, f32[8,8,8,1,1,128]{5,4,3,2,1,0:T(1,128)}, u32[]{:S(2)}) copy-start(f32[8,8,8,1,1,128]{5,4,3,2,1,0:T(1,128)} %param.11) | copy-start | bytes 786436
  45.0 2.9 %collective-permute-start.8 = (f32[8,128]{1,0:T(8,128)S(1)}, f32[8,128]{1,0:T(8,128)S(1)}, u32[]{:S(2)}, u32[]{:S(2)}) collective-permute-start(f32[8,128]{1,0:T(8,128)S(1)} %shard_map.116.refs_5_), channel_id=1, source_target_pairs={{0,32},{32,0},{1,33},{33,1},{2,34},{34,2},{3,35},{35,3},{4,36},{36... | collective-permute-start | bytes 12296 | tf_op jit(solution)/shard_map/ppermute | solution.py:519
  47.1 0.9 copy-start.6
  48.0 9.4 %copy-start.5 = (bf16[2,4,128,128]{3,2,1,0:T(8,128)(2,1)S(1)}, bf16[2,4,128,128]{3,2,1,0:T(8,128)(2,1)}, u32[]{:S(2)}) copy-start(bf16[2,4,128,128]{3,2,1,0:T(8,128)(2,1)} %constant.52.clone.refs_5_) | copy-start | bytes 786436
  50.0 1.3 %collective-permute-start.9 = (f32[8,8,128]{2,1,0:T(8,128)S(1)}, f32[8,8,128]{2,1,0:T(8,128)S(1)}, u32[]{:S(2)}, u32[]{:S(2)}) collective-permute-start(f32[8,8,128]{2,1,0:T(8,128)S(1)} %get-tuple-element.49), channel_id=1, source_target_pairs={{0,32},{32,0},{1,33},{33,1},{2,34},{34,2},{3,35},{35,3},{4,36},{36... | collective-permute-start | bytes 98312 | tf_op jit(solution)/shard_map/ppermute | solution.py:481
  50.4 3.6 %collective-permute-start.10 = (f32[8,8,128]{2,1,0:T(8,128)S(1)}, f32[8,8,128]{2,1,0:T(8,128)S(1)}, u32[]{:S(2)}, u32[]{:S(2)}) collective-permute-start(f32[8,8,128]{2,1,0:T(8,128)S(1)} %get-tuple-element.50), channel_id=1, source_target_pairs={{0,1},{1,0},{2,3},{3,2},{4,5},{5,4},{6,7},{7,6},{8,9},{9,8},{10,11... | collective-permute-start | bytes 98312 | tf_op jit(solution)/shard_map/ppermute | solution.py:480
  54.1 1.3 %collective-permute-start.12 = (f32[8,8,128]{2,1,0:T(8,128)S(1)}, f32[8,8,128]{2,1,0:T(8,128)S(1)}, u32[]{:S(2)}, u32[]{:S(2)}) collective-permute-start(f32[8,8,128]{2,1,0:T(8,128)S(1)} %get-tuple-element.100), channel_id=1, source_target_pairs={{0,32},{1,2},{2,1},{3,4},{4,3},{5,6},{6,5},{7,8},{8,7},{9,10},{10,... | collective-permute-start | bytes 98312 | tf_op jit(solution)/shard_map/ppermute | solution.py:486
  54.6 2.8 %collective-permute-start.11 = (f32[8,8,128]{2,1,0:T(8,128)S(1)}, f32[8,8,128]{2,1,0:T(8,128)S(1)}, u32[]{:S(2)}, u32[]{:S(2)}) collective-permute-start(f32[8,8,128]{2,1,0:T(8,128)S(1)} %get-tuple-element.101), channel_id=1, source_target_pairs={{0,1},{1,0},{2,3},{3,2},{4,5},{5,4},{6,7},{7,6},{8,9},{9,8},{10,11... | collective-permute-start | bytes 98312 | tf_op jit(solution)/shard_map/ppermute | solution.py:487
  57.9 10.2 %collective-permute-start.13 = (f32[8,8,128]{2,1,0:T(8,128)S(1)}, f32[8,8,128]{2,1,0:T(8,128)S(1)}, u32[]{:S(2)}, u32[]{:S(2)}) collective-permute-start(f32[8,8,128]{2,1,0:T(8,128)S(1)} %get-tuple-element.54), channel_id=1, source_target_pairs={{0,32},{32,0},{1,33},{33,1},{2,34},{34,2},{3,35},{35,3},{4,36},{36... | collective-permute-start | bytes 98312 | tf_op jit(solution)/shard_map/ppermute | solution.py:481
  59.4 21.9 %all-to-all-start.1 = ((f32[128,4,128]{2,1,0:T(4,128)}), f32[128,4,128]{2,1,0:T(4,128)S(1)}, u32[]{:S(2)}, u32[]{:S(2)}) async-start(f32[128,4,128]{2,1,0:T(4,128)} %bitcast.20), calls=%async_computation.1 | async-start | bytes 524288 | tf_op jit(solution)/shard_map/all_to_all | solution.py:492
  66.9 3.9 %collective-permute-start.14 = (f32[8,8,128]{2,1,0:T(8,128)S(1)}, f32[8,8,128]{2,1,0:T(8,128)S(1)}, u32[]{:S(2)}, u32[]{:S(2)}) collective-permute-start(f32[8,8,128]{2,1,0:T(8,128)S(1)} %get-tuple-element.55), channel_id=1, source_target_pairs={{0,1},{1,0},{2,3},{3,2},{4,5},{5,4},{6,7},{7,6},{8,9},{9,8},{10,11... | collective-permute-start | bytes 98312 | tf_op jit(solution)/shard_map/ppermute | solution.py:480
  70.9 12.8 %collective-permute-start.16 = (f32[8,8,128]{2,1,0:T(8,128)S(1)}, f32[8,8,128]{2,1,0:T(8,128)S(1)}, u32[]{:S(2)}, u32[]{:S(2)}) collective-permute-start(f32[8,8,128]{2,1,0:T(8,128)S(1)} %get-tuple-element.98), channel_id=1, source_target_pairs={{0,32},{1,2},{2,1},{3,4},{4,3},{5,6},{6,5},{7,8},{8,7},{9,10},{10,... | collective-permute-start | bytes 98312 | tf_op jit(solution)/shard_map/ppermute | solution.py:486
  74.6 9.2 %collective-permute-start.15 = (f32[8,8,128]{2,1,0:T(8,128)S(1)}, f32[8,8,128]{2,1,0:T(8,128)S(1)}, u32[]{:S(2)}, u32[]{:S(2)}) collective-permute-start(f32[8,8,128]{2,1,0:T(8,128)S(1)} %get-tuple-element.99), channel_id=1, source_target_pairs={{0,1},{1,0},{2,3},{3,2},{4,5},{5,4},{6,7},{7,6},{8,9},{9,8},{10,11... | collective-permute-start | bytes 98312 | tf_op jit(solution)/shard_map/ppermute | solution.py:487
  81.8 2.8 %collective-permute-start.17 = (f32[8,128]{1,0:T(8,128)S(1)}, f32[8,128]{1,0:T(8,128)S(1)}, u32[]{:S(2)}, u32[]{:S(2)}) collective-permute-start(f32[8,128]{1,0:T(8,128)S(1)} %shard_map.120.refs_5_), channel_id=1, source_target_pairs={{0,32},{32,0},{1,33},{33,1},{2,34},{34,2},{3,35},{35,3},{4,36},{36... | collective-permute-start | bytes 12296 | tf_op jit(solution)/shard_map/ppermute | solution.py:519
  86.5 7.3 %collective-permute-start.18 = (f32[8,8,128]{2,1,0:T(8,128)S(1)}, f32[8,8,128]{2,1,0:T(8,128)S(1)}, u32[]{:S(2)}, u32[]{:S(2)}) collective-permute-start(f32[8,8,128]{2,1,0:T(8,128)S(1)} %get-tuple-element.61), channel_id=1, source_target_pairs={{0,32},{32,0},{1,33},{33,1},{2,34},{34,2},{3,35},{35,3},{4,36},{36... | collective-permute-start | bytes 98312 | tf_op jit(solution)/shard_map/ppermute | solution.py:481
  86.9 18.4 %all-to-all-start.2 = ((f32[256,1,128]{2,1,0:T(1,128)}), f32[256,1,128]{2,1,0:T(1,128)S(1)}, u32[]{:S(2)}, u32[]{:S(2)}) async-start(f32[256,1,128]{2,1,0:T(1,128)} %bitcast.27), calls=%async_computation.2 | async-start | bytes 262144 | tf_op jit(solution)/shard_map/all_to_all | solution.py:547
  92.1 3.8 %collective-permute-start.19 = (f32[8,8,128]{2,1,0:T(8,128)S(1)}, f32[8,8,128]{2,1,0:T(8,128)S(1)}, u32[]{:S(2)}, u32[]{:S(2)}) collective-permute-start(f32[8,8,128]{2,1,0:T(8,128)S(1)} %get-tuple-element.62), channel_id=1, source_target_pairs={{0,1},{1,0},{2,3},{3,2},{4,5},{5,4},{6,7},{7,6},{8,9},{9,8},{10,11... | collective-permute-start | bytes 98312 | tf_op jit(solution)/shard_map/ppermute | solution.py:480
  96.0 3.5 %collective-permute-start.21 = (f32[8,8,128]{2,1,0:T(8,128)S(1)}, f32[8,8,128]{2,1,0:T(8,128)S(1)}, u32[]{:S(2)}, u32[]{:S(2)}) collective-permute-start(f32[8,8,128]{2,1,0:T(8,128)S(1)} %get-tuple-element.96), channel_id=1, source_target_pairs={{0,32},{1,2},{2,1},{3,4},{4,3},{5,6},{6,5},{7,8},{8,7},{9,10},{10,... | collective-permute-start | bytes 98312 | tf_op jit(solution)/shard_map/ppermute | solution.py:486
  98.6 3.1 %collective-permute-start.20 = (f32[8,8,128]{2,1,0:T(8,128)S(1)}, f32[8,8,128]{2,1,0:T(8,128)S(1)}, u32[]{:S(2)}, u32[]{:S(2)}) collective-permute-start(f32[8,8,128]{2,1,0:T(8,128)S(1)} %get-tuple-element.97), channel_id=1, source_target_pairs={{0,1},{1,0},{2,3},{3,2},{4,5},{5,4},{6,7},{7,6},{8,9},{9,8},{10,11... | collective-permute-start | bytes 98312 | tf_op jit(solution)/shard_map/ppermute | solution.py:487
